TPU v7x, 256 devices: a whole 4x4x8 slice. The times are simulated.
256 devices in a mesh: sec: 2 (over core), clu: 8 (over x, y_hi), blk: 16 (over y_lo, z).
Axes of the slice: x: 4, y: 4 (y_hi: 2, y_lo: 2; y = y_hi * 2 + y_lo), z: 8, core: 2. Of those that a mesh axis runs over, the one named last changes fastest.
Arguments:
- right_side: float32 [32, 128, 128, 128], P(None, ('sec', 'clu'), 'blk'), may hold values from -18 to 18
- block_weight: float32 [128, 128], P(('sec', 'clu'), 'blk'), may hold values from 2 to 8
- across_weight: float32 [128, 128], P(('sec', 'clu'), 'blk'), may hold values from 0.3 to 1
- along_weight: float32 [128, 128], P(('sec', 'clu'), 'blk'), may hold values from 0.3 to 1
- block_stiffness: bfloat16 [128, 128], replicated, may hold values from -0.1 to 1.1, as said below
- across_matrix: bfloat16 [128, 128], replicated, may hold values from -0.044194174 to 0.044194174
- along_matrix: bfloat16 [128, 128], replicated, may hold values from -0.044194174 to 0.044194174
- boundary_blocks: bfloat16 [2, 8, 768, 128, 128], P('sec', 'clu', 'blk'), may hold values from -0.22949219 to 0.22949219
- block_rows: int32 [2, 8, 768], P('sec', 'clu', 'blk'), may hold values from 0 to 31
- block_columns: int32 [2, 8, 768], P('sec', 'clu', 'blk'), may hold values from 0 to 15
- live_pairs: int32 [2, 8, 16], P('sec', 'clu', 'blk'), may hold values from 12 to 48, as said below
- surface_index: int32 [2, 8, 2048], P('sec', 'clu', 'blk'), may hold values from 0 to 8191, as said below
- interface_slot: int32 [32768], P('clu'), may hold values from 0 to 4095, as said below
Outputs:
- solution: float32 [32, 128, 128, 128], P(None, ('sec', 'clu'), 'blk')
Inputs may be any that keep to these rules, and one draw needn't show every extreme that they name: `block_stiffness`: symmetric. The first live_pairs[s, c, j] of a device's 48 listed pairs are live; some device has all 48 live. `surface_index`: the 128 entries of one device are distinct local dof numbers of that device. `interface_slot`: within each row range of 4096 interface dofs, each slot is taken exactly once.
All inputs are finite; a program needn't handle non-finite values.
Results may differ from a plain program's by a relative error of at most 0.0003.
The roundings to bfloat16 on the way count: a program that leaves them out, or rounds other values in their place, can miss the bound.
Values may be sent and summed in bfloat16 or wider, within the bound.
No kernel may reach another device: no remote copies, remote signals or barrier semaphores. Data moves between devices by JAX's collectives and lax.ppermute only.
A program may use at most 64 MiB of HBM per device.

v0:
```python
import jax
import jax.numpy as jnp
from jax import lax
from jax.sharding import Mesh
from jax.sharding import PartitionSpec as P

ITERS = 3
SEC_CLU_BLK = ("sec", "clu_0", "clu_1", "blk_0", "blk_1")
SEC_CLU = ("sec", "clu_0", "clu_1")
BLK = ("blk_0", "blk_1")
CLU = ("clu_0", "clu_1")
SEC_BLK = ("sec", "blk_0", "blk_1")


def one_axis_at_a_time(value, axes):
    for axis in axes:
        value = lax.psum(value, axis)
    return value


def passed_along(value, axis, by):
    count = lax.axis_size(axis)
    pairs = [(i, i + by) for i in range(count) if 0 <= i + by < count]
    return lax.ppermute(value, axis, pairs)


def with_halo(value, sides, width):
    edges = {}
    for axis, dim in sides:
        count, length = (lax.axis_size(axis), value.shape[dim])
        up = [(i, (i + 1) % count) for i in range(count - 1)]
        last = lax.slice_in_dim(value, length - width, length, axis=dim)
        initial = lax.slice_in_dim(value, 0, width, axis=dim)
        edges[dim] = (
            lax.ppermute(last, axis, up),
            lax.ppermute(initial, axis, [(b, a) for a, b in up]),
        )
    done = []
    for _, dim in sides:
        low, high = edges[dim]
        around = [(width, width) if d in done else (0, 0) for d in range(value.ndim)]
        value = jnp.concatenate([jnp.pad(low, around), value, jnp.pad(high, around)], axis=dim)
        done.append(dim)
    return value


def laid_out(pieces, dim):
    shape = list(pieces.shape[1:])
    shape[dim] *= pieces.shape[0]
    return jnp.moveaxis(pieces, 0, dim).reshape(shape)


def sent_to_all(value, axis):
    copies = jnp.broadcast_to(value, (lax.axis_size(axis), *value.shape))
    return lax.all_to_all(copies, axis, split_axis=0, concat_axis=0, tiled=True)


def gather_directly(value, axis, dim):
    return laid_out(sent_to_all(value, axis), dim)


def gathered_total(value, axis):
    pieces = lax.all_gather(value, axis)
    return pieces.sum(axis=0)


def split_up(value, dim, count):
    before, after = (value.shape[:dim], value.shape[dim + 1 :])
    return jnp.moveaxis(value.reshape(*before, count, -1, *after), dim, 0)


def summed_on_arrival(value, axis, dim):
    pieces = split_up(value, dim, lax.axis_size(axis))
    arrived = lax.all_to_all(pieces, axis, split_axis=0, concat_axis=0, tiled=True)
    return arrived.sum(axis=0)


def case_sum(left, right):
    return jnp.sum(left * right, axis=(1, 2, 3))


def squares(residual):
    return one_axis_at_a_time(case_sum(residual, residual), SEC_CLU_BLK)


def shards(
    right_side,
    block_weight,
    across_weight,
    along_weight,
    block_stiffness,
    across_matrix,
    along_matrix,
    boundary_blocks,
    block_rows,
    block_columns,
    live_pairs,
    surface_index,
    interface_slot,
):
    count_cases = right_side.shape[0]
    block_width = right_side.shape[3]
    across_edge = passed_along(across_weight[-1:, :], SEC_CLU, 1)
    across_lower = jnp.concatenate([across_edge, across_weight[:-1, :]], axis=0)
    along_edge = passed_along(along_weight[:, -1:], BLK, 1)
    along_lower = jnp.concatenate([along_edge, along_weight[:, :-1]], axis=1)
    coupled = jnp.concatenate(
        [across_matrix, across_matrix.T, along_matrix, along_matrix.T], axis=1
    )
    rows_local = block_rows[0, 0]
    columns_local = block_columns[0, 0]
    blocks_local = boundary_blocks[0, 0]
    surface_local = surface_index[0, 0]
    pair_count = rows_local.shape[0]
    cluster = blocks_local.shape[-1]
    surface_count = surface_local.shape[0]
    slot_count = interface_slot.shape[0]
    row_clusters = slot_count // cluster
    column_clusters = surface_count * lax.axis_size("sec") * lax.axis_size(CLU) // cluster
    live_mask = (jnp.arange(pair_count, dtype=jnp.int32) < live_pairs[0, 0, 0]).astype(jnp.float32)
    row_onehot = (rows_local[:, None] == jnp.arange(row_clusters, dtype=jnp.int32)[None, :]).astype(
        jnp.float32
    ) * live_mask[:, None]
    column_onehot = (
        columns_local[:, None] == jnp.arange(column_clusters, dtype=jnp.int32)[None, :]
    ).astype(jnp.float32) * live_mask[:, None]
    inverse = (
        jnp.zeros((slot_count,), jnp.int32)
        .at[interface_slot]
        .set(jnp.arange(slot_count, dtype=jnp.int32))
    )
    solution = jnp.zeros_like(right_side)
    residual = right_side
    direction = right_side
    norm_now = squares(residual)
    for iteration in range(ITERS):
        rounded = direction.astype(jnp.bfloat16)
        extended = with_halo(rounded, ((SEC_CLU, 1), (BLK, 2)), 1)
        own_part = jnp.einsum(
            "cabk,kl->cabl", rounded, block_stiffness, preferred_element_type=jnp.float32
        )
        neighbour = jnp.einsum(
            "cabk,kl->cabl", extended, coupled, preferred_element_type=jnp.float32
        )
        result = block_weight[None, :, :, None] * own_part
        result = result - across_weight[None, :, :, None] * neighbour[:, 2:, 1:-1, 0:block_width]
        result = (
            result
            - across_lower[None, :, :, None]
            * neighbour[:, :-2, 1:-1, block_width : 2 * block_width]
        )
        result = (
            result
            - along_weight[None, :, :, None]
            * neighbour[:, 1:-1, 2:, 2 * block_width : 3 * block_width]
        )
        result = result - along_lower[None, :, :, None] * neighbour[:, 1:-1, :-2, 3 * block_width :]
        mine = jnp.take(rounded.reshape(count_cases, -1), surface_local, axis=1)
        gathered = gather_directly(mine, SEC_BLK, 1)
        interface = jnp.take(gathered, interface_slot, axis=1).reshape(
            count_cases, row_clusters, cluster
        )
        picked = jnp.take(interface, rows_local, axis=1)
        terms = jnp.einsum("cpk,pkl->cpl", picked, blocks_local, preferred_element_type=jnp.float32)
        partial_columns = jnp.einsum(
            "cpl,pq->cql", terms, column_onehot, precision=lax.Precision.HIGHEST
        )
        columns = gathered_total(partial_columns, SEC_CLU).astype(jnp.bfloat16)
        chosen = jnp.take(columns, columns_local, axis=1)
        returned = jnp.einsum(
            "cpl,pkl->cpk", chosen, blocks_local, preferred_element_type=jnp.float32
        )
        partial_rows = jnp.einsum(
            "cpk,pr->crk", returned, row_onehot, precision=lax.Precision.HIGHEST
        )
        partial_rows = partial_rows.reshape(count_cases, slot_count)
        own_values = summed_on_arrival(jnp.take(partial_rows, inverse, axis=1), SEC_BLK, 1)
        image_field = (
            result.reshape(count_cases, -1)
            .at[:, surface_local]
            .add(own_values)
            .reshape(result.shape)
        )
        curvature = one_axis_at_a_time(case_sum(direction, image_field), SEC_CLU_BLK)
        alpha = (norm_now / curvature)[:, None, None, None]
        solution = solution + alpha * direction
        if iteration + 1 < ITERS:
            residual = residual - alpha * image_field
            norm_next = squares(residual)
            direction = residual + (norm_next / norm_now)[:, None, None, None] * direction
            norm_now = norm_next
    return solution


def solution(mesh):
    finer = Mesh(
        mesh.devices.reshape(mesh.shape["sec"], 4, 2, 2, 8),
        ("sec", "clu_0", "clu_1", "blk_0", "blk_1"),
    )
    placed = (
        P(None, SEC_CLU, BLK, None),
        P(SEC_CLU, BLK),
        P(SEC_CLU, BLK),
        P(SEC_CLU, BLK),
        P(),
        P(),
        P(),
        P("sec", CLU, BLK, None, None),
        P("sec", CLU, BLK),
        P("sec", CLU, BLK),
        P("sec", CLU, BLK),
        P("sec", CLU, BLK),
        P(CLU),
    )
    return jax.shard_map(
        shards, mesh=finer, in_specs=placed, out_specs=P(None, SEC_CLU, BLK, None), check_vma=False
    )
```

profile of v0, /device:TPU:8, one launch (start us, length us, event | category | flops | bytes accessed | tf_op | source)
XLA Modules:
  0.0 760.1 jit_solution(6193394905362327553)
XLA Ops:
  15.1 10.1 %all-to-all-start = ((bf16[32,32,128]{2,1,0:T(8,128)(2,1)}), bf16[32,32,128]{2,1,0:T(8,128)(2,1)S(1)}, u32[]{:S(2)}, u32[]{:S(2)}) async-start(bf16[32,32,128]{2,1,0:T(8,128)(2,1)} %broadcast_in_dim.53), calls=%async_computation | async-start | bytes 524288 | tf_op jit(solution)/shard_map/all_to_all | solution.py:55
  26.0 10.7 %all-to-all-done = bf16[32,32,128]{2,1,0:T(8,128)(2,1)S(1)} async-done(((bf16[32,32,128]{2,1,0:T(8,128)(2,1)}), bf16[32,32,128]{2,1,0:T(8,128)(2,1)S(1)}, u32[]{:S(2)}, u32[]{:S(2)}) %all-to-all-start) | async-done | bytes 262176 | tf_op jit(solution)/shard_map/all_to_all | solution.py:55
  38.0 15.6 %gather_fusion.1 = bf16[4096,32]{1,0:T(8,128)(2,1)} fusion(bf16[32,4096]{0,1:T(8,128)(2,1)} %bitcast.181, s32[4096]{0:T(1024)S(1)} %get-tuple-element.53), kind=kCustom, calls=%fused_computation.1.clone | custom fusion | bytes 540672 | tf_op jit(solution)/shard_map/jit(_take)/gather | solution.py:160
  53.6 4.2 broadcast_select_fusion.5
  69.5 6.1 collective-permute-start.1
  78.0 15.5 %scatter_custom_fusion = s32[4096]{0:T(1024)S(1)} fusion(s32[4096]{0:T(1024)S(1)} %get-tuple-element.52, s32[4096]{0:T(1024)S(1)} %iota.17, s32[]{:T(128)} %constant.47.clone.1), kind=kCustom, calls=%fused_computation.197 | custom fusion | bytes 16388 | tf_op jit(solution)/shard_map/scatter | solution.py:130
  93.7 5.1 collective-permute-start.4
  98.9 21.6 %all-gather.7.cloned.1.call-done = f32[512,16,128]{2,1,0:T(8,128)} async-done(((f32[32,16,128]{2,1,0:T(8,128)}), f32[512,16,128]{2,1,0:T(8,128)}) %all-gather.7.cloned.1.call-update) | async-done | bytes 4194320 | tf_op jit(solution)/shard_map/all_gather | solution.py:63
  127.7 15.7 %gather_fusion.4 = f32[4096,32]{1,0:T(8,128)} fusion(f32[32,4096]{0,1:T(8,128)} %bitcast.174, s32[4096]{0:T(1024)S(1)} %fusion.135), kind=kCustom, calls=%fused_computation.4.clone | custom fusion | bytes 1064960 | tf_op jit(solution)/shard_map/jit(_take)/gather | solution.py:177
  143.3 4.7 broadcast_select_fusion.2
  151.0 8.6 %all-to-all-start.1 = ((f32[32,32,128]{2,1,0:T(8,128)}), f32[32,32,128]{2,1,0:T(8,128)S(1)}, u32[]{:S(2)}, u32[]{:S(2)}) async-start(f32[32,32,128]{2,1,0:T(8,128)} %bitcast.32), calls=%async_computation.1 | async-start | bytes 1048576 | tf_op jit(solution)/shard_map/all_to_all | solution.py:74
  161.8 3.8 fusion.45
  165.6 3.6 copy.272
  169.2 5.9 all-to-all-done.1
  175.2 5.3 scatter_fusion
  180.5 3.6 copy.227
  184.1 3.8 copy.275
  192.0 10.1 %all-reduce.7 = (f32[32]{0:T(128)S(1)}, f32[32]{0:T(128)S(1)}) all-reduce(f32[32]{0:T(128)S(1)} %get-tuple-element.20, f32[32]{0:T(128)S(1)} %get-tuple-element.21), channel_id=1, replica_groups=mesh['sec'=2,'clu_0'=4,'clu_1'=2,'blk_0'=2,'blk_1'=8] {'clu_0'}, use_global_device_ids=true, to_apply=%region_2.0 | all-reduce | flops 64 | bytes 512 | tf_op jit(solution)/shard_map/psum | solution.py:17
  202.0 6.4 all-reduce.9
  208.5 4.9 all-reduce.8
  213.4 16.8 %all-reduce.6 = (f32[32]{0:T(128)S(1)}, f32[32]{0:T(128)S(1)}) all-reduce(f32[32]{0:T(128)S(1)} %get-tuple-element.16, f32[32]{0:T(128)S(1)} %get-tuple-element.17), channel_id=1, replica_groups=mesh['sec'=2,'clu_0'=4,'clu_1'=2,'blk_0'=2,'blk_1'=8] {'blk_1'}, use_global_device_ids=true, to_apply=%region_5.0 | all-reduce | flops 64 | bytes 512 | tf_op jit(solution)/shard_map/psum | solution.py:17
  235.6 7.7 %psum.221 = f32[32]{0:T(128)S(1)} all-reduce(f32[32]{0:T(128)S(1)} %psum.220), channel_id=1, replica_groups=mesh['sec'=2,'clu_0'=4,'clu_1'=2,'blk_0'=2,'blk_1'=8] {'clu_0'}, use_global_device_ids=true, to_apply=%region_18.24 | all-reduce | flops 32 | bytes 256 | tf_op jit(solution)/shard_map/psum | solution.py:17
  243.3 6.4 psum.222
  249.7 4.9 psum.223
  254.7 14.1 %psum.224 = f32[32]{0:T(128)S(1)} all-reduce(f32[32]{0:T(128)S(1)} %psum.223), channel_id=1, replica_groups=mesh['sec'=2,'clu_0'=4,'clu_1'=2,'blk_0'=2,'blk_1'=8] {'blk_1'}, use_global_device_ids=true, to_apply=%region_21.27 | all-reduce | flops 32 | bytes 256 | tf_op jit(solution)/shard_map/psum | solution.py:17
  276.2 18.0 %all_to_all.30 = bf16[32,32,128]{2,1,0:T(8,128)(2,1)S(1)} all-to-all(bf16[32,32,128]{2,1,0:T(8,128)(2,1)S(1)} %broadcast_in_dim.55), channel_id=1, replica_groups=mesh['sec'=2,'clu_0'=4,'clu_1'=2,'blk_0'=2,'blk_1'=8] {'sec','blk_0','bl..., dimensions={0} | all-to-all | bytes 524288 | tf_op jit(solution)/shard_map/all_to_all | solution.py:55
  295.5 15.6 %gather_fusion.6 = bf16[4096,32]{1,0:T(8,128)(2,1)} fusion(bf16[32,4096]{0,1:T(8,128)(2,1)} %bitcast.182, s32[4096]{0:T(1024)S(1)} %get-tuple-element.53), kind=kCustom, calls=%fused_computation.7.clone | custom fusion | bytes 540672 | tf_op jit(solution)/shard_map/jit(_take)/gather | solution.py:160
  311.1 4.2 broadcast_select_fusion.4
  330.1 6.7 collective-permute-start.7
  336.8 42.5 %all-gather.9.cloned.1.call-done = f32[512,16,128]{2,1,0:T(8,128)} async-done(((f32[32,16,128]{2,1,0:T(8,128)}), f32[512,16,128]{2,1,0:T(8,128)}) %all-gather.9.cloned.1.call-update) | async-done | bytes 4194320 | tf_op jit(solution)/shard_map/all_gather | solution.py:63
  390.2 15.7 %gather_fusion.9 = f32[4096,32]{1,0:T(8,128)} fusion(f32[32,4096]{0,1:T(8,128)} %bitcast.175, s32[4096]{0:T(1024)S(1)} %copy-done.8), kind=kCustom, calls=%fused_computation.13.clone | custom fusion | bytes 1064960 | tf_op jit(solution)/shard_map/jit(_take)/gather | solution.py:177
  405.9 4.7 broadcast_select_fusion.1
  413.6 8.7 %all-to-all-start.3 = ((f32[32,32,128]{2,1,0:T(8,128)}), f32[32,32,128]{2,1,0:T(8,128)}, u32[]{:S(2)}, u32[]{:S(2)}) async-start(f32[32,32,128]{2,1,0:T(8,128)} %bitcast.196), calls=%async_computation.3 | async-start | bytes 1048576 | tf_op jit(solution)/shard_map/all_to_all | solution.py:74
  425.3 3.8 fusion.42
  429.1 3.6 copy.277
  432.7 5.1 all-to-all-done.3
  439.0 5.3 scatter_fusion.1
  444.2 3.6 copy.248
  452.1 10.1 %psum.226 = f32[32]{0:T(128)S(1)} all-reduce(f32[32]{0:T(128)S(1)} %psum.225), channel_id=1, replica_groups=mesh['sec'=2,'clu_0'=4,'clu_1'=2,'blk_0'=2,'blk_1'=8] {'clu_0'}, use_global_device_ids=true, to_apply=%region_27.33 | all-reduce | flops 32 | bytes 256 | tf_op jit(solution)/shard_map/psum | solution.py:17
  462.2 6.4 psum.227
  468.6 4.9 psum.228
  473.5 16.8 %psum.229 = f32[32]{0:T(128)S(1)} all-reduce(f32[32]{0:T(128)S(1)} %psum.228), channel_id=1, replica_groups=mesh['sec'=2,'clu_0'=4,'clu_1'=2,'blk_0'=2,'blk_1'=8] {'blk_1'}, use_global_device_ids=true, to_apply=%region_30.36 | all-reduce | flops 32 | bytes 256 | tf_op jit(solution)/shard_map/psum | solution.py:17
  494.7 7.7 %psum.231 = f32[32]{0:T(128)S(1)} all-reduce(f32[32]{0:T(128)S(1)} %psum.230), channel_id=1, replica_groups=mesh['sec'=2,'clu_0'=4,'clu_1'=2,'blk_0'=2,'blk_1'=8] {'clu_0'}, use_global_device_ids=true, to_apply=%region_33.39 | all-reduce | flops 32 | bytes 256 | tf_op jit(solution)/shard_map/psum | solution.py:17
  502.4 6.4 psum.232
  508.8 4.9 psum.233
  513.7 14.1 %psum.234 = f32[32]{0:T(128)S(1)} all-reduce(f32[32]{0:T(128)S(1)} %psum.233), channel_id=1, replica_groups=mesh['sec'=2,'clu_0'=4,'clu_1'=2,'blk_0'=2,'blk_1'=8] {'blk_1'}, use_global_device_ids=true, to_apply=%region_36.42 | all-reduce | flops 32 | bytes 256 | tf_op jit(solution)/shard_map/psum | solution.py:17
  535.8 17.6 %all_to_all.31 = bf16[32,32,128]{2,1,0:T(8,128)(2,1)S(1)} all-to-all(bf16[32,32,128]{2,1,0:T(8,128)(2,1)S(1)} %broadcast_in_dim.56), channel_id=1, replica_groups=mesh['sec'=2,'clu_0'=4,'clu_1'=2,'blk_0'=2,'blk_1'=8] {'sec','blk_0','bl..., dimensions={0} | all-to-all | bytes 524288 | tf_op jit(solution)/shard_map/all_to_all | solution.py:55
  554.8 15.6 %gather_fusion.11 = bf16[4096,32]{1,0:T(8,128)(2,1)} fusion(bf16[32,4096]{0,1:T(8,128)(2,1)} %bitcast.180, s32[4096]{0:T(1024)S(1)} %get-tuple-element.53), kind=kCustom, calls=%fused_computation.8.clone | custom fusion | bytes 540672 | tf_op jit(solution)/shard_map/jit(_take)/gather | solution.py:160
  570.3 4.2 broadcast_select_fusion.3
  584.4 3.3 collective-permute-start.10
  589.7 6.7 collective-permute-start.11
  596.3 42.0 %all-gather.11.cloned.1.call-done = f32[512,16,128]{2,1,0:T(8,128)} async-done(((f32[32,16,128]{2,1,0:T(8,128)}), f32[512,16,128]{2,1,0:T(8,128)}) %all-gather.11.cloned.1.call-update) | async-done | bytes 4194320 | tf_op jit(solution)/shard_map/all_gather | solution.py:63
  649.3 15.7 %gather_fusion.14 = f32[4096,32]{1,0:T(8,128)} fusion(f32[32,4096]{0,1:T(8,128)} %bitcast.173, s32[4096]{0:T(1024)S(1)} %copy-done.9), kind=kCustom, calls=%fused_computation.14.clone | custom fusion | bytes 1064960 | tf_op jit(solution)/shard_map/jit(_take)/gather | solution.py:177
  665.0 4.7 broadcast_select_fusion
  672.7 8.7 %all-to-all-start.5 = ((f32[32,32,128]{2,1,0:T(8,128)}), f32[32,32,128]{2,1,0:T(8,128)}, u32[]{:S(2)}, u32[]{:S(2)}) async-start(f32[32,32,128]{2,1,0:T(8,128)} %bitcast.195), calls=%async_computation.5 | async-start | bytes 1048576 | tf_op jit(solution)/shard_map/all_to_all | solution.py:74
  684.1 3.8 fusion.39
  688.0 3.6 copy.283
  691.6 5.3 all-to-all-done.5
  698.0 5.3 scatter_fusion.2
  703.3 3.6 copy.268
  711.2 10.1 %psum.236 = f32[32]{0:T(128)S(1)} all-reduce(f32[32]{0:T(128)S(1)} %psum.235), channel_id=1, replica_groups=mesh['sec'=2,'clu_0'=4,'clu_1'=2,'blk_0'=2,'blk_1'=8] {'clu_0'}, use_global_device_ids=true, to_apply=%region_42.48 | all-reduce | flops 32 | bytes 256 | tf_op jit(solution)/shard_map/psum | solution.py:17
  721.2 6.4 psum.237
  727.7 4.9 psum.238
  732.6 16.8 %psum.239 = f32[32]{0:T(128)S(1)} all-reduce(f32[32]{0:T(128)S(1)} %psum.238), channel_id=1, replica_groups=mesh['sec'=2,'clu_0'=4,'clu_1'=2,'blk_0'=2,'blk_1'=8] {'blk_1'}, use_global_device_ids=true, to_apply=%region_45.51 | all-reduce | flops 32 | bytes 256 | tf_op jit(solution)/shard_map/psum | solution.py:17
  (266 shorter events, 142.7 us)
Async XLA Ops:
  6.5 53.5 %copy-start = (bf16[1,1,48,128,128]{4,3,2,1,0:T(8,128)(2,1)S(1)}, bf16[1,1,48,128,128]{4,3,2,1,0:T(8,128)(2,1)}, u32[]{:S(2)}) copy-start(bf16[1,1,48,128,128]{4,3,2,1,0:T(8,128)(2,1)} %param.30) | copy-start | bytes 4718596
  8.0 268.0 %copy-start.50 = (pred[128]{0:T(512)(128)(4,1)}, pred[128]{0:T(512)(128)(4,1)S(1)}, u32[]{:S(2)}) copy-start(pred[128]{0:T(512)(128)(4,1)S(1)} %compare_and_fusion.4) | copy-start | bytes 388
  9.8 15.4 %copy-start.42 = (s32[1,1,48]{2,1,0:T(1,128)S(1)}, s32[1,1,48]{2,1,0:T(1,128)}, u32[]{:S(2)}) copy-start(s32[1,1,48]{2,1,0:T(1,128)} %param.31) | copy-start | bytes 580
  9.8 16.1 %copy-start.28 = (s32[4096]{0:T(1024)S(1)}, s32[4096]{0:T(1024)}, u32[]{:S(2)}) copy-start(s32[4096]{0:T(1024)} %param.35) | copy-start | bytes 49156
  11.6 261.8 %copy-start.36 = (s32[1024]{0:T(1024)}, s32[1024]{0:T(1024)S(1)}, u32[]{:S(2)}) copy-start(s32[1024]{0:T(1024)S(1)} %pad_clamp_fusion.2) | copy-start | bytes 12292
  15.1 21.6 %all-to-all-start = ((bf16[32,32,128]{2,1,0:T(8,128)(2,1)}), bf16[32,32,128]{2,1,0:T(8,128)(2,1)S(1)}, u32[]{:S(2)}, u32[]{:S(2)}) async-start(bf16[32,32,128]{2,1,0:T(8,128)(2,1)} %broadcast_in_dim.53), calls=%async_computation | async-start | bytes 524288 | tf_op jit(solution)/shard_map/all_to_all | solution.py:55
  25.2 95.3 %all-gather.7.cloned.1.call-start = ((), (), s32[]{:S(2)}) async-start(), calls=%async_computation.6 | async-start | bytes 4456448 | tf_op jit(solution)/shard_map/all_gather | solution.py:63
  25.3 34.8 %copy-start.48 = (pred[48]{0:T(512)(128)(4,1)}, pred[48]{0:T(512)(128)(4,1)S(1)}, u32[]{:S(2)}) copy-start(pred[48]{0:T(512)(128)(4,1)S(1)} %compare_and_fusion.3) | copy-start | bytes 148
  25.3 34.1 %copy-start.37 = (s32[1024]{0:T(1024)}, s32[1024]{0:T(1024)S(1)}, u32[]{:S(2)}) copy-start(s32[1024]{0:T(1024)S(1)} %pad_clamp_fusion.1) | copy-start | bytes 12292
  26.0 98.6 %copy-start.32 = (f32[48]{0:T(128)}, f32[48]{0:T(128)S(1)}, u32[]{:S(2)}) copy-start(f32[48]{0:T(128)S(1)} %compare_convert_fusion) | copy-start | bytes 580
  26.0 27.6 %copy-start.16 = (pred[4096]{0:T(1024)(128)(4,1)}, pred[4096]{0:T(1024)(128)(4,1)S(1)}, u32[]{:S(2)}) copy-start(pred[4096]{0:T(1024)(128)(4,1)S(1)} %compare_and_fusion.1) | copy-start | bytes 12292
  60.0 15.5 %copy-start.10 = (f32[8,8]{1,0:T(8,128)S(1)}, f32[8,8]{1,0:T(8,128)}, u32[]{:S(2)}) copy-start(f32[8,8]{1,0:T(8,128)} %param.26) | copy-start | bytes 772
  60.1 17.7 %copy-start.2 = (bf16[128,128]{1,0:T(8,128)(2,1)S(1)}, bf16[128,128]{1,0:T(8,128)(2,1)}, u32[]{:S(2)}) copy-start(bf16[128,128]{1,0:T(8,128)(2,1)} %param.29) | copy-start | bytes 98308
  60.6 17.2 %copy-start.3 = (bf16[128,128]{1,0:T(8,128)(2,1)S(1)}, bf16[128,128]{1,0:T(8,128)(2,1)}, u32[]{:S(2)}) copy-start(bf16[128,128]{1,0:T(8,128)(2,1)} %param.28) | copy-start | bytes 98308
  60.6 17.4 %copy-start.22 = (f32[8,8]{1,0:T(8,128)S(1)}, f32[8,8]{1,0:T(8,128)}, u32[]{:S(2)}) copy-start(f32[8,8]{1,0:T(8,128)} %param.25) | copy-start | bytes 772
  60.7 32.9 %copy-start.58 = (s32[1,1,128]{2,1,0:T(1,128)S(1)}, s32[1,1,128]{2,1,0:T(1,128)}, u32[]{:S(2)}) copy-start(s32[1,1,128]{2,1,0:T(1,128)} %param.34) | copy-start | bytes 1540
  62.3 97.6 %collective-permute-start.3 = (bf16[32,8,1,128]{3,0,2,1:T(8,128)(2,1)S(1)}, bf16[32,8,1,128]{3,0,2,1:T(8,128)(2,1)S(1)}, u32[]{:S(2)}, u32[]{:S(2)}) collective-permute-start(bf16[32,8,1,128]{3,0,2,1:T(8,128)(2,1)S(1)} %get-tuple-element.51), channel_id=1, source_target_pairs={{1,0},{2,1},{3,2},{4,3},{5,4},{6,5},{7,6},{8,7},{9,8},{10,9},{11,1... | collective-permute-start | bytes 196616 | tf_op jit(solution)/shard_map/ppermute | solution.py:36
  65.1 94.9 %collective-permute-start = (bf16[32,8,1,128]{3,0,2,1:T(8,128)(2,1)S(1)}, bf16[32,8,1,128]{3,0,2,1:T(8,128)(2,1)S(1)}, u32[]{:S(2)}, u32[]{:S(2)}) collective-permute-start(bf16[32,8,1,128]{3,0,2,1:T(8,128)(2,1)S(1)} %get-tuple-element.50), channel_id=1, source_target_pairs={{0,1},{1,2},{2,3},{3,4},{4,5},{5,6},{6,7},{7,8},{8,9},{9,10},{10,1... | collective-permute-start | bytes 196616 | tf_op jit(solution)/shard_map/ppermute | solution.py:35
  68.2 91.8 %collective-permute-start.2 = (bf16[32,1,8,128]{3,0,2,1:T(8,128)(2,1)S(1)}, bf16[32,1,8,128]{3,0,2,1:T(8,128)(2,1)S(1)}, u32[]{:S(2)}, u32[]{:S(2)}) collective-permute-start(bf16[32,1,8,128]{3,0,2,1:T(8,128)(2,1)S(1)} %get-tuple-element.49), channel_id=1, source_target_pairs={{16,0},{32,16},{48,32},{64,48},{80,64},{96,80},{112,96},{128,112},... | collective-permute-start | bytes 196616 | tf_op jit(solution)/shard_map/ppermute | solution.py:36
  69.5 90.5 %collective-permute-start.1 = (bf16[32,1,8,128]{3,0,2,1:T(8,128)(2,1)S(1)}, bf16[32,1,8,128]{3,0,2,1:T(8,128)(2,1)S(1)}, u32[]{:S(2)}, u32[]{:S(2)}) collective-permute-start(bf16[32,1,8,128]{3,0,2,1:T(8,128)(2,1)S(1)} %get-tuple-element.48), channel_id=1, source_target_pairs={{0,16},{16,32},{32,48},{48,64},{64,80},{80,96},{96,112},{112,128},... | collective-permute-start | bytes 196616 | tf_op jit(solution)/shard_map/ppermute | solution.py:35
  75.7 18.1 %collective-permute-start.5 = (f32[8,1]{1,0:T(8,128)S(1)}, f32[8,1]{1,0:T(8,128)S(1)}, u32[]{:S(2)}, u32[]{:S(2)}) collective-permute-start(f32[8,1]{1,0:T(8,128)S(1)} %slice.93), channel_id=1, source_target_pairs={{0,1},{1,2},{2,3},{3,4},{4,5},{5,6},{6,7},{7,8},{8,9},{9,10},{10,1... | collective-permute-start | bytes 104 | tf_op jit(solution)/shard_map/ppermute | solution.py:24
  93.6 29.4 %copy-start.38 = (s32[1024]{0:T(1024)}, s32[1024]{0:T(1024)S(1)}, u32[]{:S(2)}) copy-start(s32[1024]{0:T(1024)S(1)} %pad_clamp_fusion) | copy-start | bytes 12292
  93.6 81.6 %copy-start.45 = (s32[128]{0:T(128)}, s32[128]{0:T(128)S(1)}, u32[]{:S(2)}) copy-start(s32[128]{0:T(128)S(1)} %fusion.162) | copy-start | bytes 1540
  93.7 30.0 %copy-start.52 = (pred[48]{0:T(512)(128)(4,1)}, pred[48]{0:T(512)(128)(4,1)S(1)}, u32[]{:S(2)}) copy-start(pred[48]{0:T(512)(128)(4,1)S(1)} %compare_and_fusion.2) | copy-start | bytes 148
  93.7 49.7 %copy-start.19 = (pred[4096]{0:T(1024)(128)(4,1)}, pred[4096]{0:T(1024)(128)(4,1)S(1)}, u32[]{:S(2)}) copy-start(pred[4096]{0:T(1024)(128)(4,1)S(1)} %compare_and_fusion) | copy-start | bytes 12292
  93.7 34.0 %copy-start.7 = (s32[4096]{0:T(1024)}, s32[4096]{0:T(1024)S(1)}, u32[]{:S(2)}) copy-start(s32[4096]{0:T(1024)S(1)} %fusion.135) | copy-start | bytes 49156
  93.7 66.2 %collective-permute-start.4 = (f32[1,8]{1,0:T(1,128)S(1)}, f32[1,8]{1,0:T(1,128)S(1)}, u32[]{:S(2)}, u32[]{:S(2)}) collective-permute-start(f32[1,8]{1,0:T(1,128)S(1)} %slice.89), channel_id=1, source_target_pairs={{0,16},{16,32},{32,48},{48,64},{64,80},{80,96},{96,112},{112,128},... | collective-permute-start | bytes 104 | tf_op jit(solution)/shard_map/ppermute | solution.py:24
  98.9 62.7 %copy-start.13 = (f32[8,8]{1,0:T(8,128)}, f32[8,8]{1,0:T(8,128)S(1)}, u32[]{:S(2)}) copy-start(f32[8,8]{1,0:T(8,128)S(1)} %pad_maximum_fusion.1) | copy-start | bytes 772
  151.0 24.1 %all-to-all-start.1 = ((f32[32,32,128]{2,1,0:T(8,128)}), f32[32,32,128]{2,1,0:T(8,128)S(1)}, u32[]{:S(2)}, u32[]{:S(2)}) async-start(f32[32,32,128]{2,1,0:T(8,128)} %bitcast.32), calls=%async_computation.1 | async-start | bytes 1048576 | tf_op jit(solution)/shard_map/all_to_all | solution.py:74
  159.7 219.6 %all-gather.9.cloned.1.call-start = ((), (), s32[]{:S(2)}) async-start(), calls=%async_computation.7 | async-start | bytes 4456448 | tf_op jit(solution)/shard_map/all_gather | solution.py:63
  184.1 3.9 copy-start.1
  230.2 41.5 %copy-start.56 = (f32[32]{0:T(128)}, f32[32]{0:T(128)S(1)}, u32[]{:S(2)}) copy-start(f32[32]{0:T(128)S(1)} %div.15) | copy-start | bytes 388
  295.5 15.6 %copy-start.17 = (pred[4096]{0:T(1024)(128)(4,1)S(1)}, pred[4096]{0:T(1024)(128)(4,1)}, u32[]{:S(2)}) copy-start(pred[4096]{0:T(1024)(128)(4,1)} %copy-done.16) | copy-start | bytes 12292
  322.3 100.2 %collective-permute-start.9 = (bf16[32,8,1,128]{3,0,2,1:T(8,128)(2,1)}, bf16[32,8,1,128]{3,0,2,1:T(8,128)(2,1)}, u32[]{:S(2)}, u32[]{:S(2)}) collective-permute-start(bf16[32,8,1,128]{3,0,2,1:T(8,128)(2,1)} %get-tuple-element.47), channel_id=1, source_target_pairs={{1,0},{2,1},{3,2},{4,3},{5,4},{6,5},{7,6},{8,7},{9,8},{10,9},{11,1... | collective-permute-start | bytes 196616 | tf_op jit(solution)/shard_map/ppermute | solution.py:36
  325.0 97.5 %collective-permute-start.6 = (bf16[32,8,1,128]{3,0,2,1:T(8,128)(2,1)}, bf16[32,8,1,128]{3,0,2,1:T(8,128)(2,1)}, u32[]{:S(2)}, u32[]{:S(2)}) collective-permute-start(bf16[32,8,1,128]{3,0,2,1:T(8,128)(2,1)} %get-tuple-element.46), channel_id=1, source_target_pairs={{0,1},{1,2},{2,3},{3,4},{4,5},{5,6},{6,7},{7,8},{8,9},{9,10},{10,1... | collective-permute-start | bytes 196616 | tf_op jit(solution)/shard_map/ppermute | solution.py:35
  328.8 93.7 %collective-permute-start.8 = (bf16[32,1,8,128]{3,0,2,1:T(8,128)(2,1)}, bf16[32,1,8,128]{3,0,2,1:T(8,128)(2,1)}, u32[]{:S(2)}, u32[]{:S(2)}) collective-permute-start(bf16[32,1,8,128]{3,0,2,1:T(8,128)(2,1)} %get-tuple-element.45), channel_id=1, source_target_pairs={{16,0},{32,16},{48,32},{64,48},{80,64},{96,80},{112,96},{128,112},... | collective-permute-start | bytes 196616 | tf_op jit(solution)/shard_map/ppermute | solution.py:36
  330.1 92.4 %collective-permute-start.7 = (bf16[32,1,8,128]{3,0,2,1:T(8,128)(2,1)}, bf16[32,1,8,128]{3,0,2,1:T(8,128)(2,1)}, u32[]{:S(2)}, u32[]{:S(2)}) collective-permute-start(bf16[32,1,8,128]{3,0,2,1:T(8,128)(2,1)} %get-tuple-element.44), channel_id=1, source_target_pairs={{0,16},{16,32},{32,48},{48,64},{64,80},{80,96},{96,112},{112,128},... | collective-permute-start | bytes 196616 | tf_op jit(solution)/shard_map/ppermute | solution.py:35
  381.8 3.6 copy-start.34
  381.8 3.6 copy-start.43
  390.2 15.7 %copy-start.20 = (pred[4096]{0:T(1024)(128)(4,1)S(1)}, pred[4096]{0:T(1024)(128)(4,1)}, u32[]{:S(2)}) copy-start(pred[4096]{0:T(1024)(128)(4,1)} %copy-done.19) | copy-start | bytes 12292
  413.6 24.2 %all-to-all-start.3 = ((f32[32,32,128]{2,1,0:T(8,128)}), f32[32,32,128]{2,1,0:T(8,128)}, u32[]{:S(2)}, u32[]{:S(2)}) async-start(f32[32,32,128]{2,1,0:T(8,128)} %bitcast.196), calls=%async_computation.3 | async-start | bytes 1048576 | tf_op jit(solution)/shard_map/all_to_all | solution.py:74
  422.3 216.0 %all-gather.11.cloned.1.call-start = ((), (), s32[]{:S(2)}) async-start(), calls=%async_computation.8 | async-start | bytes 4456448 | tf_op jit(solution)/shard_map/all_gather | solution.py:63
  429.1 9.8 %copy-start.46 = (s32[128]{0:T(128)S(1)}, s32[128]{0:T(128)}, u32[]{:S(2)}) copy-start(s32[128]{0:T(128)} %copy-done.45) | copy-start | bytes 1540
  447.8 42.5 %copy-start.62 = (f32[32]{0:T(128)S(1)}, f32[32]{0:T(128)}, u32[]{:S(2)}) copy-start(f32[32]{0:T(128)} %copy-done.61) | copy-start | bytes 388
  490.3 40.8 %copy-start.54 = (f32[32]{0:T(128)}, f32[32]{0:T(128)S(1)}, u32[]{:S(2)}) copy-start(f32[32]{0:T(128)S(1)} %div.17) | copy-start | bytes 388
  527.8 3.3 copy-start.59
  531.1 4.4 copy-start.51
  554.7 15.6 %copy-start.18 = (pred[4096]{0:T(1024)(128)(4,1)S(1)}, pred[4096]{0:T(1024)(128)(4,1)}, u32[]{:S(2)}) copy-start(pred[4096]{0:T(1024)(128)(4,1)} %copy-done.16) | copy-start | bytes 12292
  570.3 7.4 copy-start.49
  576.1 3.2 copy-start.35
  576.1 3.2 copy-start.41
  581.7 99.7 %collective-permute-start.13 = (bf16[32,8,1,128]{3,0,2,1:T(8,128)(2,1)}, bf16[32,8,1,128]{3,0,2,1:T(8,128)(2,1)}, u32[]{:S(2)}, u32[]{:S(2)}) collective-permute-start(bf16[32,8,1,128]{3,0,2,1:T(8,128)(2,1)} %get-tuple-element.43), channel_id=1, source_target_pairs={{1,0},{2,1},{3,2},{4,3},{5,4},{6,5},{7,6},{8,7},{9,8},{10,9},{11,1... | collective-permute-start | bytes 196616 | tf_op jit(solution)/shard_map/ppermute | solution.py:36
  584.4 97.0 %collective-permute-start.10 = (bf16[32,8,1,128]{3,0,2,1:T(8,128)(2,1)}, bf16[32,8,1,128]{3,0,2,1:T(8,128)(2,1)}, u32[]{:S(2)}, u32[]{:S(2)}) collective-permute-start(bf16[32,8,1,128]{3,0,2,1:T(8,128)(2,1)} %get-tuple-element.42), channel_id=1, source_target_pairs={{0,1},{1,2},{2,3},{3,4},{4,5},{5,6},{6,7},{7,8},{8,9},{9,10},{10,1... | collective-permute-start | bytes 196616 | tf_op jit(solution)/shard_map/ppermute | solution.py:35
  588.4 93.0 %collective-permute-start.12 = (bf16[32,1,8,128]{3,0,2,1:T(8,128)(2,1)}, bf16[32,1,8,128]{3,0,2,1:T(8,128)(2,1)}, u32[]{:S(2)}, u32[]{:S(2)}) collective-permute-start(bf16[32,1,8,128]{3,0,2,1:T(8,128)(2,1)} %get-tuple-element.41), channel_id=1, source_target_pairs={{16,0},{32,16},{48,32},{64,48},{80,64},{96,80},{112,96},{128,112},... | collective-permute-start | bytes 196616 | tf_op jit(solution)/shard_map/ppermute | solution.py:36
  589.7 91.7 %collective-permute-start.11 = (bf16[32,1,8,128]{3,0,2,1:T(8,128)(2,1)}, bf16[32,1,8,128]{3,0,2,1:T(8,128)(2,1)}, u32[]{:S(2)}, u32[]{:S(2)}) collective-permute-start(bf16[32,1,8,128]{3,0,2,1:T(8,128)(2,1)} %get-tuple-element.40), channel_id=1, source_target_pairs={{0,16},{16,32},{32,48},{48,64},{64,80},{80,96},{96,112},{112,128},... | collective-permute-start | bytes 196616 | tf_op jit(solution)/shard_map/ppermute | solution.py:35
  638.3 4.1 copy-start.53
  640.8 3.6 copy-start.44
  646.2 3.0 copy-start.9
  649.3 15.7 %copy-start.21 = (pred[4096]{0:T(1024)(128)(4,1)S(1)}, pred[4096]{0:T(1024)(128)(4,1)}, u32[]{:S(2)}) copy-start(pred[4096]{0:T(1024)(128)(4,1)} %copy-done.19) | copy-start | bytes 12292
  672.7 24.2 %all-to-all-start.5 = ((f32[32,32,128]{2,1,0:T(8,128)}), f32[32,32,128]{2,1,0:T(8,128)}, u32[]{:S(2)}, u32[]{:S(2)}) async-start(f32[32,32,128]{2,1,0:T(8,128)} %bitcast.195), calls=%async_computation.5 | async-start | bytes 1048576 | tf_op jit(solution)/shard_map/all_to_all | solution.py:74
  688.0 10.1 %copy-start.47 = (s32[128]{0:T(128)S(1)}, s32[128]{0:T(128)}, u32[]{:S(2)}) copy-start(s32[128]{0:T(128)} %copy-done.45) | copy-start | bytes 1540
  706.9 42.5 %copy-start.60 = (f32[32]{0:T(128)S(1)}, f32[32]{0:T(128)}, u32[]{:S(2)}) copy-start(f32[32]{0:T(128)} %copy-done.59) | copy-start | bytes 388
  706.9 42.5 %copy-start.55 = (f32[32]{0:T(128)S(1)}, f32[32]{0:T(128)}, u32[]{:S(2)}) copy-start(f32[32]{0:T(128)} %copy-done.54) | copy-start | bytes 388
  706.9 42.5 %copy-start.57 = (f32[32]{0:T(128)S(1)}, f32[32]{0:T(128)}, u32[]{:S(2)}) copy-start(f32[32]{0:T(128)} %copy-done.56) | copy-start | bytes 388
  (20 other events, 22.5 us)
Sparse Core Ops, SparseCore 0:
  62.4 58.0 all-gather.6
  321.8 57.4 all-gather.8
  581.1 57.1 all-gather.10
where the time goes:
time: 771 us; the launch traced here: 760 us
  blocking collectives  229 us (30%)
  local copies, waits for them, and re-layouts  191 us (25%)
  waiting for transfers between devices  133 us (17%)
  starting transfers between devices  84.7 us (11%)
  other arithmetic  72.4 us (9%)
  matrix products  34.5 us (4%)
  between operations  15.3 us (2%)
    psum x25, blocking collectives, one_axis_at_a_time(): value = lax.psum(value, axis)  193 us
    all_gather x3, waiting for transfers between devices, gathered_total(): pieces = lax.all_gather(value, axis)  106 us
    gather x3, local copies, waits for them, and re-layouts, shards(): jnp.take(partial_rows, inverse, axis=1)  47 us
    gather x3, local copies, waits for them, and re-layouts, shards(): jnp.take(gathered, interface_slot, axis=1)  46.7 us
    all_to_all x2, blocking collectives, sent_to_all(): return lax.all_to_all(copies, axis, split_axis=0, concat_axis=0, tiled=True)  35.5 us
    ppermute x6, starting transfers between devices, with_halo(): lax.ppermute(last, axis, up)  28.9 us
    all_to_all x3, starting transfers between devices, summed_on_arrival(): lax.all_to_all(pieces, axis, split_axis=0, concat_axis=0, tiled=True)  26 us
    all_to_all x3, waiting for transfers between devices, summed_on_arrival(): lax.all_to_all(pieces, axis, split_axis=0, concat_axis=0, tiled=True)  16.3 us
  transfers between devices with their start and end apart: 21, of which 7 were waited for; matrix products, arithmetic and copies ran while one was open for 19% of the time, Pallas kernels for 0%

commit v1 on v0

v1 whole, which is shorter than its diff:
```python
import functools

import jax
import jax.numpy as jnp
from jax import lax
from jax.experimental import pallas as pl
from jax.experimental.pallas import tpu as pltpu
from jax.sharding import Mesh
from jax.sharding import PartitionSpec as P

ITERS = 3
ALL = ("sec", "clu_0", "clu_1", "blk_0", "blk_1")
SEC_CLU = ("sec", "clu_0", "clu_1")
BLK = ("blk_0", "blk_1")
CLU = ("clu_0", "clu_1")
F32 = jnp.float32
BF16 = jnp.bfloat16
SMEM = pl.BlockSpec(memory_space=pltpu.SMEM)
VMEM = pl.BlockSpec(memory_space=pltpu.VMEM)


def passed_along(value, axis, by):
    count = lax.axis_size(axis)
    pairs = [(i, i + by) for i in range(count) if 0 <= i + by < count]
    return lax.ppermute(value, axis, pairs)


def partner(value):
    return lax.ppermute(value, "sec", [(0, 1), (1, 0)])


def exchanged(pieces, axes):
    return lax.all_to_all(pieces, axes, split_axis=0, concat_axis=0, tiled=True)


def lanes_taken(rows, index):
    return jnp.take_along_axis(rows, index, axis=1)


def like(shape, dtype=F32):
    return jax.ShapeDtypeStruct(shape, dtype)


def lane_iota(shape):
    return lax.broadcasted_iota(jnp.int32, shape, len(shape) - 1)


def row_iota(shape):
    return lax.broadcasted_iota(jnp.int32, shape, len(shape) - 2)


def column_to_row(column, at):
    cases = column.shape[0]
    shape = (cases, 128)
    here = lane_iota(shape) == row_iota(shape) + at
    return jnp.sum(jnp.where(here, column, 0.0), axis=0, keepdims=True)


def row_to_column(row, at, cases):
    shape = (cases, 128)
    here = lane_iota(shape) == row_iota(shape) + at
    return jnp.sum(jnp.where(here, row, 0.0), axis=1, keepdims=True)


def trace_of(ref, case, lane_index, block_index):
    slabs, width = ref.shape[1], ref.shape[2]
    sub = row_iota((width, 128))
    total = jnp.zeros((width, 128), F32)
    for a in range(slabs):
        picked = lanes_taken(ref[case, a], lane_index)
        total = jnp.where(block_index == a * width + sub, picked, total)
    return jnp.sum(total, axis=0, keepdims=True)


def first_trace_kernel(field_ref, surface_ref, out_ref):
    copies = out_ref.shape[0]
    lane_index = jnp.broadcast_to(surface_ref[0:1, :], (8, 128))
    block_index = jnp.broadcast_to(surface_ref[1:2, :], (8, 128))

    def step(case, carry):
        row = trace_of(field_ref, case, lane_index, block_index)
        out_ref[0, pl.ds(case, 1), :] = row
        return carry

    lax.fori_loop(0, field_ref.shape[0], step, 0, unroll=4)
    value = out_ref[0]
    for i in range(1, copies):
        out_ref[i] = value


def permuted_block(source_ref, lanes_ref, blocks_ref, d):
    count, cases = source_ref.shape[0], source_ref.shape[1]
    lane_index = jnp.broadcast_to(lanes_ref[pl.ds(d, 1), :], (8, 128))
    block_index = jnp.broadcast_to(blocks_ref[pl.ds(d, 1), :], (8, 128))
    groups = cases // 8
    totals = [jnp.zeros((8, 128), F32) for _ in range(groups)]
    for b in range(count):
        here = block_index == b
        for g in range(groups):
            picked = lanes_taken(source_ref[b, 8 * g : 8 * g + 8, :], lane_index)
            totals[g] = jnp.where(here, picked, totals[g])
    return totals


def scalars_of(pieces_ref):
    return jnp.sum(pieces_ref[...], axis=0)


def alpha_beta(sums):
    norm = sums[:, 0:1]
    curvature = sums[:, 1:2]
    alpha = norm / curvature
    following = norm - 2.0 * alpha * sums[:, 2:3] + alpha * alpha * sums[:, 3:4]
    beta = jnp.maximum(following, 0.0) / norm
    return alpha, beta


def forward_kernel(first, last, *refs):
    refs = list(refs)
    rows_ref, columns_ref, live_ref, half_ref = refs[:4]
    lanes_ref, blocks_ref, boundary_ref = refs[4:7]
    refs = refs[7:]
    if first:
        mine_ref, other_ref, direction_ref, keep_ref, send_ref, low_ref = refs[:6]
        rest = refs[6:]
        count = mine_ref.shape[0]
        direction_ref[:count] = mine_ref[...]
        direction_ref[count:] = other_ref[...]
    else:
        old_residual_ref, old_direction_ref, mine_ref, other_ref, sums_ref = refs[:5]
        if last:
            keep_ref, send_ref, direction_ref, low_ref = refs[5:9]
            rest = refs[9:]
        else:
            residual_ref, direction_ref, keep_ref, send_ref, low_ref = refs[5:10]
            rest = refs[10:]
        cases = old_direction_ref.shape[1]
        count = mine_ref.shape[0]
        alpha, beta = alpha_beta(scalars_of(sums_ref))
        alpha = jnp.broadcast_to(alpha, (cases, 128))
        beta = jnp.broadcast_to(beta, (cases, 128))
        for half, image_ref in ((0, mine_ref), (1, other_ref)):
            for i in range(count):
                b = half * count + i
                residual = old_residual_ref[b] - alpha * image_ref[i, :cases, :]
                if not last:
                    residual_ref[b] = residual
                direction_ref[b] = residual + beta * old_direction_ref[b]
    cases = direction_ref.shape[1]
    groups = cases // 8

    def step(d, carry):
        totals = permuted_block(direction_ref, lanes_ref, blocks_ref, d)
        value = jnp.concatenate(totals, axis=0)
        low = value.astype(BF16)
        if last:
            left = value - low.astype(F32)
            second = left.astype(BF16)
            low_ref[d] = jnp.concatenate([low, second], axis=0)
        else:
            low_ref[d] = low
        return carry

    lax.fori_loop(0, direction_ref.shape[0], step, 0)
    half_count = keep_ref.shape[0]
    keep_ref[...] = jnp.zeros(keep_ref.shape, F32)
    send_ref[...] = jnp.zeros(send_ref.shape, F32)
    sums_scratch = rest[0]
    sums_scratch[...] = jnp.zeros(sums_scratch.shape, F32)
    live = live_ref[0]
    flip = half_ref[0] * half_count
    for p in range(boundary_ref.shape[0]):
        product = jnp.dot(low_ref[rows_ref[p]], boundary_ref[p], preferred_element_type=F32)
        product = jnp.where(p < live, product, 0.0)
        where = columns_ref[p] ^ flip
        sums_scratch[where] += product
    keep_ref[...] = sums_scratch[:half_count]
    send_ref[...] = sums_scratch[half_count:]


def backward_kernel(
    rows_ref,
    columns_ref,
    live_ref,
    half_ref,
    lanes_ref,
    blocks_ref,
    boundary_ref,
    mine_ref,
    other_ref,
    keep_ref,
    send_ref,
    low_ref,
    rows_scratch,
):
    half_count = mine_ref.shape[0]
    low_ref[:half_count] = mine_ref[...]
    low_ref[half_count:] = other_ref[...]
    rows_scratch[...] = jnp.zeros(rows_scratch.shape, F32)
    live = live_ref[0]
    flip = half_ref[0] * half_count
    for p in range(boundary_ref.shape[0]):
        product = lax.dot_general(
            low_ref[columns_ref[p] ^ flip],
            boundary_ref[p],
            (((1,), (1,)), ((), ())),
            preferred_element_type=F32,
        )
        product = jnp.where(p < live, product, 0.0)
        rows_scratch[rows_ref[p]] += product
    count = keep_ref.shape[0]
    for at, out_ref in ((0, keep_ref), (count, send_ref)):

        def step(d, carry, at=at, out_ref=out_ref):
            totals = permuted_block(rows_scratch, lanes_ref, blocks_ref, at + d)
            for g, total in enumerate(totals):
                out_ref[d, 8 * g : 8 * g + 8, :] = total
            return carry

        lax.fori_loop(0, count, step, 0)


def stiffness_kernel(
    want_trace,
    direction_ref,
    residual_ref,
    before_ref,
    after_ref,
    left_ref,
    right_ref,
    weights_ref,
    matrices_ref,
    surface_ref,
    *out_refs,
):
    if want_trace:
        image_ref, trace_ref, dots_ref, low_ref, high_ref, sums_ref = out_refs
    else:
        dots_ref, image_ref, low_ref, high_ref, sums_ref = out_refs
    cases, slabs, width = direction_ref.shape[:3]
    rows = cases * width

    def product(value, which):
        return jnp.dot(
            value.reshape(rows, 128), matrices_ref[which], preferred_element_type=F32
        ).reshape(cases, width, 128)

    def low(a):
        if a < 0:
            return before_ref[...]
        if a == slabs:
            return after_ref[...]
        return direction_ref[:, a].astype(BF16)

    high_ref[...] = product(right_ref[...], 3)
    low_ref[...] = product(left_ref[...], 4)
    for a in range(slabs):
        own = low(a)
        result = weights_ref[0, a][None] * product(own, 0)
        result = result - weights_ref[1, a][None] * product(low(a + 1), 1)
        result = result - weights_ref[2, a][None] * product(low(a - 1), 2)
        result = result - weights_ref[3, a][None] * pltpu.roll(product(own, 3), width - 1, 1)
        result = result - weights_ref[4, a][None] * pltpu.roll(product(own, 4), 1, 1)
        result = result - weights_ref[5, a][None] * high_ref[:, a : a + 1, :]
        result = result - weights_ref[6, a][None] * low_ref[:, a : a + 1, :]
        image_ref[:, a] = result
    lane_index = jnp.broadcast_to(surface_ref[0:1, :], (8, 128))
    block_index = jnp.broadcast_to(surface_ref[1:2, :], (8, 128))

    def step(case, carry):
        r = residual_ref[case]
        d = direction_ref[case]
        q = image_ref[case]
        pairs = ((r, r), (d, q), (r, q), (q, q)) if want_trace else ((r, r), (d, q))
        for i, (one, two) in enumerate(pairs):
            sums_ref[i, pl.ds(case, 1), :] = jnp.sum(
                jnp.sum(one * two, axis=0), axis=0, keepdims=True
            )
        if want_trace:
            trace_ref[pl.ds(case, 1), :] = trace_of(image_ref, case, lane_index, block_index)
        return carry

    lax.fori_loop(0, cases, step, 0, unroll=4)
    lane = lane_iota((cases, 128))
    dots = jnp.zeros((cases, 128), F32)
    for i in range(4 if want_trace else 2):
        dots = jnp.where(lane == i, jnp.sum(sums_ref[i], axis=1, keepdims=True), dots)
    dots_ref[...] = dots


def own_kernel(
    place_ref, arrived_ref, trace_ref, dots_ref, residual_ref, direction_ref, out_ref, own_ref
):
    copies, cases = out_ref.shape[0], trace_ref.shape[0]
    y = jnp.sum(arrived_ref[...], axis=0)
    own_ref[...] = y
    trace = trace_ref[...]
    r = residual_ref[place_ref[0]]
    d = direction_ref[place_ref[0]]
    dots = dots_ref[...]
    terms = (None, d * y, r * y, (2.0 * trace + y) * y)
    row = jnp.zeros((1, 128), F32)
    for i, term in enumerate(terms):
        column = dots[:, i : i + 1]
        if term is not None:
            column = column + jnp.sum(term, axis=1, keepdims=True)
        row = row + column_to_row(column, i * cases)
    image = trace + y
    row8 = jnp.broadcast_to(row, (8, 128))
    for i in range(copies):
        out_ref[i, :cases, :] = image
        out_ref[i, cases:, :] = row8


def range_sum_kernel(mine_ref, other_ref, out_ref):
    copies, cases = out_ref.shape[0], out_ref.shape[1]
    row = jnp.sum(mine_ref[:, cases : cases + 8, :], axis=0) + jnp.sum(
        other_ref[:, cases : cases + 8, :], axis=0
    )
    row = row[0:1, :]
    lane = lane_iota((cases, 128))
    sums = jnp.zeros((cases, 128), F32)
    for i in range(4):
        sums = jnp.where(lane == i, row_to_column(row, i * cases, cases), sums)
    for i in range(copies):
        out_ref[i] = sums


def update_kernel(first, *refs):
    if first:
        sums_ref, own_ref, inverse_ref, image_ref, residual_ref, direction_ref = refs[:6]
        solution_ref = None
        refs = refs[6:]
    else:
        sums_ref, own_ref, inverse_ref, image_ref, residual_ref, direction_ref, solution_ref = refs[
            :7
        ]
        refs = refs[7:]
    new_solution_ref, new_residual_ref, new_direction_ref, alpha_ref, beta_ref = refs
    cases, slabs, width = direction_ref.shape[:3]
    alpha, beta = alpha_beta(scalars_of(sums_ref))
    alpha_ref[...] = jnp.broadcast_to(alpha, (cases, 128))
    beta_ref[...] = jnp.broadcast_to(beta, (cases, 128))

    def step(case, carry):
        alpha = jnp.broadcast_to(alpha_ref[pl.ds(case, 1), :], (width, 128))
        beta = jnp.broadcast_to(beta_ref[pl.ds(case, 1), :], (width, 128))
        own = jnp.broadcast_to(own_ref[pl.ds(case, 1), :], (width, 128))
        for a in range(slabs):
            slot = inverse_ref[a]
            there = slot > 0
            extra = lanes_taken(own, jnp.where(there, slot - 1, 0))
            image = image_ref[case, a] + jnp.where(there, extra, 0.0)
            d = direction_ref[case, a]
            r = residual_ref[case, a] - alpha * image
            new_residual_ref[case, a] = r
            moved = alpha * d
            if solution_ref is not None:
                moved = solution_ref[case, a] + moved
            new_solution_ref[case, a] = moved
            new_direction_ref[case, a] = r + beta * d
        return carry

    lax.fori_loop(0, cases, step, 0, unroll=2)


def last_sums_kernel(arrived_ref, dots_ref, out_ref):
    copies = out_ref.shape[0]
    cases = dots_ref.shape[0]
    total = jnp.sum(arrived_ref[...], axis=0)
    z = total[:cases]
    rest = total[cases:]
    low = z.astype(BF16).astype(F32)
    dots = dots_ref[...]
    curvature = dots[:, 1:2] + jnp.sum((z + rest) * low, axis=1, keepdims=True)
    row = column_to_row(dots[:, 0:1], 0) + column_to_row(curvature, cases)
    out_ref[...] = jnp.broadcast_to(row[None], (copies, 1, 128))


def final_kernel(sums_ref, direction_ref, solution_ref, out_ref, alpha_ref):
    cases, slabs, width = direction_ref.shape[:3]
    row = jnp.sum(sums_ref[...], axis=0)
    norm = row_to_column(row, 0, cases)
    curvature = row_to_column(row, cases, cases)
    alpha_ref[...] = jnp.broadcast_to(norm / curvature, (cases, 128))

    def step(case, carry):
        alpha = jnp.broadcast_to(alpha_ref[pl.ds(case, 1), :], (width, 128))
        for a in range(slabs):
            out_ref[case, a] = solution_ref[case, a] + alpha * direction_ref[case, a]
        return carry

    lax.fori_loop(0, cases, step, 0, unroll=2)


def shards(
    right_side,
    block_weight,
    across_weight,
    along_weight,
    block_stiffness,
    across_matrix,
    along_matrix,
    boundary_blocks,
    block_rows,
    block_columns,
    live_pairs,
    surface_index,
    interface_slot,
):
    cases, slabs, width, lanes = right_side.shape
    field = right_side.shape
    rows_local = block_rows[0, 0]
    columns_local = block_columns[0, 0]
    blocks_local = boundary_blocks[0, 0]
    live_local = live_pairs[0, 0]
    surface_local = surface_index[0, 0]
    half = lax.axis_index("sec").astype(jnp.int32)
    place = lax.axis_index(BLK).astype(jnp.int32)
    half_local = half.reshape(1)
    place_local = place.reshape(1)
    blk_count = lax.axis_size(BLK)
    clu_count = lax.axis_size(CLU)
    owners = 2 * blk_count
    all_count = owners * clu_count
    slot_count = interface_slot.shape[0]
    surface = jnp.stack([surface_local % lanes, surface_local // lanes])

    trace = pl.pallas_call(
        first_trace_kernel,
        out_shape=like((blk_count, cases, lanes)),
        name="first_trace",
    )(right_side, surface)
    mine = exchanged(trace, BLK)
    other = partner(mine)

    owner = (interface_slot // lanes) ^ (half * blk_count)
    slot_blocks = owner.reshape(slot_count // lanes, lanes)
    slot_lanes = (interface_slot % lanes).reshape(slot_count // lanes, lanes)
    number = jnp.arange(slot_count, dtype=jnp.int32)
    lane_number = jnp.arange(lanes, dtype=jnp.int32)
    by_owner = (jnp.arange(owners, dtype=jnp.int32)[:, None] == owner[None, :]).astype(BF16)
    by_lane = (interface_slot % lanes)[:, None] == lane_number[None, :]
    parts = jnp.concatenate(
        [
            jnp.where(by_lane, (number // lanes)[:, None], 0),
            jnp.where(by_lane, (number % lanes)[:, None], 0),
        ],
        axis=1,
    ).astype(BF16)
    found = jnp.dot(by_owner, parts, preferred_element_type=F32).astype(jnp.int32)
    dof_blocks, dof_lanes = found[:, :lanes], found[:, lanes:]
    by_block = (
        jnp.arange(slabs * width, dtype=jnp.int32)[:, None] == (surface_local // lanes)[None, :]
    ).astype(BF16)
    marks = jnp.where(
        (surface_local % lanes)[:, None] == lane_number[None, :],
        jnp.arange(1, surface_local.shape[0] + 1, dtype=jnp.int32)[:, None],
        0,
    ).astype(BF16)
    inverse = (
        jnp.dot(by_block, marks, preferred_element_type=F32)
        .astype(jnp.int32)
        .reshape(slabs, width, lanes)
    )

    across_edge = passed_along(across_weight[-1:, :], SEC_CLU, 1)
    across_lower = jnp.concatenate([across_edge, across_weight[:-1, :]], axis=0)
    along_edge = passed_along(along_weight[:, -1:], BLK, 1)
    along_lower = jnp.concatenate([along_edge, along_weight[:, :-1]], axis=1)
    tile = jnp.arange(width, dtype=jnp.int32)[None, :]
    weights = jnp.stack(
        [
            block_weight,
            across_weight,
            across_lower,
            jnp.where(tile < width - 1, along_weight, 0.0),
            jnp.where(tile > 0, along_lower, 0.0),
            jnp.where(tile == width - 1, along_weight, 0.0),
            jnp.where(tile == 0, along_lower, 0.0),
        ]
    )
    weights = jnp.broadcast_to(weights[..., None], (*weights.shape, lanes))
    matrices = jnp.stack(
        [block_stiffness, across_matrix, across_matrix.T, along_matrix, along_matrix.T]
    )

    half_columns = clu_count
    slots_shape = (owners, cases, lanes)
    forward_inputs = (rows_local, columns_local, live_local, half_local)
    forward_inputs += (slot_lanes, slot_blocks, blocks_local)
    forward_specs = [SMEM] * 4 + [VMEM] * 3
    solution = None
    residual = right_side
    direction = right_side
    slot_residual = slot_direction = sums = None
    for iteration in range(ITERS):
        first = iteration == 0
        last = iteration + 1 == ITERS
        deep = 2 * cases if last else cases
        scratch = [
            pltpu.VMEM((slot_count // lanes, deep, lanes), BF16),
            pltpu.VMEM((2 * half_columns, deep, lanes), F32),
        ]
        halves = (like((half_columns, deep, lanes)),) * 2
        if first:
            slot_direction, keep, send = pl.pallas_call(
                functools.partial(forward_kernel, True, False),
                out_shape=(like(slots_shape), *halves),
                in_specs=forward_specs + [VMEM] * 2,
                scratch_shapes=scratch,
                name="forward_first",
            )(*forward_inputs, mine, other)
            slot_residual = slot_direction
        elif not last:
            slot_residual, slot_direction, keep, send = pl.pallas_call(
                functools.partial(forward_kernel, False, False),
                out_shape=(like(slots_shape), like(slots_shape), *halves),
                in_specs=forward_specs + [VMEM] * 5,
                scratch_shapes=scratch,
                name="forward",
            )(*forward_inputs, slot_residual, slot_direction, mine, other, sums)
        else:
            keep, send = pl.pallas_call(
                functools.partial(forward_kernel, False, True),
                out_shape=halves,
                in_specs=forward_specs + [VMEM] * 5,
                scratch_shapes=[pltpu.VMEM(slots_shape, F32)] + scratch,
                name="forward_last",
            )(*forward_inputs, slot_residual, slot_direction, mine, other, sums)
        column_pieces = exchanged(keep + partner(send), CLU)

        if not first:
            inputs = (sums, own, inverse, image, residual, direction)
            if iteration > 1:
                inputs += (solution,)
            solution, residual, direction = pl.pallas_call(
                functools.partial(update_kernel, iteration == 1),
                out_shape=(like(field),) * 3,
                scratch_shapes=[pltpu.VMEM((cases, lanes), F32)] * 2,
                name="update",
            )(*inputs)
        rounded_before = direction[:, -1].astype(BF16)
        rounded_after = direction[:, 0].astype(BF16)
        rounded_left = direction[:, :, -1].astype(BF16)
        rounded_right = direction[:, :, 0].astype(BF16)
        before = passed_along(rounded_before, SEC_CLU, 1)
        after = passed_along(rounded_after, SEC_CLU, -1)
        left = passed_along(rounded_left, BLK, 1)
        right = passed_along(rounded_right, BLK, -1)
        stiffness_inputs = (direction, residual, before, after, left, right)
        stiffness_inputs += (weights, matrices, surface)
        edges = [pltpu.VMEM((cases, slabs, lanes), F32)] * 2
        edges += [pltpu.VMEM((4, cases, lanes), F32)]
        if last:
            dots = pl.pallas_call(
                functools.partial(stiffness_kernel, False),
                out_shape=like((cases, lanes)),
                scratch_shapes=[pltpu.VMEM(field, F32)] + edges,
                name="stiffness_last",
            )(*stiffness_inputs)
            rows = pl.pallas_call(
                last_sums_kernel,
                out_shape=like((all_count, 1, lanes)),
                name="last_sums",
            )(column_pieces, dots)
            totals = exchanged(rows, ALL)
            return pl.pallas_call(
                final_kernel,
                out_shape=like(field),
                scratch_shapes=[pltpu.VMEM((cases, lanes), F32)],
                name="final",
            )(totals, direction, solution)
        image, image_trace, dots = pl.pallas_call(
            functools.partial(stiffness_kernel, True),
            out_shape=(like(field), like((cases, lanes)), like((cases, lanes))),
            scratch_shapes=edges,
            name="stiffness",
        )(*stiffness_inputs)

        z_low = column_pieces.sum(axis=0).astype(BF16)
        low_mine = exchanged(jnp.broadcast_to(z_low, (clu_count, *z_low.shape)), CLU)
        low_other = partner(low_mine)
        keep, send = pl.pallas_call(
            backward_kernel,
            out_shape=(like((blk_count, cases, lanes)),) * 2,
            in_specs=[SMEM] * 4 + [VMEM] * 5,
            scratch_shapes=[
                pltpu.VMEM((2 * half_columns, cases, lanes), BF16),
                pltpu.VMEM((slot_count // lanes, cases, lanes), F32),
            ],
            name="backward",
        )(
            rows_local,
            columns_local,
            live_local,
            half_local,
            dof_lanes,
            dof_blocks,
            blocks_local,
            low_mine,
            low_other,
        )
        arrived = exchanged(keep + partner(send), BLK)
        payload, own = pl.pallas_call(
            own_kernel,
            out_shape=(like((blk_count, cases + 8, lanes)), like((cases, lanes))),
            in_specs=[SMEM] + [VMEM] * 5,
            name="own",
        )(place_local, arrived, image_trace, dots, slot_residual, slot_direction)
        mine = exchanged(payload, BLK)
        other = partner(mine)
        range_sums = pl.pallas_call(
            range_sum_kernel,
            out_shape=like((clu_count, cases, lanes)),
            name="range_sums",
        )(mine, other)
        sums = exchanged(range_sums, CLU)


def solution(mesh):
    finer = Mesh(
        mesh.devices.reshape(mesh.shape["sec"], 4, 2, 2, 8),
        ("sec", "clu_0", "clu_1", "blk_0", "blk_1"),
    )
    placed = (
        P(None, SEC_CLU, BLK, None),
        P(SEC_CLU, BLK),
        P(SEC_CLU, BLK),
        P(SEC_CLU, BLK),
        P(),
        P(),
        P(),
        P("sec", CLU, BLK, None, None),
        P("sec", CLU, BLK),
        P("sec", CLU, BLK),
        P("sec", CLU, BLK),
        P("sec", CLU, BLK),
        P(CLU),
    )
    return jax.shard_map(
        shards, mesh=finer, in_specs=placed, out_specs=P(None, SEC_CLU, BLK, None), check_vma=False
    )
```

time: 771 us -> 342 us (0.44)
  local copies, waits for them, and re-layouts: 191 us -> 13 us
  blocking collectives: 229 us -> 104 us
  waiting for transfers between devices: 133 us -> 33.6 us
  Pallas kernels: 0 us -> 85.3 us
  other arithmetic: 72.4 us -> 10.8 us
  matrix products: 34.5 us -> 1.28 us
  between operations: 15.3 us -> 1.35 us
    psum x25 -> x0, blocking collectives: 193 us -> none  [one_axis_at_a_time(): value = lax.psum(value, axis)]
    gather x15 -> x0, local copies, waits for them, and re-layouts: 109 us -> none  [the longest x3 47 us: shards(): jnp.take(partial_rows, inverse, axis=1)]
    all_gather x3 -> x0, waiting for transfers between devices: 106 us -> none  [gathered_total(): pieces = lax.all_gather(value, axis)]
    pallas_call x0 -> x17, Pallas kernels: none -> 85.3 us  [the longest x2 19.4 us: shards(): pl.pallas_call(backward_kernel, out_shape=(like((blk_count, cases, lanes)...]
    all_to_all x2 -> x7, blocking collectives: 35.5 us -> 104 us  [exchanged(): return lax.all_to_all(pieces, axes, split_axis=0, concat_axis=0, tiled=True)]
    reshape x19 -> x0, local copies, waits for them, and re-layouts: 52.5 us -> none  [the longest x4 14.7 us: shards(): image_field = result.reshape(count_cases, -1).at[:, surface_local].add(ow...]
    ppermute x2 -> x14, starting transfers between devices: 7.19 us -> 41.8 us  [passed_along(): return lax.ppermute(value, axis, pairs)]
    ppermute x12 -> x10, starting transfers between devices: 41 us -> 6.63 us  [partner(): return lax.ppermute(value, 'sec', [(0, 1), (1, 0)])]
  transfers between devices with their start and end apart: 21 -> 30, of which waited for: 7 -> 15; matrix products, arithmetic and copies ran while one was open for 19% -> 5% of each run, Pallas kernels for 0% -> 12%
where the time goes in v1:
time: 342 us; the launch traced here: 338 us
  blocking collectives  104 us (30%)
  starting transfers between devices  88.1 us (26%)
  Pallas kernels  85.3 us (25%)
  waiting for transfers between devices  33.6 us (10%)
  local copies, waits for them, and re-layouts  13 us (4%)
  other arithmetic  10.8 us (3%)
    all_to_all x7, blocking collectives, exchanged(): return lax.all_to_all(pieces, axes, split_axis=0, concat_axis=0, tiled=True)  104 us
    ppermute x14, starting transfers between devices, passed_along(): return lax.ppermute(value, axis, pairs)  41.8 us
    all_to_all x6, starting transfers between devices, exchanged(): return lax.all_to_all(pieces, axes, split_axis=0, concat_axis=0, tiled=True)  39.6 us
    pallas_call x2, Pallas kernels, shards(): pl.pallas_call(backward_kernel, out_shape=(like((blk_count, cases, lanes)...  19.4 us
    all_to_all x6, waiting for transfers between devices, exchanged(): return lax.all_to_all(pieces, axes, split_axis=0, concat_axis=0, tiled=True)  19.2 us
    pallas_call x2, Pallas kernels, shards(): pl.pallas_call(functools.partial(update_kernel, iteration == 1), out_shap...  11.4 us
    pallas_call x1, Pallas kernels, shards(): pl.pallas_call(functools.partial(forward_kernel, False, True), out_shape=...  10.3 us
    ppermute x10, waiting for transfers between devices, partner(): return lax.ppermute(value, 'sec', [(0, 1), (1, 0)])  10.2 us
  transfers between devices with their start and end apart: 30, of which 15 were waited for; matrix products, arithmetic and copies ran while one was open for 5% of the time, Pallas kernels for 12%

profile of v1, /device:TPU:8, one launch (start us, length us, event | category | flops | bytes accessed | tf_op | source)
XLA Modules:
  0.0 337.6 jit_solution(17565781262616243936)
XLA Ops:
  1.3 2.8 first_trace.1
  4.2 10.1 %all-to-all-start = ((f32[16,32,128]{2,1,0:T(8,128)}), f32[16,32,128]{2,1,0:T(8,128)S(1)}, u32[]{:S(2)}, u32[]{:S(2)}) async-start(f32[16,32,128]{2,1,0:T(8,128)} %first_trace.1), calls=%async_computation | async-start | bytes 524288 | tf_op jit(solution)/shard_map/all_to_all | solution.py:33
  14.8 4.2 %collective-permute-start.4 = (bf16[32,8,128]{2,1,0:T(8,128)(2,1)S(1)}, bf16[32,8,128]{2,1,0:T(8,128)(2,1)S(1)}, u32[]{:S(2)}, u32[]{:S(2)}) collective-permute-start(bf16[32,8,128]{2,1,0:T(8,128)(2,1)S(1)} %bitcast.114), channel_id=1, source_target_pairs={{0,16},{16,32},{32,48},{48,64},{64,80},{80,96},{96,112},{112,128},... | collective-permute-start | bytes 196616 | tf_op jit(solution)/shard_map/ppermute | solution.py:25
  19.1 1.3 collective-permute-start.5
  20.4 3.4 collective-permute-start.6
  23.8 4.6 %collective-permute-start.7 = (bf16[32,8,128]{2,1,0:T(8,128)(2,1)S(1)}, bf16[32,8,128]{2,1,0:T(8,128)(2,1)S(1)}, u32[]{:S(2)}, u32[]{:S(2)}) collective-permute-start(bf16[32,8,128]{2,1,0:T(8,128)(2,1)S(1)} %get-tuple-element.71), channel_id=1, source_target_pairs={{1,0},{2,1},{3,2},{4,3},{5,4},{6,5},{7,6},{8,7},{9,8},{10,9},{11,1... | collective-permute-start | bytes 196616 | tf_op jit(solution)/shard_map/ppermute | solution.py:25
  29.0 2.9 select_convert_fusion.1
  33.3 2.5 collective-permute-start
  37.7 7.3 %forward_first.1 = (f32[32,32,128]{2,1,0:T(8,128)}, f32[8,32,128]{2,1,0:T(8,128)}, f32[8,32,128]{2,1,0:T(8,128)}) custom-call(s32[48]{0:T(128)} %bitcast.123, s32[48]{0:T(128)} %bitcast.128, s32[1]{0:T(128)} %bitcast.101.refs_2_, s32[1]{0:T(128)} %bitcast.3.refs_3_.half_ref, s32[32,128]{1,0:T(8,128)} %get-tuple-element.80.refs_4_, s32[32,128]{1,0:T(8,128)} %bitcast.111, ...), custom_call_target="tpu_custom_call" | custom-call | tf_op jit(solution)/shard_map/forward_first/pallas_call | solution.py:507
  45.4 1.2 collective-permute-done.1
  46.6 1.6 add.82
  48.2 5.9 %all-to-all-start.1 = ((f32[8,32,128]{2,1,0:T(8,128)}), f32[8,32,128]{2,1,0:T(8,128)S(1)}, u32[]{:S(2)}, u32[]{:S(2)}) async-start(f32[8,32,128]{2,1,0:T(8,128)} %add.82), calls=%async_computation.1 | async-start | bytes 262144 | tf_op jit(solution)/shard_map/all_to_all | solution.py:33
  54.1 7.8 %all-to-all-done.1 = f32[8,32,128]{2,1,0:T(8,128)S(1)} async-done(((f32[8,32,128]{2,1,0:T(8,128)}), f32[8,32,128]{2,1,0:T(8,128)S(1)}, u32[]{:S(2)}, u32[]{:S(2)}) %all-to-all-start.1) | async-done | bytes 131104 | tf_op jit(solution)/shard_map/all_to_all | solution.py:33
  62.6 3.4 all-to-all-start.2
  66.0 7.7 %all-to-all-done.2.mine_ref = bf16[8,32,128]{2,1,0:T(8,128)(2,1)S(1)} async-done(((bf16[8,32,128]{2,1,0:T(8,128)(2,1)}), bf16[8,32,128]{2,1,0:T(8,128)(2,1)S(1)}, u32[]{:S(2)}, u32[]{:S(2)}) %all-to-all-start.2) | async-done | bytes 65568 | tf_op jit(solution)/shard_map/all_to_all | solution.py:33
  73.7 1.2 collective-permute-done.2.other_ref
  74.9 2.7 collective-permute-start.8
  77.7 9.7 %backward.2 = (f32[16,32,128]{2,1,0:T(8,128)}, f32[16,32,128]{2,1,0:T(8,128)}) custom-call(s32[48]{0:T(128)} %bitcast.124, s32[48]{0:T(128)} %bitcast.129, s32[1]{0:T(128)} %bitcast.102.live_ref, s32[1]{0:T(128)} %bitcast.3.refs_3_.half_ref, s32[32,128]{1,0:T(8,128)} %get-tuple-element.76.lanes_ref, s32[32,128]{1,0:T(8,128)} %get-tuple-element.75.blocks_ref, ...), custom_call_target="tpu_custom_call" | custom-call | tf_op jit(solution)/shard_map/backward/pallas_call | solution.py:584
  87.4 1.7 collective-permute-done.3
  89.1 1.9 collective-permute-start.9
  91.1 1.7 add.83
  92.8 7.8 %all-to-all-start.3 = ((f32[16,32,128]{2,1,0:T(8,128)}), f32[16,32,128]{2,1,0:T(8,128)S(1)}, u32[]{:S(2)}, u32[]{:S(2)}) async-start(f32[16,32,128]{2,1,0:T(8,128)} %add.83), calls=%async_computation.3 | async-start | bytes 524288 | tf_op jit(solution)/shard_map/all_to_all | solution.py:33
  101.6 4.6 %stiffness.2 = (f32[32,8,8,128]{3,2,1,0:T(8,128)}, f32[32,128]{1,0:T(8,128)}, f32[32,128]{1,0:T(8,128)}) custom-call(f32[32,8,8,128]{3,2,1,0:T(8,128)} %refs_5_.1, f32[32,8,8,128]{3,2,1,0:T(8,128)} %refs_5_.1, bf16[32,8,128]{2,1,0:T(8,128)(2,1)} %copy-done.18, bf16[32,8,128]{2,1,0:T(8,128)(2,1)} %copy-done.19, bf16[32,8,128]{2,1,0:T(8,128)(2,1)} %copy-done.20, ...), custom_call_target="tpu_custom_call" | custom-call | tf_op jit(solution)/shard_map/stiffness/pallas_call | solution.py:574
  106.2 3.7 %all-to-all-done.3.arrived_ref = f32[16,32,128]{2,1,0:T(8,128)S(1)} async-done(((f32[16,32,128]{2,1,0:T(8,128)}), f32[16,32,128]{2,1,0:T(8,128)S(1)}, u32[]{:S(2)}, u32[]{:S(2)}) %all-to-all-start.3) | async-done | bytes 262176 | tf_op jit(solution)/shard_map/all_to_all | solution.py:33
  110.6 2.3 own.2
  112.9 15.5 %all_to_all.65.mine_ref.refs_9_ = f32[16,40,128]{2,1,0:T(8,128)S(1)} all-to-all(f32[16,40,128]{2,1,0:T(8,128)} %get-tuple-element.41), channel_id=1, replica_groups=mesh['sec'=2,'clu_0'=4,'clu_1'=2,'blk_0'=2,'blk_1'=8] {'blk_0','blk_1'}, dimensions={0} | all-to-all | bytes 655360 | tf_op jit(solution)/shard_map/all_to_all | solution.py:33
  128.4 1.6 collective-permute-done.10.other_ref.refs_10_
  130.7 1.8 range_sums.2
  132.6 13.9 %all_to_all.66.refs_11_.refs_0_ = f32[8,32,128]{2,1,0:T(8,128)} all-to-all(f32[8,32,128]{2,1,0:T(8,128)} %range_sums.2), channel_id=1, replica_groups=mesh['sec'=2,'clu_0'=4,'clu_1'=2,'blk_0'=2,'blk_1'=8] {'clu_0','clu_1'}, dimensions={0} | all-to-all | bytes 262144 | tf_op jit(solution)/shard_map/all_to_all | solution.py:33
  146.4 8.2 %forward.1 = (f32[32,32,128]{2,1,0:T(8,128)}, f32[32,32,128]{2,1,0:T(8,128)}, f32[8,32,128]{2,1,0:T(8,128)}, f32[8,32,128]{2,1,0:T(8,128)}) custom-call(s32[48]{0:T(128)} %bitcast.125, s32[48]{0:T(128)} %bitcast.130, s32[1]{0:T(128)} %bitcast.103.refs_2_, s32[1]{0:T(128)} %bitcast.3.refs_3_.half_ref, s32[32,128]{1,0:T(8,128)} %get-tuple-element.80.refs_4_, ...), custom_call_target="tpu_custom_call" | custom-call | tf_op jit(solution)/shard_map/forward/pallas_call | solution.py:516
  154.7 1.5 collective-permute-done.11
  156.3 0.9 add.84
  157.2 10.6 %all_to_all.67 = f32[8,32,128]{2,1,0:T(8,128)S(1)} all-to-all(f32[8,32,128]{2,1,0:T(8,128)S(1)} %add.84), channel_id=1, replica_groups=mesh['sec'=2,'clu_0'=4,'clu_1'=2,'blk_0'=2,'blk_1'=8] {'clu_0','clu_1'}, dimensions={0} | all-to-all | bytes 262144 | tf_op jit(solution)/shard_map/all_to_all | solution.py:33
  167.9 10.5 %all_to_all.68.mine_ref = bf16[8,32,128]{2,1,0:T(8,128)(2,1)S(1)} all-to-all(bf16[8,32,128]{2,1,0:T(8,128)(2,1)S(1)} %broadcast_in_dim.97), channel_id=1, replica_groups=mesh['sec'=2,'clu_0'=4,'clu_1'=2,'blk_0'=2,'blk_1'=8] {'clu_0','clu_1'}, dimensions={0} | all-to-all | bytes 131072 | tf_op jit(solution)/shard_map/all_to_all | solution.py:33
  178.3 1.3 collective-permute-done.12.other_ref
  180.2 9.7 %backward.3 = (f32[16,32,128]{2,1,0:T(8,128)}, f32[16,32,128]{2,1,0:T(8,128)}) custom-call(s32[48]{0:T(128)} %bitcast.126, s32[48]{0:T(128)} %bitcast.131, s32[1]{0:T(128)} %bitcast.104.live_ref, s32[1]{0:T(128)} %bitcast.3.refs_3_.half_ref, s32[32,128]{1,0:T(8,128)} %get-tuple-element.76.lanes_ref, s32[32,128]{1,0:T(8,128)} %get-tuple-element.75.blocks_ref, ...), custom_call_target="tpu_custom_call" | custom-call | tf_op jit(solution)/shard_map/backward/pallas_call | solution.py:584
  190.9 5.5 %update.2 = (f32[32,8,8,128]{3,2,1,0:T(8,128)}, f32[32,8,8,128]{3,2,1,0:T(8,128)}, f32[32,8,8,128]{3,2,1,0:T(8,128)}) custom-call(f32[8,32,128]{2,1,0:T(8,128)} %all_to_all.66.refs_11_.refs_0_, f32[32,128]{1,0:T(8,128)} %get-tuple-element.48.refs_1_, s32[8,8,128]{2,1,0:T(8,128)} %fusion.7.refs_2_, f32[32,8,8,128]{3,2,1,0:T(8,128)} %get-tuple-element.49.refs_3_, ...), custom_call_target="tpu_custom_call" | custom-call | tf_op jit(solution)/shard_map/update/pallas_call | solution.py:537
  196.4 1.5 copy.48
  198.7 5.8 %all-to-all-start.8 = ((f32[16,32,128]{2,1,0:T(8,128)}), f32[16,32,128]{2,1,0:T(8,128)S(1)}, u32[]{:S(2)}, u32[]{:S(2)}) async-start(f32[16,32,128]{2,1,0:T(8,128)} %add.85), calls=%async_computation.8 | async-start | bytes 524288 | tf_op jit(solution)/shard_map/all_to_all | solution.py:33
  204.8 2.3 collective-permute-start.14
  207.3 1.3 collective-permute-start.15
  208.6 3.4 collective-permute-start.16
  212.0 4.6 %collective-permute-start.17 = (bf16[32,8,128]{2,1,0:T(8,128)(2,1)S(1)}, bf16[32,8,128]{2,1,0:T(8,128)(2,1)S(1)}, u32[]{:S(2)}, u32[]{:S(2)}) collective-permute-start(bf16[32,8,128]{2,1,0:T(8,128)(2,1)S(1)} %get-tuple-element.67), channel_id=1, source_target_pairs={{1,0},{2,1},{3,2},{4,3},{5,4},{6,5},{7,6},{8,7},{9,8},{10,9},{11,1... | collective-permute-start | bytes 196616 | tf_op jit(solution)/shard_map/ppermute | solution.py:25
  216.9 1.6 collective-permute-done.17.right_ref
  219.1 4.5 %stiffness.3 = (f32[32,8,8,128]{3,2,1,0:T(8,128)}, f32[32,128]{1,0:T(8,128)}, f32[32,128]{1,0:T(8,128)}) custom-call(f32[32,8,8,128]{3,2,1,0:T(8,128)} %get-tuple-element.50.direction_ref.refs_5_, f32[32,8,8,128]{3,2,1,0:T(8,128)} %get-tuple-element.51.residual_ref.refs_4_, bf16[32,8,128]{2,1,0:T(8,128)(2,1)} %copy-done.24, bf16[32,8,128]{2,1,0:T(8,128)(2,1)} %copy-done.25, ...), custom_call_target="tpu_custom_call" | custom-call | tf_op jit(solution)/shard_map/stiffness/pallas_call | solution.py:574
  224.2 2.3 own.3
  226.5 16.3 %all_to_all.69.mine_ref.refs_9_ = f32[16,40,128]{2,1,0:T(8,128)S(1)} all-to-all(f32[16,40,128]{2,1,0:T(8,128)} %get-tuple-element.54), channel_id=1, replica_groups=mesh['sec'=2,'clu_0'=4,'clu_1'=2,'blk_0'=2,'blk_1'=8] {'blk_0','blk_1'}, dimensions={0} | all-to-all | bytes 655360 | tf_op jit(solution)/shard_map/all_to_all | solution.py:33
  242.8 3.5 %collective-permute-start.18 = (f32[16,40,128]{2,1,0:T(8,128)S(1)}, f32[16,40,128]{2,1,0:T(8,128)S(1)}, u32[]{:S(2)}, u32[]{:S(2)}) collective-permute-start(f32[16,40,128]{2,1,0:T(8,128)S(1)} %all_to_all.69.mine_ref.refs_9_), channel_id=1, source_target_pairs={{0,128},{128,0},{1,129},{129,1},{2,130},{130,2},{3,131},{131,3},{4... | collective-permute-start | bytes 983048 | tf_op jit(solution)/shard_map/ppermute | solution.py:29
  246.4 1.3 collective-permute-done.18.other_ref.refs_10_
  248.3 1.8 range_sums.3
  250.2 12.6 %all_to_all.70.refs_11_.refs_0_ = f32[8,32,128]{2,1,0:T(8,128)} all-to-all(f32[8,32,128]{2,1,0:T(8,128)} %range_sums.3), channel_id=1, replica_groups=mesh['sec'=2,'clu_0'=4,'clu_1'=2,'blk_0'=2,'blk_1'=8] {'clu_0','clu_1'}, dimensions={0} | all-to-all | bytes 262144 | tf_op jit(solution)/shard_map/all_to_all | solution.py:33
  262.8 10.3 %forward_last.1 = (f32[8,64,128]{2,1,0:T(8,128)}, f32[8,64,128]{2,1,0:T(8,128)}) custom-call(s32[48]{0:T(128)} %bitcast.127, s32[48]{0:T(128)} %bitcast.132, s32[1]{0:T(128)} %bitcast.105.refs_2_, s32[1]{0:T(128)} %bitcast.3.refs_3_.half_ref, s32[32,128]{1,0:T(8,128)} %get-tuple-element.80.refs_4_, s32[32,128]{1,0:T(8,128)} %bitcast.113, ...), custom_call_target="tpu_custom_call" | custom-call | tf_op jit(solution)/shard_map/forward_last/pallas_call | solution.py:524
  273.1 5.9 %update.3 = (f32[32,8,8,128]{3,2,1,0:T(8,128)}, f32[32,8,8,128]{3,2,1,0:T(8,128)}, f32[32,8,8,128]{3,2,1,0:T(8,128)}) custom-call(f32[8,32,128]{2,1,0:T(8,128)} %all_to_all.70.refs_11_.refs_0_, f32[32,128]{1,0:T(8,128)} %get-tuple-element.57.refs_1_, s32[8,8,128]{2,1,0:T(8,128)} %fusion.7.refs_2_, f32[32,8,8,128]{3,2,1,0:T(8,128)} %get-tuple-element.58.refs_3_, ...), custom_call_target="tpu_custom_call" | custom-call | tf_op jit(solution)/shard_map/update/pallas_call | solution.py:537
  279.0 1.5 copy.47
  280.8 2.9 collective-permute-start.20
  283.8 1.3 collective-permute-start.21
  285.8 6.8 %all-to-all-start.11 = ((f32[8,64,128]{2,1,0:T(8,128)}), f32[8,64,128]{2,1,0:T(8,128)S(1)}, u32[]{:S(2)}, u32[]{:S(2)}) async-start(f32[8,64,128]{2,1,0:T(8,128)} %add.88), calls=%async_computation.11 | async-start | bytes 524288 | tf_op jit(solution)/shard_map/all_to_all | solution.py:33
  292.6 4.2 %collective-permute-start.22 = (bf16[32,8,128]{2,1,0:T(8,128)(2,1)S(1)}, bf16[32,8,128]{2,1,0:T(8,128)(2,1)S(1)}, u32[]{:S(2)}, u32[]{:S(2)}) collective-permute-start(bf16[32,8,128]{2,1,0:T(8,128)(2,1)S(1)} %get-tuple-element.64), channel_id=1, source_target_pairs={{0,1},{1,2},{2,3},{3,4},{4,5},{5,6},{6,7},{7,8},{8,9},{9,10},{10,1... | collective-permute-start | bytes 196616 | tf_op jit(solution)/shard_map/ppermute | solution.py:25
  296.9 3.7 %collective-permute-start.23 = (bf16[32,8,128]{2,1,0:T(8,128)(2,1)S(1)}, bf16[32,8,128]{2,1,0:T(8,128)(2,1)S(1)}, u32[]{:S(2)}, u32[]{:S(2)}) collective-permute-start(bf16[32,8,128]{2,1,0:T(8,128)(2,1)S(1)} %get-tuple-element.63), channel_id=1, source_target_pairs={{1,0},{2,1},{3,2},{4,3},{5,4},{6,5},{7,6},{8,7},{9,8},{10,9},{11,1... | collective-permute-start | bytes 196616 | tf_op jit(solution)/shard_map/ppermute | solution.py:25
  301.2 1.8 collective-permute-done.23.right_ref
  303.6 3.6 %stiffness_last.1.dots_ref = f32[32,128]{1,0:T(8,128)} custom-call(f32[32,8,8,128]{3,2,1,0:T(8,128)} %get-tuple-element.60.direction_ref, f32[32,8,8,128]{3,2,1,0:T(8,128)} %get-tuple-element.61.residual_ref, bf16[32,8,128]{2,1,0:T(8,128)(2,1)} %copy-done.22, bf16[32,8,128]{2,1,0:T(8,128)(2,1)} %copy-done.23, bf16[32,8,128]{2,1,0:T(8,128)(2,1)} %copy-done.26, ...), custom_call_target="tpu_custom_call" | custom-call | tf_op jit(solution)/shard_map/stiffness_last/pallas_call | solution.py:556
  307.9 1.8 last_sums.1
  309.8 24.8 %all_to_all.71.sums_ref = f32[256,1,128]{2,1,0:T(1,128)} all-to-all(f32[256,1,128]{2,1,0:T(1,128)} %last_sums.1), channel_id=1, replica_groups=mesh['sec'=2,'clu_0'=4,'clu_1'=2,'blk_0'=2,'blk_1'=8] {'sec','clu_0','cl..., dimensions={0} | all-to-all | bytes 262144 | tf_op jit(solution)/shard_map/all_to_all | solution.py:33
  334.6 3.1 final.1
  (152 shorter events, 16.9 us)
Async XLA Ops:
  0.0 14.3 %copy-start = (f32[32,8,8,128]{3,2,1,0:T(8,128)S(1)}, f32[32,8,8,128]{3,2,1,0:T(8,128)}, u32[]{:S(2)}) copy-start(f32[32,8,8,128]{3,2,1,0:T(8,128)} %refs_5_.1) | copy-start | bytes 3145732
  4.2 24.2 %copy-start.35 = (s32[4096]{0:T(1024)S(1)}, s32[4096]{0:T(1024)}, u32[]{:S(2)}) copy-start(s32[4096]{0:T(1024)} %param.25) | copy-start | bytes 49156
  4.2 29.1 %all-to-all-start = ((f32[16,32,128]{2,1,0:T(8,128)}), f32[16,32,128]{2,1,0:T(8,128)S(1)}, u32[]{:S(2)}, u32[]{:S(2)}) async-start(f32[16,32,128]{2,1,0:T(8,128)} %first_trace.1), calls=%async_computation | async-start | bytes 524288 | tf_op jit(solution)/shard_map/all_to_all | solution.py:33
  14.8 85.9 %collective-permute-start.4 = (bf16[32,8,128]{2,1,0:T(8,128)(2,1)S(1)}, bf16[32,8,128]{2,1,0:T(8,128)(2,1)S(1)}, u32[]{:S(2)}, u32[]{:S(2)}) collective-permute-start(bf16[32,8,128]{2,1,0:T(8,128)(2,1)S(1)} %bitcast.114), channel_id=1, source_target_pairs={{0,16},{16,32},{32,48},{48,64},{64,80},{80,96},{96,112},{112,128},... | collective-permute-start | bytes 196616 | tf_op jit(solution)/shard_map/ppermute | solution.py:25
  19.1 81.6 %collective-permute-start.5 = (bf16[32,8,128]{2,1,0:T(8,128)(2,1)S(1)}, bf16[32,8,128]{2,1,0:T(8,128)(2,1)S(1)}, u32[]{:S(2)}, u32[]{:S(2)}) collective-permute-start(bf16[32,8,128]{2,1,0:T(8,128)(2,1)S(1)} %bitcast.115), channel_id=1, source_target_pairs={{16,0},{32,16},{48,32},{64,48},{80,64},{96,80},{112,96},{128,112},... | collective-permute-start | bytes 196616 | tf_op jit(solution)/shard_map/ppermute | solution.py:25
  20.4 80.3 %collective-permute-start.6 = (bf16[32,8,128]{2,1,0:T(8,128)(2,1)S(1)}, bf16[32,8,128]{2,1,0:T(8,128)(2,1)S(1)}, u32[]{:S(2)}, u32[]{:S(2)}) collective-permute-start(bf16[32,8,128]{2,1,0:T(8,128)(2,1)S(1)} %get-tuple-element.72), channel_id=1, source_target_pairs={{0,1},{1,2},{2,3},{3,4},{4,5},{5,6},{6,7},{7,8},{8,9},{9,10},{10,1... | collective-permute-start | bytes 196616 | tf_op jit(solution)/shard_map/ppermute | solution.py:25
  23.8 77.0 %collective-permute-start.7 = (bf16[32,8,128]{2,1,0:T(8,128)(2,1)S(1)}, bf16[32,8,128]{2,1,0:T(8,128)(2,1)S(1)}, u32[]{:S(2)}, u32[]{:S(2)}) collective-permute-start(bf16[32,8,128]{2,1,0:T(8,128)(2,1)S(1)} %get-tuple-element.71), channel_id=1, source_target_pairs={{1,0},{2,1},{3,2},{4,3},{5,4},{6,5},{7,6},{8,7},{9,8},{10,9},{11,1... | collective-permute-start | bytes 196616 | tf_op jit(solution)/shard_map/ppermute | solution.py:25
  29.0 3.4 %copy-start.10 = (s32[4096]{0:T(1024)}, s32[4096]{0:T(1024)S(1)}, u32[]{:S(2)}) copy-start(s32[4096]{0:T(1024)S(1)} %get-tuple-element.81) | copy-start | bytes 49156
  31.9 1.2 copy-start.33
  32.0 1.1 copy-start.16
  32.0 1.2 copy-start.36
  32.0 1.3 copy-start.17
  32.0 3.8 %copy-start.30 = (f32[8,8]{1,0:T(8,128)S(1)}, f32[8,8]{1,0:T(8,128)}, u32[]{:S(2)}) copy-start(f32[8,8]{1,0:T(8,128)} %param.16) | copy-start | bytes 772
  32.5 12.9 %copy-start.34 = (f32[8,8]{1,0:T(8,128)S(1)}, f32[8,8]{1,0:T(8,128)}, u32[]{:S(2)}) copy-start(f32[8,8]{1,0:T(8,128)} %param.15) | copy-start | bytes 772
  33.3 3.7 %copy-start.6 = (f32[16,32,128]{2,1,0:T(8,128)}, f32[16,32,128]{2,1,0:T(8,128)S(1)}, u32[]{:S(2)}) copy-start(f32[16,32,128]{2,1,0:T(8,128)S(1)} %all-to-all-done.refs_7_) | copy-start | bytes 786436
  33.3 3.6 %collective-permute-start = (f32[16,32,128]{2,1,0:T(8,128)S(1)}, f32[16,32,128]{2,1,0:T(8,128)S(1)}, u32[]{:S(2)}, u32[]{:S(2)}) collective-permute-start(f32[16,32,128]{2,1,0:T(8,128)S(1)} %all-to-all-done.refs_7_), channel_id=1, source_target_pairs={{0,128},{128,0},{1,129},{129,1},{2,130},{130,2},{3,131},{131,3},{4... | collective-permute-start | bytes 786440 | tf_op jit(solution)/shard_map/ppermute | solution.py:29
  36.6 26.0 %copy-start.3 = (bf16[5,128,128]{2,1,0:T(8,128)(2,1)}, bf16[5,128,128]{2,1,0:T(8,128)(2,1)S(1)}, u32[]{:S(2)}) copy-start(bf16[5,128,128]{2,1,0:T(8,128)(2,1)S(1)} %bitcast_dynamic-update-slice_fusion.matrices_ref) | copy-start | bytes 491524
  37.0 0.7 copy-start.13
  45.0 1.6 collective-permute-start.1
  48.2 13.8 %all-to-all-start.1 = ((f32[8,32,128]{2,1,0:T(8,128)}), f32[8,32,128]{2,1,0:T(8,128)S(1)}, u32[]{:S(2)}, u32[]{:S(2)}) async-start(f32[8,32,128]{2,1,0:T(8,128)} %add.82), calls=%async_computation.1 | async-start | bytes 262144 | tf_op jit(solution)/shard_map/all_to_all | solution.py:33
  62.6 11.0 %all-to-all-start.2 = ((bf16[8,32,128]{2,1,0:T(8,128)(2,1)}), bf16[8,32,128]{2,1,0:T(8,128)(2,1)S(1)}, u32[]{:S(2)}, u32[]{:S(2)}) async-start(bf16[8,32,128]{2,1,0:T(8,128)(2,1)} %broadcast_in_dim.89), calls=%async_computation.2 | async-start | bytes 131072 | tf_op jit(solution)/shard_map/all_to_all | solution.py:33
  73.7 4.0 %copy-start.14 = (bf16[8,32,128]{2,1,0:T(8,128)(2,1)}, bf16[8,32,128]{2,1,0:T(8,128)(2,1)S(1)}, u32[]{:S(2)}) copy-start(bf16[8,32,128]{2,1,0:T(8,128)(2,1)S(1)} %all-to-all-done.2.mine_ref) | copy-start | bytes 196612
  73.7 1.3 collective-permute-start.2
  74.9 2.7 copy-start.31
  74.9 12.5 %collective-permute-start.8 = (f32[1,8]{1,0:T(1,128)S(1)}, f32[1,8]{1,0:T(1,128)S(1)}, u32[]{:S(2)}, u32[]{:S(2)}) collective-permute-start(f32[1,8]{1,0:T(1,128)S(1)} %slice.72), channel_id=1, source_target_pairs={{0,16},{16,32},{32,48},{48,64},{64,80},{80,96},{96,112},{112,128},... | collective-permute-start | bytes 104 | tf_op jit(solution)/shard_map/ppermute | solution.py:25
  87.4 1.7 collective-permute-start.3
  89.1 11.4 %collective-permute-start.9 = (f32[8,1]{1,0:T(8,128)S(1)}, f32[8,1]{1,0:T(8,128)S(1)}, u32[]{:S(2)}, u32[]{:S(2)}) collective-permute-start(f32[8,1]{1,0:T(8,128)S(1)} %slice.74), channel_id=1, source_target_pairs={{0,1},{1,2},{2,3},{3,4},{4,5},{5,6},{6,7},{7,8},{8,9},{9,10},{10,1... | collective-permute-start | bytes 104 | tf_op jit(solution)/shard_map/ppermute | solution.py:25
  92.8 17.1 %all-to-all-start.3 = ((f32[16,32,128]{2,1,0:T(8,128)}), f32[16,32,128]{2,1,0:T(8,128)S(1)}, u32[]{:S(2)}, u32[]{:S(2)}) async-start(f32[16,32,128]{2,1,0:T(8,128)} %add.83), calls=%async_computation.3 | async-start | bytes 524288 | tf_op jit(solution)/shard_map/all_to_all | solution.py:33
  100.7 0.9 copy-start.18
  100.7 0.9 copy-start.19
  100.7 0.9 copy-start.20
  100.8 0.9 copy-start.21
  128.4 1.6 copy-start.2
  128.4 1.6 collective-permute-start.10
  130.0 0.7 copy-start.5
  154.7 35.4 %copy-start.37 = (s32[1,1,128]{2,1,0:T(1,128)S(1)}, s32[1,1,128]{2,1,0:T(1,128)}, u32[]{:S(2)}) copy-start(s32[1,1,128]{2,1,0:T(1,128)} %param.24) | copy-start | bytes 1540
  154.7 1.6 collective-permute-start.11
  178.3 1.3 copy-start.15
  178.3 1.3 collective-permute-start.12
  189.9 8.0 %collective-permute-start.13 = (f32[16,32,128]{2,1,0:T(8,128)}, f32[16,32,128]{2,1,0:T(8,128)S(1)}, u32[]{:S(2)}, u32[]{:S(2)}) collective-permute-start(f32[16,32,128]{2,1,0:T(8,128)} %get-tuple-element.47), channel_id=1, source_target_pairs={{0,128},{128,0},{1,129},{129,1},{2,130},{130,2},{3,131},{131,3},{4... | collective-permute-start | bytes 786440 | tf_op jit(solution)/shard_map/ppermute | solution.py:29
  196.4 1.5 copy-start.12
  198.7 24.8 %all-to-all-start.8 = ((f32[16,32,128]{2,1,0:T(8,128)}), f32[16,32,128]{2,1,0:T(8,128)S(1)}, u32[]{:S(2)}, u32[]{:S(2)}) async-start(f32[16,32,128]{2,1,0:T(8,128)} %add.85), calls=%async_computation.8 | async-start | bytes 524288 | tf_op jit(solution)/shard_map/all_to_all | solution.py:33
  204.8 11.7 %collective-permute-start.14 = (bf16[32,8,128]{2,1,0:T(8,128)(2,1)S(1)}, bf16[32,8,128]{2,1,0:T(8,128)(2,1)S(1)}, u32[]{:S(2)}, u32[]{:S(2)}) collective-permute-start(bf16[32,8,128]{2,1,0:T(8,128)(2,1)S(1)} %bitcast.118), channel_id=1, source_target_pairs={{0,16},{16,32},{32,48},{48,64},{64,80},{80,96},{96,112},{112,128},... | collective-permute-start | bytes 196616 | tf_op jit(solution)/shard_map/ppermute | solution.py:25
  207.3 9.3 %collective-permute-start.15 = (bf16[32,8,128]{2,1,0:T(8,128)(2,1)S(1)}, bf16[32,8,128]{2,1,0:T(8,128)(2,1)S(1)}, u32[]{:S(2)}, u32[]{:S(2)}) collective-permute-start(bf16[32,8,128]{2,1,0:T(8,128)(2,1)S(1)} %bitcast.119), channel_id=1, source_target_pairs={{16,0},{32,16},{48,32},{64,48},{80,64},{96,80},{112,96},{128,112},... | collective-permute-start | bytes 196616 | tf_op jit(solution)/shard_map/ppermute | solution.py:25
  208.6 8.3 %collective-permute-start.16 = (bf16[32,8,128]{2,1,0:T(8,128)(2,1)S(1)}, bf16[32,8,128]{2,1,0:T(8,128)(2,1)S(1)}, u32[]{:S(2)}, u32[]{:S(2)}) collective-permute-start(bf16[32,8,128]{2,1,0:T(8,128)(2,1)S(1)} %get-tuple-element.68), channel_id=1, source_target_pairs={{0,1},{1,2},{2,3},{3,4},{4,5},{5,6},{6,7},{7,8},{8,9},{9,10},{10,1... | collective-permute-start | bytes 196616 | tf_op jit(solution)/shard_map/ppermute | solution.py:25
  212.0 6.5 %collective-permute-start.17 = (bf16[32,8,128]{2,1,0:T(8,128)(2,1)S(1)}, bf16[32,8,128]{2,1,0:T(8,128)(2,1)S(1)}, u32[]{:S(2)}, u32[]{:S(2)}) collective-permute-start(bf16[32,8,128]{2,1,0:T(8,128)(2,1)S(1)} %get-tuple-element.67), channel_id=1, source_target_pairs={{1,0},{2,1},{3,2},{4,3},{5,4},{6,5},{7,6},{8,7},{9,8},{10,9},{11,1... | collective-permute-start | bytes 196616 | tf_op jit(solution)/shard_map/ppermute | solution.py:25
  216.6 1.9 copy-start.24
  216.6 1.9 copy-start.25
  216.9 1.6 copy-start.27
  223.5 0.7 copy-start.7
  242.8 4.8 %copy-start.1 = (f32[16,40,128]{2,1,0:T(8,128)}, f32[16,40,128]{2,1,0:T(8,128)S(1)}, u32[]{:S(2)}) copy-start(f32[16,40,128]{2,1,0:T(8,128)S(1)} %all_to_all.69.mine_ref.refs_9_) | copy-start | bytes 983044
  242.8 4.8 %collective-permute-start.18 = (f32[16,40,128]{2,1,0:T(8,128)S(1)}, f32[16,40,128]{2,1,0:T(8,128)S(1)}, u32[]{:S(2)}, u32[]{:S(2)}) collective-permute-start(f32[16,40,128]{2,1,0:T(8,128)S(1)} %all_to_all.69.mine_ref.refs_9_), channel_id=1, source_target_pairs={{0,128},{128,0},{1,129},{129,1},{2,130},{130,2},{3,131},{131,3},{4... | collective-permute-start | bytes 983048 | tf_op jit(solution)/shard_map/ppermute | solution.py:29
  247.6 0.7 copy-start.4
  273.1 12.0 %collective-permute-start.19 = (f32[8,64,128]{2,1,0:T(8,128)}, f32[8,64,128]{2,1,0:T(8,128)S(1)}, u32[]{:S(2)}, u32[]{:S(2)}) collective-permute-start(f32[8,64,128]{2,1,0:T(8,128)} %get-tuple-element.56), channel_id=1, source_target_pairs={{0,128},{128,0},{1,129},{129,1},{2,130},{130,2},{3,131},{131,3},{4... | collective-permute-start | bytes 786440 | tf_op jit(solution)/shard_map/ppermute | solution.py:29
  279.0 6.2 %copy-start.11 = (f32[8,64,128]{2,1,0:T(8,128)S(1)}, f32[8,64,128]{2,1,0:T(8,128)}, u32[]{:S(2)}) copy-start(f32[8,64,128]{2,1,0:T(8,128)} %get-tuple-element.55) | copy-start | bytes 786436
  280.8 19.8 %collective-permute-start.20 = (bf16[32,8,128]{2,1,0:T(8,128)(2,1)S(1)}, bf16[32,8,128]{2,1,0:T(8,128)(2,1)S(1)}, u32[]{:S(2)}, u32[]{:S(2)}) collective-permute-start(bf16[32,8,128]{2,1,0:T(8,128)(2,1)S(1)} %bitcast.116), channel_id=1, source_target_pairs={{0,16},{16,32},{32,48},{48,64},{64,80},{80,96},{96,112},{112,128},... | collective-permute-start | bytes 196616 | tf_op jit(solution)/shard_map/ppermute | solution.py:25
  283.8 16.8 %collective-permute-start.21 = (bf16[32,8,128]{2,1,0:T(8,128)(2,1)S(1)}, bf16[32,8,128]{2,1,0:T(8,128)(2,1)S(1)}, u32[]{:S(2)}, u32[]{:S(2)}) collective-permute-start(bf16[32,8,128]{2,1,0:T(8,128)(2,1)S(1)} %bitcast.117), channel_id=1, source_target_pairs={{16,0},{32,16},{48,32},{64,48},{80,64},{96,80},{112,96},{128,112},... | collective-permute-start | bytes 196616 | tf_op jit(solution)/shard_map/ppermute | solution.py:25
  285.8 21.4 %all-to-all-start.11 = ((f32[8,64,128]{2,1,0:T(8,128)}), f32[8,64,128]{2,1,0:T(8,128)S(1)}, u32[]{:S(2)}, u32[]{:S(2)}) async-start(f32[8,64,128]{2,1,0:T(8,128)} %add.88), calls=%async_computation.11 | async-start | bytes 524288 | tf_op jit(solution)/shard_map/all_to_all | solution.py:33
  292.6 8.6 %collective-permute-start.22 = (bf16[32,8,128]{2,1,0:T(8,128)(2,1)S(1)}, bf16[32,8,128]{2,1,0:T(8,128)(2,1)S(1)}, u32[]{:S(2)}, u32[]{:S(2)}) collective-permute-start(bf16[32,8,128]{2,1,0:T(8,128)(2,1)S(1)} %get-tuple-element.64), channel_id=1, source_target_pairs={{0,1},{1,2},{2,3},{3,4},{4,5},{5,6},{6,7},{7,8},{8,9},{9,10},{10,1... | collective-permute-start | bytes 196616 | tf_op jit(solution)/shard_map/ppermute | solution.py:25
  296.9 6.2 %collective-permute-start.23 = (bf16[32,8,128]{2,1,0:T(8,128)(2,1)S(1)}, bf16[32,8,128]{2,1,0:T(8,128)(2,1)S(1)}, u32[]{:S(2)}, u32[]{:S(2)}) collective-permute-start(bf16[32,8,128]{2,1,0:T(8,128)(2,1)S(1)} %get-tuple-element.63), channel_id=1, source_target_pairs={{1,0},{2,1},{3,2},{4,3},{5,4},{6,5},{7,6},{8,7},{9,8},{10,9},{11,1... | collective-permute-start | bytes 196616 | tf_op jit(solution)/shard_map/ppermute | solution.py:25
  300.6 2.4 copy-start.22
  300.6 2.4 copy-start.23
  301.2 1.8 copy-start.26
  307.2 0.7 copy-start.9
  (4 other events, 2.5 us)

commit v2 on v1

--- a/solution.py
+++ b/solution.py
@@ -17,6 +17,7 @@
 BF16 = jnp.bfloat16
 SMEM = pl.BlockSpec(memory_space=pltpu.SMEM)
 VMEM = pl.BlockSpec(memory_space=pltpu.VMEM)
+LIMIT = 24 * 1024 * 1024
 
 
 def passed_along(value, axis, by):
@@ -33,12 +34,39 @@
     return lax.all_to_all(pieces, axes, split_axis=0, concat_axis=0, tiled=True)
 
 
+class near:
+    def __init__(self, value):
+        self.value = value
+
+
+def kernel(body, outs, inputs, scratch=(), scalars=0):
+    inputs = [
+        pltpu.with_memory_space_constraint(x.value, pltpu.VMEM)
+        if isinstance(x, near)
+        else x
+        if i < scalars
+        else pltpu.with_memory_space_constraint(x, pltpu.HBM)
+        for i, x in enumerate(inputs)
+    ]
+    return pl.pallas_call(
+        body,
+        out_shape=outs,
+        in_specs=[SMEM] * scalars + [pl.BlockSpec()] * (len(inputs) - scalars),
+        scratch_shapes=list(scratch),
+        compiler_params=pltpu.CompilerParams(vmem_limit_bytes=LIMIT),
+    )(*inputs)
+
+
 def lanes_taken(rows, index):
     return jnp.take_along_axis(rows, index, axis=1)
 
 
 def like(shape, dtype=F32):
-    return jax.ShapeDtypeStruct(shape, dtype)
+    return pltpu.HBM(shape, dtype)
+
+
+def kept(shape, dtype=F32):
+    return pltpu.VMEM(shape, dtype)
 
 
 def lane_iota(shape):
@@ -72,7 +100,22 @@
     return jnp.sum(total, axis=0, keepdims=True)
 
 
-def first_trace_kernel(field_ref, surface_ref, out_ref):
+def edges_stored(case, a, value, slabs, edge_refs):
+    before_ref, after_ref, left_ref, right_ref = edge_refs
+    if a == slabs - 1:
+        before_ref[case] = value
+    if a == 0:
+        after_ref[case] = value
+    left_ref[case, a : a + 1, :] = value[-1:, :]
+    right_ref[case, a : a + 1, :] = value[:1, :]
+
+
+def edge_outputs(cases, slabs, width, lanes, make):
+    return (make((cases, width, lanes)),) * 2 + (make((cases, slabs, lanes)),) * 2
+
+
+def first_trace_kernel(field_ref, surface_ref, out_ref, *edge_refs):
+    slabs = field_ref.shape[1]
     copies = out_ref.shape[0]
     lane_index = jnp.broadcast_to(surface_ref[0:1, :], (8, 128))
     block_index = jnp.broadcast_to(surface_ref[1:2, :], (8, 128))
@@ -80,6 +123,8 @@
     def step(case, carry):
         row = trace_of(field_ref, case, lane_index, block_index)
         out_ref[0, pl.ds(case, 1), :] = row
+        for a in range(slabs):
+            edges_stored(case, a, field_ref[case, a], slabs, edge_refs)
         return carry
 
     lax.fori_loop(0, field_ref.shape[0], step, 0, unroll=4)
@@ -117,12 +162,11 @@
 
 def forward_kernel(first, last, *refs):
     refs = list(refs)
-    rows_ref, columns_ref, live_ref, half_ref = refs[:4]
-    lanes_ref, blocks_ref, boundary_ref = refs[4:7]
-    refs = refs[7:]
+    pairs_ref, lanes_ref, blocks_ref, boundary_ref = refs[:4]
+    refs = refs[4:]
     if first:
-        mine_ref, other_ref, direction_ref, keep_ref, send_ref, low_ref = refs[:6]
-        rest = refs[6:]
+        mine_ref, other_ref, direction_ref, slots_ref, keep_ref, send_ref, low_ref = refs[:7]
+        rest = refs[7:]
         count = mine_ref.shape[0]
         direction_ref[:count] = mine_ref[...]
         direction_ref[count:] = other_ref[...]
@@ -132,8 +176,8 @@
             keep_ref, send_ref, direction_ref, low_ref = refs[5:9]
             rest = refs[9:]
         else:
-            residual_ref, direction_ref, keep_ref, send_ref, low_ref = refs[5:10]
-            rest = refs[10:]
+            residual_ref, direction_ref, slots_ref, keep_ref, send_ref, low_ref = refs[5:11]
+            rest = refs[11:]
         cases = old_direction_ref.shape[1]
         count = mine_ref.shape[0]
         alpha, beta = alpha_beta(scalars_of(sums_ref))
@@ -147,7 +191,10 @@
                     residual_ref[b] = residual
                 direction_ref[b] = residual + beta * old_direction_ref[b]
     cases = direction_ref.shape[1]
-    groups = cases // 8
+    if not last:
+        place = pairs_ref[3, 0]
+        slots_ref[0] = direction_ref[place] if first else residual_ref[place]
+        slots_ref[1] = direction_ref[place]
 
     def step(d, carry):
         totals = permuted_block(direction_ref, lanes_ref, blocks_ref, d)
@@ -161,28 +208,21 @@
             low_ref[d] = low
         return carry
 
-    lax.fori_loop(0, direction_ref.shape[0], step, 0)
+    lax.fori_loop(0, direction_ref.shape[0], step, 0, unroll=2)
     half_count = keep_ref.shape[0]
-    keep_ref[...] = jnp.zeros(keep_ref.shape, F32)
-    send_ref[...] = jnp.zeros(send_ref.shape, F32)
     sums_scratch = rest[0]
     sums_scratch[...] = jnp.zeros(sums_scratch.shape, F32)
-    live = live_ref[0]
-    flip = half_ref[0] * half_count
+    live = pairs_ref[2, 0]
     for p in range(boundary_ref.shape[0]):
-        product = jnp.dot(low_ref[rows_ref[p]], boundary_ref[p], preferred_element_type=F32)
+        product = jnp.dot(low_ref[pairs_ref[0, p]], boundary_ref[p], preferred_element_type=F32)
         product = jnp.where(p < live, product, 0.0)
-        where = columns_ref[p] ^ flip
-        sums_scratch[where] += product
+        sums_scratch[pairs_ref[1, p]] += product
     keep_ref[...] = sums_scratch[:half_count]
     send_ref[...] = sums_scratch[half_count:]
 
 
 def backward_kernel(
-    rows_ref,
-    columns_ref,
-    live_ref,
-    half_ref,
+    pairs_ref,
     lanes_ref,
     blocks_ref,
     boundary_ref,
@@ -197,17 +237,16 @@
     low_ref[:half_count] = mine_ref[...]
     low_ref[half_count:] = other_ref[...]
     rows_scratch[...] = jnp.zeros(rows_scratch.shape, F32)
-    live = live_ref[0]
-    flip = half_ref[0] * half_count
+    live = pairs_ref[2, 0]
     for p in range(boundary_ref.shape[0]):
         product = lax.dot_general(
-            low_ref[columns_ref[p] ^ flip],
+            low_ref[pairs_ref[1, p]],
             boundary_ref[p],
             (((1,), (1,)), ((), ())),
             preferred_element_type=F32,
         )
         product = jnp.where(p < live, product, 0.0)
-        rows_scratch[rows_ref[p]] += product
+        rows_scratch[pairs_ref[0, p]] += product
     count = keep_ref.shape[0]
     for at, out_ref in ((0, keep_ref), (count, send_ref)):
 
@@ -217,48 +256,45 @@
                 out_ref[d, 8 * g : 8 * g + 8, :] = total
             return carry
 
-        lax.fori_loop(0, count, step, 0)
-
-
-def stiffness_kernel(
-    want_trace,
-    direction_ref,
-    residual_ref,
-    before_ref,
-    after_ref,
-    left_ref,
-    right_ref,
-    weights_ref,
-    matrices_ref,
-    surface_ref,
-    *out_refs,
-):
-    if want_trace:
-        image_ref, trace_ref, dots_ref, low_ref, high_ref, sums_ref = out_refs
-    else:
-        dots_ref, image_ref, low_ref, high_ref, sums_ref = out_refs
+        lax.fori_loop(0, count, step, 0, unroll=2)
+
+
+def low_kernel(pieces_ref, out_ref):
+    low = jnp.sum(pieces_ref[...], axis=0).astype(BF16)
+    for i in range(out_ref.shape[0]):
+        out_ref[i] = low
+
+
+def stiffness(direction_ref, residual_ref, halo_refs, given_refs, out_refs, scratch_refs):
+    before_ref, after_ref, left_ref, right_ref = halo_refs
+    weights_ref, matrices_ref, surface_ref = given_refs
+    image_ref, dots_ref, *more_refs = out_refs
+    low_ref, high_ref, sums_ref = scratch_refs
+    want_trace = len(more_refs) > 0
     cases, slabs, width = direction_ref.shape[:3]
     rows = cases * width
 
     def product(value, which):
         return jnp.dot(
-            value.reshape(rows, 128), matrices_ref[which], preferred_element_type=F32
+            value.reshape(rows, 128).astype(BF16),
+            matrices_ref[which],
+            preferred_element_type=F32,
         ).reshape(cases, width, 128)
 
-    def low(a):
+    def taken(a):
         if a < 0:
             return before_ref[...]
         if a == slabs:
             return after_ref[...]
-        return direction_ref[:, a].astype(BF16)
+        return direction_ref[:, a]
 
     high_ref[...] = product(right_ref[...], 3)
     low_ref[...] = product(left_ref[...], 4)
     for a in range(slabs):
-        own = low(a)
+        own = taken(a)
         result = weights_ref[0, a][None] * product(own, 0)
-        result = result - weights_ref[1, a][None] * product(low(a + 1), 1)
-        result = result - weights_ref[2, a][None] * product(low(a - 1), 2)
+        result = result - weights_ref[1, a][None] * product(taken(a + 1), 1)
+        result = result - weights_ref[2, a][None] * product(taken(a - 1), 2)
         result = result - weights_ref[3, a][None] * pltpu.roll(product(own, 3), width - 1, 1)
         result = result - weights_ref[4, a][None] * pltpu.roll(product(own, 4), 1, 1)
         result = result - weights_ref[5, a][None] * high_ref[:, a : a + 1, :]
@@ -277,7 +313,9 @@
                 jnp.sum(one * two, axis=0), axis=0, keepdims=True
             )
         if want_trace:
-            trace_ref[pl.ds(case, 1), :] = trace_of(image_ref, case, lane_index, block_index)
+            more_refs[0][pl.ds(case, 1), :] = trace_of(image_ref, case, lane_index, block_index)
+            for a in range(slabs):
+                edges_stored(case, a, image_ref[case, a], slabs, more_refs[1:])
         return carry
 
     lax.fori_loop(0, cases, step, 0, unroll=4)
@@ -288,55 +326,34 @@
     dots_ref[...] = dots
 
 
-def own_kernel(
-    place_ref, arrived_ref, trace_ref, dots_ref, residual_ref, direction_ref, out_ref, own_ref
-):
-    copies, cases = out_ref.shape[0], trace_ref.shape[0]
-    y = jnp.sum(arrived_ref[...], axis=0)
-    own_ref[...] = y
-    trace = trace_ref[...]
-    r = residual_ref[place_ref[0]]
-    d = direction_ref[place_ref[0]]
-    dots = dots_ref[...]
-    terms = (None, d * y, r * y, (2.0 * trace + y) * y)
-    row = jnp.zeros((1, 128), F32)
-    for i, term in enumerate(terms):
-        column = dots[:, i : i + 1]
-        if term is not None:
-            column = column + jnp.sum(term, axis=1, keepdims=True)
-        row = row + column_to_row(column, i * cases)
-    image = trace + y
-    row8 = jnp.broadcast_to(row, (8, 128))
-    for i in range(copies):
-        out_ref[i, :cases, :] = image
-        out_ref[i, cases:, :] = row8
-
-
-def range_sum_kernel(mine_ref, other_ref, out_ref):
-    copies, cases = out_ref.shape[0], out_ref.shape[1]
-    row = jnp.sum(mine_ref[:, cases : cases + 8, :], axis=0) + jnp.sum(
-        other_ref[:, cases : cases + 8, :], axis=0
-    )
-    row = row[0:1, :]
-    lane = lane_iota((cases, 128))
-    sums = jnp.zeros((cases, 128), F32)
-    for i in range(4):
-        sums = jnp.where(lane == i, row_to_column(row, i * cases, cases), sums)
-    for i in range(copies):
-        out_ref[i] = sums
-
-
-def update_kernel(first, *refs):
-    if first:
-        sums_ref, own_ref, inverse_ref, image_ref, residual_ref, direction_ref = refs[:6]
-        solution_ref = None
-        refs = refs[6:]
+def first_stiffness_kernel(direction_ref, *refs):
+    stiffness(direction_ref, direction_ref, refs[:4], refs[4:7], refs[7:14], refs[14:])
+
+
+def field_kernel(first, last, *refs):
+    refs = list(refs)
+
+    def take(n):
+        taken = refs[:n]
+        del refs[:n]
+        return taken
+
+    sums_ref, own_ref, inverse_ref, image_ref, residual_ref, direction_ref = take(6)
+    solution_ref = None if first else take(1)[0]
+    halo_image_refs, halo_residual_refs, halo_direction_refs = take(4), take(4), take(4)
+    given_refs = take(3)
+    new_solution_ref, new_direction_ref = take(2)
+    if last:
+        (dots_ref,) = take(1)
+        new_residual_ref, new_image_ref = take(2)
+        new_halo_direction_refs = take(4)
+        new_halo_residual_refs = None
+        out_refs = (new_image_ref, dots_ref)
     else:
-        sums_ref, own_ref, inverse_ref, image_ref, residual_ref, direction_ref, solution_ref = refs[
-            :7
-        ]
-        refs = refs[7:]
-    new_solution_ref, new_residual_ref, new_direction_ref, alpha_ref, beta_ref = refs
+        (new_residual_ref,) = take(1)
+        new_halo_residual_refs, new_halo_direction_refs = take(4), take(4)
+        out_refs = take(7)
+    alpha_ref, beta_ref = take(2)
     cases, slabs, width = direction_ref.shape[:3]
     alpha, beta = alpha_beta(scalars_of(sums_ref))
     alpha_ref[...] = jnp.broadcast_to(alpha, (cases, 128))
@@ -346,6 +363,11 @@
         alpha = jnp.broadcast_to(alpha_ref[pl.ds(case, 1), :], (width, 128))
         beta = jnp.broadcast_to(beta_ref[pl.ds(case, 1), :], (width, 128))
         own = jnp.broadcast_to(own_ref[pl.ds(case, 1), :], (width, 128))
+        for i in range(4):
+            r = halo_residual_refs[i][case] - alpha * halo_image_refs[i][case]
+            if not last:
+                new_halo_residual_refs[i][case] = r
+            new_halo_direction_refs[i][case] = r + beta * halo_direction_refs[i][case]
         for a in range(slabs):
             slot = inverse_ref[a]
             there = slot > 0
@@ -361,7 +383,64 @@
             new_direction_ref[case, a] = r + beta * d
         return carry
 
-    lax.fori_loop(0, cases, step, 0, unroll=2)
+    lax.fori_loop(0, cases, step, 0, unroll=4)
+    stiffness(
+        new_direction_ref, new_residual_ref, new_halo_direction_refs, given_refs, out_refs, refs
+    )
+
+
+def own_kernel(arrived_ref, trace_ref, dots_ref, slots_ref, inverse_ref, *refs):
+    edge_refs, (out_ref, own_ref), new_edge_refs = refs[:4], refs[4:6], refs[6:]
+    copies, cases = out_ref.shape[0], trace_ref.shape[0]
+    slabs, width = inverse_ref.shape[:2]
+    y = jnp.sum(arrived_ref[...], axis=0)
+    own_ref[...] = y
+    trace = trace_ref[...]
+    r = slots_ref[0]
+    d = slots_ref[1]
+    dots = dots_ref[...]
+    terms = (None, d * y, r * y, (2.0 * trace + y) * y)
+    row = jnp.zeros((1, 128), F32)
+    for i, term in enumerate(terms):
+        column = dots[:, i : i + 1]
+        if term is not None:
+            column = column + jnp.sum(term, axis=1, keepdims=True)
+        row = row + column_to_row(column, i * cases)
+    image = trace + y
+    row8 = jnp.broadcast_to(row, (8, 128))
+    for i in range(copies):
+        out_ref[i, :cases, :] = image
+        out_ref[i, cases:, :] = row8
+    sides = (
+        inverse_ref[slabs - 1],
+        inverse_ref[0],
+        jnp.concatenate([inverse_ref[a, width - 1 :, :] for a in range(slabs)], axis=0),
+        jnp.concatenate([inverse_ref[a, :1, :] for a in range(slabs)], axis=0),
+    )
+
+    def step(case, carry):
+        values = jnp.broadcast_to(own_ref[pl.ds(case, 1), :], (8, 128))
+        for slot, edge_ref, new_edge_ref in zip(sides, edge_refs, new_edge_refs):
+            there = slot > 0
+            extra = lanes_taken(values, jnp.where(there, slot - 1, 0))
+            new_edge_ref[case] = edge_ref[case] + jnp.where(there, extra, 0.0)
+        return carry
+
+    lax.fori_loop(0, cases, step, 0, unroll=4)
+
+
+def range_sum_kernel(mine_ref, other_ref, out_ref):
+    copies, cases = out_ref.shape[0], out_ref.shape[1]
+    row = jnp.sum(mine_ref[:, cases : cases + 8, :], axis=0) + jnp.sum(
+        other_ref[:, cases : cases + 8, :], axis=0
+    )
+    row = row[0:1, :]
+    lane = lane_iota((cases, 128))
+    sums = jnp.zeros((cases, 128), F32)
+    for i in range(4):
+        sums = jnp.where(lane == i, row_to_column(row, i * cases, cases), sums)
+    for i in range(copies):
+        out_ref[i] = sums
 
 
 def last_sums_kernel(arrived_ref, dots_ref, out_ref):
@@ -417,8 +496,6 @@
     surface_local = surface_index[0, 0]
     half = lax.axis_index("sec").astype(jnp.int32)
     place = lax.axis_index(BLK).astype(jnp.int32)
-    half_local = half.reshape(1)
-    place_local = place.reshape(1)
     blk_count = lax.axis_size(BLK)
     clu_count = lax.axis_size(CLU)
     owners = 2 * blk_count
@@ -426,11 +503,21 @@
     slot_count = interface_slot.shape[0]
     surface = jnp.stack([surface_local % lanes, surface_local // lanes])
 
-    trace = pl.pallas_call(
+    def edges_by(make):
+        return edge_outputs(cases, slabs, width, lanes, make)
+
+    def sent(edges):
+        before = passed_along(edges[0], SEC_CLU, 1)
+        after = passed_along(edges[1], SEC_CLU, -1)
+        left = passed_along(edges[2], BLK, 1)
+        right = passed_along(edges[3], BLK, -1)
+        return before, after, left, right
+
+    trace, *edges = kernel(
         first_trace_kernel,
-        out_shape=like((blk_count, cases, lanes)),
-        name="first_trace",
-    )(right_side, surface)
+        (kept((blk_count, cases, lanes)), *edges_by(kept)),
+        (right_side, surface),
+    )
     mine = exchanged(trace, BLK)
     other = partner(mine)
 
@@ -487,9 +574,22 @@
 
     half_columns = clu_count
     slots_shape = (owners, cases, lanes)
-    forward_inputs = (rows_local, columns_local, live_local, half_local)
-    forward_inputs += (slot_lanes, slot_blocks, blocks_local)
-    forward_specs = [SMEM] * 4 + [VMEM] * 3
+    pairs = jnp.stack(
+        [
+            rows_local,
+            columns_local ^ (half * half_columns),
+            jnp.broadcast_to(live_local, rows_local.shape),
+            jnp.broadcast_to(place, rows_local.shape),
+        ]
+    )
+    forward_inputs = (pairs, slot_lanes, slot_blocks, near(blocks_local))
+    given = (weights, matrices, surface)
+    edge_kept, edge_like = edges_by(kept), edges_by(like)
+    own_slots_shape = like((2, cases, lanes))
+    image_outputs = (like(field), like((cases, lanes)), like((cases, lanes)), *edge_like)
+    stiffness_scratch = [pltpu.VMEM((cases, slabs, lanes), F32)] * 2
+    stiffness_scratch += [pltpu.VMEM((4, cases, lanes), F32)]
+    field_scratch = [pltpu.VMEM((cases, lanes), F32)] * 2 + stiffness_scratch
     solution = None
     residual = right_side
     direction = right_side
@@ -502,119 +602,119 @@
             pltpu.VMEM((slot_count // lanes, deep, lanes), BF16),
             pltpu.VMEM((2 * half_columns, deep, lanes), F32),
         ]
-        halves = (like((half_columns, deep, lanes)),) * 2
+        halves = (kept((half_columns, deep, lanes)),) * 2
         if first:
-            slot_direction, keep, send = pl.pallas_call(
+            slot_direction, own_slots, keep, send = kernel(
                 functools.partial(forward_kernel, True, False),
-                out_shape=(like(slots_shape), *halves),
-                in_specs=forward_specs + [VMEM] * 2,
-                scratch_shapes=scratch,
-                name="forward_first",
-            )(*forward_inputs, mine, other)
+                (like(slots_shape), own_slots_shape, *halves),
+                (*forward_inputs, near(mine), near(other)),
+                scratch,
+                1,
+            )
             slot_residual = slot_direction
-        elif not last:
-            slot_residual, slot_direction, keep, send = pl.pallas_call(
-                functools.partial(forward_kernel, False, False),
-                out_shape=(like(slots_shape), like(slots_shape), *halves),
-                in_specs=forward_specs + [VMEM] * 5,
-                scratch_shapes=scratch,
-                name="forward",
-            )(*forward_inputs, slot_residual, slot_direction, mine, other, sums)
         else:
-            keep, send = pl.pallas_call(
-                functools.partial(forward_kernel, False, True),
-                out_shape=halves,
-                in_specs=forward_specs + [VMEM] * 5,
-                scratch_shapes=[pltpu.VMEM(slots_shape, F32)] + scratch,
-                name="forward_last",
-            )(*forward_inputs, slot_residual, slot_direction, mine, other, sums)
-        column_pieces = exchanged(keep + partner(send), CLU)
-
-        if not first:
+            inputs = (*forward_inputs, slot_residual, slot_direction)
+            inputs += (near(mine), near(other), near(sums))
+            if last:
+                keep, send = kernel(
+                    functools.partial(forward_kernel, False, True),
+                    halves,
+                    inputs,
+                    [pltpu.VMEM(slots_shape, F32)] + scratch,
+                    1,
+                )
+            else:
+                slot_residual, slot_direction, own_slots, keep, send = kernel(
+                    functools.partial(forward_kernel, False, False),
+                    (like(slots_shape), like(slots_shape), own_slots_shape, *halves),
+                    inputs,
+                    scratch,
+                    1,
+                )
+        pieces = keep + partner(send)
+        column_pieces = exchanged(pieces, CLU)
+
+        if first:
+            halo_residual = halo_direction = sent(edges)
+            image, dots, image_trace, *edges = kernel(
+                first_stiffness_kernel,
+                image_outputs,
+                (right_side, *halo_direction, *given),
+                stiffness_scratch,
+            )
+        else:
             inputs = (sums, own, inverse, image, residual, direction)
             if iteration > 1:
                 inputs += (solution,)
-            solution, residual, direction = pl.pallas_call(
-                functools.partial(update_kernel, iteration == 1),
-                out_shape=(like(field),) * 3,
-                scratch_shapes=[pltpu.VMEM((cases, lanes), F32)] * 2,
-                name="update",
-            )(*inputs)
-        rounded_before = direction[:, -1].astype(BF16)
-        rounded_after = direction[:, 0].astype(BF16)
-        rounded_left = direction[:, :, -1].astype(BF16)
-        rounded_right = direction[:, :, 0].astype(BF16)
-        before = passed_along(rounded_before, SEC_CLU, 1)
-        after = passed_along(rounded_after, SEC_CLU, -1)
-        left = passed_along(rounded_left, BLK, 1)
-        right = passed_along(rounded_right, BLK, -1)
-        stiffness_inputs = (direction, residual, before, after, left, right)
-        stiffness_inputs += (weights, matrices, surface)
-        edges = [pltpu.VMEM((cases, slabs, lanes), F32)] * 2
-        edges += [pltpu.VMEM((4, cases, lanes), F32)]
+            inputs += (*halo_image, *halo_residual, *halo_direction, *given)
+            if last:
+                solution, direction, dots = kernel(
+                    functools.partial(field_kernel, iteration == 1, True),
+                    (like(field), like(field), like((cases, lanes))),
+                    inputs,
+                    [pltpu.VMEM(field, F32)] * 2
+                    + [pltpu.VMEM(edge.shape, F32) for edge in halo_image]
+                    + field_scratch,
+                )
+            else:
+                outs = kernel(
+                    functools.partial(field_kernel, iteration == 1, False),
+                    (like(field),) * 3 + edge_like * 2 + image_outputs,
+                    inputs,
+                    field_scratch,
+                )
+                solution, direction, residual = outs[:3]
+                halo_residual, halo_direction = outs[3:7], outs[7:11]
+                image, dots, image_trace, *edges = outs[11:]
         if last:
-            dots = pl.pallas_call(
-                functools.partial(stiffness_kernel, False),
-                out_shape=like((cases, lanes)),
-                scratch_shapes=[pltpu.VMEM(field, F32)] + edges,
-                name="stiffness_last",
-            )(*stiffness_inputs)
-            rows = pl.pallas_call(
+            rows = kernel(
                 last_sums_kernel,
-                out_shape=like((all_count, 1, lanes)),
-                name="last_sums",
-            )(column_pieces, dots)
+                kept((all_count, 1, lanes)),
+                (near(column_pieces), dots),
+            )
             totals = exchanged(rows, ALL)
-            return pl.pallas_call(
+            return kernel(
                 final_kernel,
-                out_shape=like(field),
-                scratch_shapes=[pltpu.VMEM((cases, lanes), F32)],
-                name="final",
-            )(totals, direction, solution)
-        image, image_trace, dots = pl.pallas_call(
-            functools.partial(stiffness_kernel, True),
-            out_shape=(like(field), like((cases, lanes)), like((cases, lanes))),
-            scratch_shapes=edges,
-            name="stiffness",
-        )(*stiffness_inputs)
-
-        z_low = column_pieces.sum(axis=0).astype(BF16)
-        low_mine = exchanged(jnp.broadcast_to(z_low, (clu_count, *z_low.shape)), CLU)
+                like(field),
+                (near(totals), direction, solution),
+                [pltpu.VMEM((cases, lanes), F32)],
+            )
+
+        z_low = kernel(
+            low_kernel, kept((clu_count, cases, lanes), BF16), (near(column_pieces),)
+        )
+        low_mine = exchanged(z_low, CLU)
         low_other = partner(low_mine)
-        keep, send = pl.pallas_call(
+        keep, send = kernel(
             backward_kernel,
-            out_shape=(like((blk_count, cases, lanes)),) * 2,
-            in_specs=[SMEM] * 4 + [VMEM] * 5,
-            scratch_shapes=[
+            (kept((blk_count, cases, lanes)),) * 2,
+            (
+                pairs,
+                dof_lanes,
+                dof_blocks,
+                near(blocks_local),
+                near(low_mine),
+                near(low_other),
+            ),
+            [
                 pltpu.VMEM((2 * half_columns, cases, lanes), BF16),
                 pltpu.VMEM((slot_count // lanes, cases, lanes), F32),
             ],
-            name="backward",
-        )(
-            rows_local,
-            columns_local,
-            live_local,
-            half_local,
-            dof_lanes,
-            dof_blocks,
-            blocks_local,
-            low_mine,
-            low_other,
+            1,
         )
-        arrived = exchanged(keep + partner(send), BLK)
-        payload, own = pl.pallas_call(
+        row_pieces = keep + partner(send)
+        arrived = exchanged(row_pieces, BLK)
+        payload, own, *edges = kernel(
             own_kernel,
-            out_shape=(like((blk_count, cases + 8, lanes)), like((cases, lanes))),
-            in_specs=[SMEM] + [VMEM] * 5,
-            name="own",
-        )(place_local, arrived, image_trace, dots, slot_residual, slot_direction)
+            (kept((blk_count, cases + 8, lanes)), like((cases, lanes)), *edge_kept),
+            (near(arrived), image_trace, dots, own_slots, inverse, *edges),
+        )
         mine = exchanged(payload, BLK)
+        halo_image = sent(edges)
         other = partner(mine)
-        range_sums = pl.pallas_call(
-            range_sum_kernel,
-            out_shape=like((clu_count, cases, lanes)),
-            name="range_sums",
-        )(mine, other)
+        range_sums = kernel(
+            range_sum_kernel, kept((clu_count, cases, lanes)), (near(mine), near(other))
+        )
         sums = exchanged(range_sums, CLU)
 
 

time: 342 us -> 312 us (0.912)
  Pallas kernels: 85.3 us -> 67.2 us
  local copies, waits for them, and re-layouts: 13 us -> 3.33 us
    pallas_call x17, Pallas kernels: 85.3 us -> 67.2 us  [kernel(): pl.pallas_call(body, out_shape=outs, in_specs=[SMEM] * scalars + [pl.Bloc...]
    unnamed x85 -> x62, local copies, waits for them, and re-layouts: 6.69 us -> 1.65 us
    all_to_all x6, starting transfers between devices: 39.6 us -> 36.2 us  [exchanged(): return lax.all_to_all(pieces, axes, split_axis=0, concat_axis=0, tiled=True)]
  transfers between devices with their start and end apart: 30 -> 30, of which waited for: 15 -> 18; matrix products, arithmetic and copies ran while one was open for 5% -> 3% of each run, Pallas kernels for 12% -> 11%
where the time goes in v2:
time: 312 us; the launch traced here: 309 us
  blocking collectives  103 us (33%)
  starting transfers between devices  87.2 us (28%)
  Pallas kernels  67.2 us (22%)
  waiting for transfers between devices  37 us (12%)
  other arithmetic  7.98 us (3%)
  local copies, waits for them, and re-layouts  3.33 us (1%)
    all_to_all x7, blocking collectives, exchanged(): return lax.all_to_all(pieces, axes, split_axis=0, concat_axis=0, tiled=True)  103 us
    pallas_call x17, Pallas kernels, kernel(): pl.pallas_call(body, out_shape=outs, in_specs=[SMEM] * scalars + [pl.Bloc...  67.2 us
    ppermute x14, starting transfers between devices, passed_along(): return lax.ppermute(value, axis, pairs)  44.2 us
    all_to_all x6, starting transfers between devices, exchanged(): return lax.all_to_all(pieces, axes, split_axis=0, concat_axis=0, tiled=True)  36.2 us
    all_to_all x6, waiting for transfers between devices, exchanged(): return lax.all_to_all(pieces, axes, split_axis=0, concat_axis=0, tiled=True)  18.5 us
    ppermute x10, waiting for transfers between devices, partner(): return lax.ppermute(value, 'sec', [(0, 1), (1, 0)])  13 us
    ppermute x10, starting transfers between devices, partner(): return lax.ppermute(value, 'sec', [(0, 1), (1, 0)])  6.84 us
  transfers between devices with their start and end apart: 30, of which 18 were waited for; matrix products, arithmetic and copies ran while one was open for 3% of the time, Pallas kernels for 11%

profile of v2, /device:TPU:8, one launch (start us, length us, event | category | flops | bytes accessed | tf_op | source)
XLA Modules:
  0.0 308.6 jit_solution(8159928416911052962)
XLA Ops:
  1.3 2.8 shard_map.127
  4.1 9.9 %all-to-all-start = ((f32[16,32,128]{2,1,0:T(8,128)}), f32[16,32,128]{2,1,0:T(8,128)S(1)}, u32[]{:S(2)}, u32[]{:S(2)}) async-start(f32[16,32,128]{2,1,0:T(8,128)} %get-tuple-element.65), calls=%async_computation | async-start | bytes 524288 | tf_op jit(solution)/shard_map/all_to_all | solution.py:34
  14.1 4.2 %collective-permute-start.4 = (f32[32,8,128]{2,1,0:T(8,128)S(1)}, f32[32,8,128]{2,1,0:T(8,128)S(1)}, u32[]{:S(2)}, u32[]{:S(2)}) collective-permute-start(f32[32,8,128]{2,1,0:T(8,128)S(1)} %get-tuple-element.71), channel_id=1, source_target_pairs={{0,16},{16,32},{32,48},{48,64},{64,80},{80,96},{96,112},{112,128},... | collective-permute-start | bytes 393224 | tf_op jit(solution)/shard_map/ppermute | solution.py:26
  18.3 1.3 collective-permute-start.5
  19.6 3.4 %collective-permute-start.6 = (f32[32,8,128]{2,1,0:T(8,128)S(1)}, f32[32,8,128]{2,1,0:T(8,128)S(1)}, u32[]{:S(2)}, u32[]{:S(2)}) collective-permute-start(f32[32,8,128]{2,1,0:T(8,128)S(1)} %get-tuple-element.73), channel_id=1, source_target_pairs={{0,1},{1,2},{2,3},{3,4},{4,5},{5,6},{6,7},{7,8},{8,9},{9,10},{10,1... | collective-permute-start | bytes 393224 | tf_op jit(solution)/shard_map/ppermute | solution.py:26
  22.9 4.6 %collective-permute-start.7 = (f32[32,8,128]{2,1,0:T(8,128)S(1)}, f32[32,8,128]{2,1,0:T(8,128)S(1)}, u32[]{:S(2)}, u32[]{:S(2)}) collective-permute-start(f32[32,8,128]{2,1,0:T(8,128)S(1)} %get-tuple-element.74), channel_id=1, source_target_pairs={{1,0},{2,1},{3,2},{4,3},{5,4},{6,5},{7,6},{8,7},{9,8},{10,9},{11,1... | collective-permute-start | bytes 393224 | tf_op jit(solution)/shard_map/ppermute | solution.py:26
  29.0 2.9 select_convert_fusion.1
  33.5 2.5 collective-permute-start
  36.1 1.0 collective-permute-done.refs_5_
  37.1 5.4 %shard_map.128 = (f32[32,32,128]{2,1,0:T(8,128)}, f32[2,32,128]{2,1,0:T(8,128)}, f32[8,32,128]{2,1,0:T(8,128)S(1)}, f32[8,32,128]{2,1,0:T(8,128)S(1)}) custom-call(s32[4,48]{1,0:T(4,128)S(1)} %add_add_fusion.refs_0_.pairs_ref, s32[32,128]{1,0:T(8,128)} %get-tuple-element.130.refs_1_, s32[32,128]{1,0:T(8,128)} %bitcast.79, ...), custom_call_target="tpu_custom_call" | custom-call | tf_op jit(solution)/shard_map/pallas_call | solution.py:51
  43.0 0.9 collective-permute-done.1
  44.6 5.8 %all-to-all-start.1 = ((f32[8,32,128]{2,1,0:T(8,128)}), f32[8,32,128]{2,1,0:T(8,128)S(1)}, u32[]{:S(2)}, u32[]{:S(2)}) async-start(f32[8,32,128]{2,1,0:T(8,128)} %add.82), calls=%async_computation.1 | async-start | bytes 262144 | tf_op jit(solution)/shard_map/all_to_all | solution.py:34
  50.4 0.8 fusion.7.inverse_ref.refs_2_
  51.2 7.1 %all-to-all-done.1.pieces_ref = f32[8,32,128]{2,1,0:T(8,128)S(1)} async-done(((f32[8,32,128]{2,1,0:T(8,128)}), f32[8,32,128]{2,1,0:T(8,128)S(1)}, u32[]{:S(2)}, u32[]{:S(2)}) %all-to-all-start.1) | async-done | bytes 131104 | tf_op jit(solution)/shard_map/all_to_all | solution.py:34
  59.0 3.4 %all-to-all-start.2 = ((bf16[8,32,128]{2,1,0:T(8,128)(2,1)}), bf16[8,32,128]{2,1,0:T(8,128)(2,1)S(1)}, u32[]{:S(2)}, u32[]{:S(2)}) async-start(bf16[8,32,128]{2,1,0:T(8,128)(2,1)} %shard_map.129), calls=%async_computation.2 | async-start | bytes 131072 | tf_op jit(solution)/shard_map/all_to_all | solution.py:34
  62.3 7.7 %all-to-all-done.2.mine_ref = bf16[8,32,128]{2,1,0:T(8,128)(2,1)S(1)} async-done(((bf16[8,32,128]{2,1,0:T(8,128)(2,1)}), bf16[8,32,128]{2,1,0:T(8,128)(2,1)S(1)}, u32[]{:S(2)}, u32[]{:S(2)}) %all-to-all-start.2) | async-done | bytes 65568 | tf_op jit(solution)/shard_map/all_to_all | solution.py:34
  70.0 1.2 collective-permute-done.2.other_ref
  71.3 2.7 collective-permute-start.8
  74.0 7.2 %shard_map.130 = (f32[16,32,128]{2,1,0:T(8,128)S(1)}, f32[16,32,128]{2,1,0:T(8,128)S(1)}) custom-call(s32[4,48]{1,0:T(4,128)S(1)} %add_add_fusion.refs_0_.pairs_ref, s32[32,128]{1,0:T(8,128)} %get-tuple-element.126.lanes_ref, s32[32,128]{1,0:T(8,128)} %get-tuple-element.125.blocks_ref, bf16[48,128,128]{2,1,0:T(8,128)(2,1)S(1)} %bitcast.75, ...), custom_call_target="tpu_custom_call" | custom-call | tf_op jit(solution)/shard_map/pallas_call | solution.py:51
  81.3 1.5 collective-permute-done.3
  82.8 1.9 collective-permute-start.9
  84.7 0.7 add.83
  85.5 7.8 %all-to-all-start.3 = ((f32[16,32,128]{2,1,0:T(8,128)}), f32[16,32,128]{2,1,0:T(8,128)S(1)}, u32[]{:S(2)}, u32[]{:S(2)}) async-start(f32[16,32,128]{2,1,0:T(8,128)} %add.83), calls=%async_computation.3 | async-start | bytes 524288 | tf_op jit(solution)/shard_map/all_to_all | solution.py:34
  93.5 0.8 broadcast_in_dim.89.refs_4_.refs_18_.refs_19_
  94.3 4.5 %shard_map.131 = (f32[32,8,8,128]{3,2,1,0:T(8,128)}, f32[32,128]{1,0:T(8,128)}, f32[32,128]{1,0:T(8,128)}, f32[32,8,128]{2,1,0:T(8,128)}, f32[32,8,128]{2,1,0:T(...) custom-call(f32[32,8,8,128]{3,2,1,0:T(8,128)} %refs_5_.1, f32[32,8,128]{2,1,0:T(8,128)} %copy-done.4, ...), custom_call_target="tpu_custom_call" | custom-call | tf_op jit(solution)/shard_map/pallas_call | solution.py:51
  98.8 3.8 %all-to-all-done.3.arrived_ref = f32[16,32,128]{2,1,0:T(8,128)S(1)} async-done(((f32[16,32,128]{2,1,0:T(8,128)}), f32[16,32,128]{2,1,0:T(8,128)S(1)}, u32[]{:S(2)}, u32[]{:S(2)}) %all-to-all-start.3) | async-done | bytes 262176 | tf_op jit(solution)/shard_map/all_to_all | solution.py:34
  102.6 2.8 shard_map.132
  105.4 15.3 %all_to_all.65.mine_ref.refs_6_ = f32[16,40,128]{2,1,0:T(8,128)S(1)} all-to-all(f32[16,40,128]{2,1,0:T(8,128)S(1)} %get-tuple-element.82), channel_id=1, replica_groups=mesh['sec'=2,'clu_0'=4,'clu_1'=2,'blk_0'=2,'blk_1'=8] {'blk_0','blk_1'}, dimensions={0} | all-to-all | bytes 655360 | tf_op jit(solution)/shard_map/all_to_all | solution.py:34
  120.7 1.6 collective-permute-done.10.other_ref.refs_7_
  122.4 13.6 %all_to_all.66.refs_8_.refs_0_ = f32[8,32,128]{2,1,0:T(8,128)S(1)} all-to-all(f32[8,32,128]{2,1,0:T(8,128)S(1)} %shard_map.133), channel_id=1, replica_groups=mesh['sec'=2,'clu_0'=4,'clu_1'=2,'blk_0'=2,'blk_1'=8] {'clu_0','clu_1'}, dimensions={0} | all-to-all | bytes 262144 | tf_op jit(solution)/shard_map/all_to_all | solution.py:34
  136.0 6.4 %shard_map.134 = (f32[32,32,128]{2,1,0:T(8,128)}, f32[32,32,128]{2,1,0:T(8,128)}, f32[2,32,128]{2,1,0:T(8,128)}, f32[8,32,128]{2,1,0:T(8,128)S(1)}, f32[8,32,128]{2,1,0:T(8,128)S(1)}) custom-call(s32[4,48]{1,0:T(4,128)S(1)} %add_add_fusion.refs_0_.pairs_ref, s32[32,128]{1,0:T(8,128)} %get-tuple-element.130.refs_1_, s32[32,128]{1,0:T(8,128)} %bitcast.80, ...), custom_call_target="tpu_custom_call" | custom-call | tf_op jit(solution)/shard_map/pallas_call | solution.py:51
  142.4 1.3 collective-permute-done.11
  143.8 10.6 %all_to_all.67.pieces_ref = f32[8,32,128]{2,1,0:T(8,128)S(1)} all-to-all(f32[8,32,128]{2,1,0:T(8,128)S(1)} %add.86), channel_id=1, replica_groups=mesh['sec'=2,'clu_0'=4,'clu_1'=2,'blk_0'=2,'blk_1'=8] {'clu_0','clu_1'}, dimensions={0} | all-to-all | bytes 262144 | tf_op jit(solution)/shard_map/all_to_all | solution.py:34
  154.4 10.5 %all_to_all.68.mine_ref = bf16[8,32,128]{2,1,0:T(8,128)(2,1)S(1)} all-to-all(bf16[8,32,128]{2,1,0:T(8,128)(2,1)S(1)} %shard_map.135), channel_id=1, replica_groups=mesh['sec'=2,'clu_0'=4,'clu_1'=2,'blk_0'=2,'blk_1'=8] {'clu_0','clu_1'}, dimensions={0} | all-to-all | bytes 131072 | tf_op jit(solution)/shard_map/all_to_all | solution.py:34
  164.9 1.3 collective-permute-done.12.other_ref
  166.1 7.2 %shard_map.136 = (f32[16,32,128]{2,1,0:T(8,128)S(1)}, f32[16,32,128]{2,1,0:T(8,128)S(1)}) custom-call(s32[4,48]{1,0:T(4,128)S(1)} %add_add_fusion.refs_0_.pairs_ref, s32[32,128]{1,0:T(8,128)} %get-tuple-element.126.lanes_ref, s32[32,128]{1,0:T(8,128)} %get-tuple-element.125.blocks_ref, bf16[48,128,128]{2,1,0:T(8,128)(2,1)S(1)} %bitcast.77, ...), custom_call_target="tpu_custom_call" | custom-call | tf_op jit(solution)/shard_map/pallas_call | solution.py:51
  173.5 1.4 collective-permute-done.13
  174.9 0.7 add.87
  175.6 5.8 %all-to-all-start.8 = ((f32[16,32,128]{2,1,0:T(8,128)}), f32[16,32,128]{2,1,0:T(8,128)S(1)}, u32[]{:S(2)}, u32[]{:S(2)}) async-start(f32[16,32,128]{2,1,0:T(8,128)} %add.87), calls=%async_computation.8 | async-start | bytes 524288 | tf_op jit(solution)/shard_map/all_to_all | solution.py:34
  181.5 2.3 collective-permute-start.14
  183.8 1.3 collective-permute-start.15
  185.1 3.4 %collective-permute-start.16 = (f32[32,8,128]{2,1,0:T(8,128)S(1)}, f32[32,8,128]{2,1,0:T(8,128)S(1)}, u32[]{:S(2)}, u32[]{:S(2)}) collective-permute-start(f32[32,8,128]{2,1,0:T(8,128)S(1)} %get-tuple-element.93), channel_id=1, source_target_pairs={{0,1},{1,2},{2,3},{3,4},{4,5},{5,6},{6,7},{7,8},{8,9},{9,10},{10,1... | collective-permute-start | bytes 393224 | tf_op jit(solution)/shard_map/ppermute | solution.py:26
  188.5 4.6 %collective-permute-start.17 = (f32[32,8,128]{2,1,0:T(8,128)S(1)}, f32[32,8,128]{2,1,0:T(8,128)S(1)}, u32[]{:S(2)}, u32[]{:S(2)}) collective-permute-start(f32[32,8,128]{2,1,0:T(8,128)S(1)} %get-tuple-element.94), channel_id=1, source_target_pairs={{1,0},{2,1},{3,2},{4,3},{5,4},{6,5},{7,6},{8,7},{9,8},{10,9},{11,1... | collective-permute-start | bytes 393224 | tf_op jit(solution)/shard_map/ppermute | solution.py:26
  194.4 1.2 collective-permute-done.17.refs_9_
  196.2 8.7 %shard_map.137 = (f32[32,8,8,128]{3,2,1,0:T(8,128)}, f32[32,8,8,128]{3,2,1,0:T(8,128)}, f32[32,8,8,128]{3,2,1,0:T(8,128)}, f32[32,8,128]{2,1,0:T(8,128)}, f32[32...) custom-call(f32[8,32,128]{2,1,0:T(8,128)} %copy-done.1, ...), custom_call_target="tpu_custom_call" | custom-call | tf_op jit(solution)/shard_map/pallas_call | solution.py:51
  204.9 2.8 shard_map.138
  207.7 16.2 %all_to_all.69.mine_ref.refs_6_ = f32[16,40,128]{2,1,0:T(8,128)S(1)} all-to-all(f32[16,40,128]{2,1,0:T(8,128)S(1)} %get-tuple-element.102), channel_id=1, replica_groups=mesh['sec'=2,'clu_0'=4,'clu_1'=2,'blk_0'=2,'blk_1'=8] {'blk_0','blk_1'}, dimensions={0} | all-to-all | bytes 655360 | tf_op jit(solution)/shard_map/all_to_all | solution.py:34
  224.0 3.5 %collective-permute-start.18 = (f32[16,40,128]{2,1,0:T(8,128)S(1)}, f32[16,40,128]{2,1,0:T(8,128)S(1)}, u32[]{:S(2)}, u32[]{:S(2)}) collective-permute-start(f32[16,40,128]{2,1,0:T(8,128)S(1)} %all_to_all.69.mine_ref.refs_6_), channel_id=1, source_target_pairs={{0,128},{128,0},{1,129},{129,1},{2,130},{130,2},{3,131},{131,3},{4... | collective-permute-start | bytes 983048 | tf_op jit(solution)/shard_map/ppermute | solution.py:30
  227.5 1.3 collective-permute-done.18.other_ref.refs_7_
  228.9 12.1 %all_to_all.70.refs_8_.refs_0_ = f32[8,32,128]{2,1,0:T(8,128)S(1)} all-to-all(f32[8,32,128]{2,1,0:T(8,128)S(1)} %shard_map.139), channel_id=1, replica_groups=mesh['sec'=2,'clu_0'=4,'clu_1'=2,'blk_0'=2,'blk_1'=8] {'clu_0','clu_1'}, dimensions={0} | all-to-all | bytes 262144 | tf_op jit(solution)/shard_map/all_to_all | solution.py:34
  241.0 7.7 %shard_map.140 = (f32[8,64,128]{2,1,0:T(8,128)S(1)}, f32[8,64,128]{2,1,0:T(8,128)S(1)}) custom-call(s32[4,48]{1,0:T(4,128)S(1)} %add_add_fusion.refs_0_.pairs_ref, s32[32,128]{1,0:T(8,128)} %get-tuple-element.130.refs_1_, s32[32,128]{1,0:T(8,128)} %bitcast.81, bf16[48,128,128]{2,1,0:T(8,128)(2,1)S(1)} %bitcast.78, f32[32,32,128]{2,1,0:T(8,128)} %get-tuple-element.83.refs_4_, ...), custom_call_target="tpu_custom_call" | custom-call | tf_op jit(solution)/shard_map/pallas_call | solution.py:51
  248.8 1.5 collective-permute-done.19
  250.3 0.7 add.88
  251.0 3.4 %all-to-all-start.11 = ((f32[8,64,128]{2,1,0:T(8,128)}), f32[8,64,128]{2,1,0:T(8,128)S(1)}, u32[]{:S(2)}, u32[]{:S(2)}) async-start(f32[8,64,128]{2,1,0:T(8,128)} %add.88), calls=%async_computation.11 | async-start | bytes 524288 | tf_op jit(solution)/shard_map/all_to_all | solution.py:34
  254.5 5.3 %collective-permute-start.20 = (f32[32,8,128]{2,1,0:T(8,128)S(1)}, f32[32,8,128]{2,1,0:T(8,128)S(1)}, u32[]{:S(2)}, u32[]{:S(2)}) collective-permute-start(f32[32,8,128]{2,1,0:T(8,128)S(1)} %get-tuple-element.110), channel_id=1, source_target_pairs={{0,16},{16,32},{32,48},{48,64},{64,80},{80,96},{96,112},{112,128},... | collective-permute-start | bytes 393224 | tf_op jit(solution)/shard_map/ppermute | solution.py:26
  259.8 1.3 collective-permute-start.21
  261.1 4.1 %collective-permute-start.22 = (f32[32,8,128]{2,1,0:T(8,128)S(1)}, f32[32,8,128]{2,1,0:T(8,128)S(1)}, u32[]{:S(2)}, u32[]{:S(2)}) collective-permute-start(f32[32,8,128]{2,1,0:T(8,128)S(1)} %get-tuple-element.112), channel_id=1, source_target_pairs={{0,1},{1,2},{2,3},{3,4},{4,5},{5,6},{6,7},{7,8},{8,9},{9,10},{10,1... | collective-permute-start | bytes 393224 | tf_op jit(solution)/shard_map/ppermute | solution.py:26
  265.2 3.8 %collective-permute-start.23 = (f32[32,8,128]{2,1,0:T(8,128)S(1)}, f32[32,8,128]{2,1,0:T(8,128)S(1)}, u32[]{:S(2)}, u32[]{:S(2)}) collective-permute-start(f32[32,8,128]{2,1,0:T(8,128)S(1)} %get-tuple-element.113), channel_id=1, source_target_pairs={{1,0},{2,1},{3,2},{4,3},{5,4},{6,5},{7,6},{8,7},{9,8},{10,9},{11,1... | collective-permute-start | bytes 393224 | tf_op jit(solution)/shard_map/ppermute | solution.py:26
  269.1 1.0 collective-permute-done.22.refs_9_
  270.1 2.0 collective-permute-done.23.refs_10_
  272.7 6.9 %shard_map.141 = (f32[32,8,8,128]{3,2,1,0:T(8,128)}, f32[32,8,8,128]{3,2,1,0:T(8,128)}, f32[32,128]{1,0:T(8,128)}) custom-call(f32[8,32,128]{2,1,0:T(8,128)} %copy-done.2, f32[32,128]{1,0:T(8,128)} %get-tuple-element.105.refs_1_, s32[8,8,128]{2,1,0:T(8,128)} %fusion.7.inverse_ref.refs_2_, f32[32,8,8,128]{3,2,1,0:T(8,128)} %get-tuple-element.106.refs_3_, ...), custom_call_target="tpu_custom_call" | custom-call | tf_op jit(solution)/shard_map/pallas_call | solution.py:51
  279.6 1.0 shard_map.142
  280.6 25.0 %all_to_all.71.sums_ref = f32[256,1,128]{2,1,0:T(1,128)S(1)} all-to-all(f32[256,1,128]{2,1,0:T(1,128)S(1)} %shard_map.142), channel_id=1, replica_groups=mesh['sec'=2,'clu_0'=4,'clu_1'=2,'blk_0'=2,'blk_1'=8] {'sec','clu_0','cl..., dimensions={0} | all-to-all | bytes 262144 | tf_op jit(solution)/shard_map/all_to_all | solution.py:34
  305.5 3.0 shard_map.143
  (115 shorter events, 8.8 us)
Async XLA Ops:
  0.0 28.4 %copy-start.22 = (s32[4096]{0:T(1024)S(1)}, s32[4096]{0:T(1024)}, u32[]{:S(2)}) copy-start(s32[4096]{0:T(1024)} %param.25) | copy-start | bytes 49156
  4.1 29.3 %all-to-all-start = ((f32[16,32,128]{2,1,0:T(8,128)}), f32[16,32,128]{2,1,0:T(8,128)S(1)}, u32[]{:S(2)}, u32[]{:S(2)}) async-start(f32[16,32,128]{2,1,0:T(8,128)} %get-tuple-element.65), calls=%async_computation | async-start | bytes 524288 | tf_op jit(solution)/shard_map/all_to_all | solution.py:34
  14.1 79.3 %collective-permute-start.4 = (f32[32,8,128]{2,1,0:T(8,128)S(1)}, f32[32,8,128]{2,1,0:T(8,128)S(1)}, u32[]{:S(2)}, u32[]{:S(2)}) collective-permute-start(f32[32,8,128]{2,1,0:T(8,128)S(1)} %get-tuple-element.71), channel_id=1, source_target_pairs={{0,16},{16,32},{32,48},{48,64},{64,80},{80,96},{96,112},{112,128},... | collective-permute-start | bytes 393224 | tf_op jit(solution)/shard_map/ppermute | solution.py:26
  18.3 75.1 %collective-permute-start.5 = (f32[32,8,128]{2,1,0:T(8,128)S(1)}, f32[32,8,128]{2,1,0:T(8,128)S(1)}, u32[]{:S(2)}, u32[]{:S(2)}) collective-permute-start(f32[32,8,128]{2,1,0:T(8,128)S(1)} %get-tuple-element.72), channel_id=1, source_target_pairs={{16,0},{32,16},{48,32},{64,48},{80,64},{96,80},{112,96},{128,112},... | collective-permute-start | bytes 393224 | tf_op jit(solution)/shard_map/ppermute | solution.py:26
  19.6 73.9 %collective-permute-start.6 = (f32[32,8,128]{2,1,0:T(8,128)S(1)}, f32[32,8,128]{2,1,0:T(8,128)S(1)}, u32[]{:S(2)}, u32[]{:S(2)}) collective-permute-start(f32[32,8,128]{2,1,0:T(8,128)S(1)} %get-tuple-element.73), channel_id=1, source_target_pairs={{0,1},{1,2},{2,3},{3,4},{4,5},{5,6},{6,7},{7,8},{8,9},{9,10},{10,1... | collective-permute-start | bytes 393224 | tf_op jit(solution)/shard_map/ppermute | solution.py:26
  22.9 70.5 %collective-permute-start.7 = (f32[32,8,128]{2,1,0:T(8,128)S(1)}, f32[32,8,128]{2,1,0:T(8,128)S(1)}, u32[]{:S(2)}, u32[]{:S(2)}) collective-permute-start(f32[32,8,128]{2,1,0:T(8,128)S(1)} %get-tuple-element.74), channel_id=1, source_target_pairs={{1,0},{2,1},{3,2},{4,3},{5,4},{6,5},{7,6},{8,7},{9,8},{10,9},{11,1... | collective-permute-start | bytes 393224 | tf_op jit(solution)/shard_map/ppermute | solution.py:26
  29.0 3.5 %copy-start.8 = (s32[4096]{0:T(1024)}, s32[4096]{0:T(1024)S(1)}, u32[]{:S(2)}) copy-start(s32[4096]{0:T(1024)S(1)} %get-tuple-element.131) | copy-start | bytes 49156
  31.9 1.2 copy-start.23
  31.9 1.2 copy-start.19
  31.9 1.2 copy-start.20
  31.9 1.2 copy-start.25
  31.9 1.2 copy-start.21
  31.9 1.2 copy-start.13
  31.9 1.2 copy-start.24
  32.0 1.3 copy-start.26
  32.0 1.4 copy-start.14
  32.0 5.1 %copy-start = (bf16[1,1,48,128,128]{4,3,2,1,0:T(8,128)(2,1)S(1)}, bf16[1,1,48,128,128]{4,3,2,1,0:T(8,128)(2,1)}, u32[]{:S(2)}) copy-start(bf16[1,1,48,128,128]{4,3,2,1,0:T(8,128)(2,1)} %param.20) | copy-start | bytes 4718596
  33.5 3.6 %collective-permute-start = (f32[16,32,128]{2,1,0:T(8,128)S(1)}, f32[16,32,128]{2,1,0:T(8,128)S(1)}, u32[]{:S(2)}, u32[]{:S(2)}) collective-permute-start(f32[16,32,128]{2,1,0:T(8,128)S(1)} %all-to-all-done.refs_4_), channel_id=1, source_target_pairs={{0,128},{128,0},{1,129},{129,1},{2,130},{130,2},{3,131},{131,3},{4... | collective-permute-start | bytes 786440 | tf_op jit(solution)/shard_map/ppermute | solution.py:30
  36.1 22.9 %copy-start.3 = (bf16[5,128,128]{2,1,0:T(8,128)(2,1)}, bf16[5,128,128]{2,1,0:T(8,128)(2,1)S(1)}, u32[]{:S(2)}) copy-start(bf16[5,128,128]{2,1,0:T(8,128)(2,1)S(1)} %bitcast_dynamic-update-slice_fusion.refs_5_.refs_19_.refs_20_) | copy-start | bytes 491524
  42.5 1.4 collective-permute-start.1
  44.6 13.8 %all-to-all-start.1 = ((f32[8,32,128]{2,1,0:T(8,128)}), f32[8,32,128]{2,1,0:T(8,128)S(1)}, u32[]{:S(2)}, u32[]{:S(2)}) async-start(f32[8,32,128]{2,1,0:T(8,128)} %add.82), calls=%async_computation.1 | async-start | bytes 262144 | tf_op jit(solution)/shard_map/all_to_all | solution.py:34
  59.0 11.0 %all-to-all-start.2 = ((bf16[8,32,128]{2,1,0:T(8,128)(2,1)}), bf16[8,32,128]{2,1,0:T(8,128)(2,1)S(1)}, u32[]{:S(2)}, u32[]{:S(2)}) async-start(bf16[8,32,128]{2,1,0:T(8,128)(2,1)} %shard_map.129), calls=%async_computation.2 | async-start | bytes 131072 | tf_op jit(solution)/shard_map/all_to_all | solution.py:34
  70.0 1.3 collective-permute-start.2
  71.3 9.9 %collective-permute-start.8 = (f32[1,8]{1,0:T(1,128)S(1)}, f32[1,8]{1,0:T(1,128)S(1)}, u32[]{:S(2)}, u32[]{:S(2)}) collective-permute-start(f32[1,8]{1,0:T(1,128)S(1)} %slice.20), channel_id=1, source_target_pairs={{0,16},{16,32},{32,48},{48,64},{64,80},{80,96},{96,112},{112,128},... | collective-permute-start | bytes 104 | tf_op jit(solution)/shard_map/ppermute | solution.py:26
  81.2 1.6 collective-permute-start.3
  82.8 10.4 %collective-permute-start.9 = (f32[8,1]{1,0:T(8,128)S(1)}, f32[8,1]{1,0:T(8,128)S(1)}, u32[]{:S(2)}, u32[]{:S(2)}) collective-permute-start(f32[8,1]{1,0:T(8,128)S(1)} %slice.22), channel_id=1, source_target_pairs={{0,1},{1,2},{2,3},{3,4},{4,5},{5,6},{6,7},{7,8},{8,9},{9,10},{10,1... | collective-permute-start | bytes 104 | tf_op jit(solution)/shard_map/ppermute | solution.py:26
  85.5 17.1 %all-to-all-start.3 = ((f32[16,32,128]{2,1,0:T(8,128)}), f32[16,32,128]{2,1,0:T(8,128)S(1)}, u32[]{:S(2)}, u32[]{:S(2)}) async-start(f32[16,32,128]{2,1,0:T(8,128)} %add.83), calls=%async_computation.3 | async-start | bytes 524288 | tf_op jit(solution)/shard_map/all_to_all | solution.py:34
  93.4 0.9 copy-start.4
  93.4 0.9 copy-start.5
  93.4 0.9 copy-start.6
  93.5 0.9 copy-start.7
  120.7 1.6 collective-permute-start.10
  136.0 6.4 %copy-start.1 = (f32[8,32,128]{2,1,0:T(8,128)}, f32[8,32,128]{2,1,0:T(8,128)S(1)}, u32[]{:S(2)}) copy-start(f32[8,32,128]{2,1,0:T(8,128)S(1)} %all_to_all.66.refs_8_.refs_0_) | copy-start | bytes 393220
  142.4 1.3 collective-permute-start.11
  164.9 1.3 collective-permute-start.12
  173.3 1.6 collective-permute-start.13
  175.6 29.3 %all-to-all-start.8 = ((f32[16,32,128]{2,1,0:T(8,128)}), f32[16,32,128]{2,1,0:T(8,128)S(1)}, u32[]{:S(2)}, u32[]{:S(2)}) async-start(f32[16,32,128]{2,1,0:T(8,128)} %add.87), calls=%async_computation.8 | async-start | bytes 524288 | tf_op jit(solution)/shard_map/all_to_all | solution.py:34
  181.5 11.6 %collective-permute-start.14 = (f32[32,8,128]{2,1,0:T(8,128)S(1)}, f32[32,8,128]{2,1,0:T(8,128)S(1)}, u32[]{:S(2)}, u32[]{:S(2)}) collective-permute-start(f32[32,8,128]{2,1,0:T(8,128)S(1)} %get-tuple-element.91), channel_id=1, source_target_pairs={{0,16},{16,32},{32,48},{48,64},{64,80},{80,96},{96,112},{112,128},... | collective-permute-start | bytes 393224 | tf_op jit(solution)/shard_map/ppermute | solution.py:26
  183.8 10.0 %collective-permute-start.15 = (f32[32,8,128]{2,1,0:T(8,128)S(1)}, f32[32,8,128]{2,1,0:T(8,128)S(1)}, u32[]{:S(2)}, u32[]{:S(2)}) collective-permute-start(f32[32,8,128]{2,1,0:T(8,128)S(1)} %get-tuple-element.92), channel_id=1, source_target_pairs={{16,0},{32,16},{48,32},{64,48},{80,64},{96,80},{112,96},{128,112},... | collective-permute-start | bytes 393224 | tf_op jit(solution)/shard_map/ppermute | solution.py:26
  185.1 9.2 %collective-permute-start.16 = (f32[32,8,128]{2,1,0:T(8,128)S(1)}, f32[32,8,128]{2,1,0:T(8,128)S(1)}, u32[]{:S(2)}, u32[]{:S(2)}) collective-permute-start(f32[32,8,128]{2,1,0:T(8,128)S(1)} %get-tuple-element.93), channel_id=1, source_target_pairs={{0,1},{1,2},{2,3},{3,4},{4,5},{5,6},{6,7},{7,8},{8,9},{9,10},{10,1... | collective-permute-start | bytes 393224 | tf_op jit(solution)/shard_map/ppermute | solution.py:26
  188.5 7.1 %collective-permute-start.17 = (f32[32,8,128]{2,1,0:T(8,128)S(1)}, f32[32,8,128]{2,1,0:T(8,128)S(1)}, u32[]{:S(2)}, u32[]{:S(2)}) collective-permute-start(f32[32,8,128]{2,1,0:T(8,128)S(1)} %get-tuple-element.94), channel_id=1, source_target_pairs={{1,0},{2,1},{3,2},{4,3},{5,4},{6,5},{7,6},{8,7},{9,8},{10,9},{11,1... | collective-permute-start | bytes 393224 | tf_op jit(solution)/shard_map/ppermute | solution.py:26
  193.1 2.5 copy-start.9
  193.8 1.8 copy-start.10
  194.4 1.2 copy-start.11
  195.6 0.7 copy-start.12
  224.0 4.8 %collective-permute-start.18 = (f32[16,40,128]{2,1,0:T(8,128)S(1)}, f32[16,40,128]{2,1,0:T(8,128)S(1)}, u32[]{:S(2)}, u32[]{:S(2)}) collective-permute-start(f32[16,40,128]{2,1,0:T(8,128)S(1)} %all_to_all.69.mine_ref.refs_6_), channel_id=1, source_target_pairs={{0,128},{128,0},{1,129},{129,1},{2,130},{130,2},{3,131},{131,3},{4... | collective-permute-start | bytes 983048 | tf_op jit(solution)/shard_map/ppermute | solution.py:30
  241.0 7.7 %copy-start.2 = (f32[8,32,128]{2,1,0:T(8,128)}, f32[8,32,128]{2,1,0:T(8,128)S(1)}, u32[]{:S(2)}) copy-start(f32[8,32,128]{2,1,0:T(8,128)S(1)} %all_to_all.70.refs_8_.refs_0_) | copy-start | bytes 393220
  248.7 1.6 collective-permute-start.19
  251.0 28.6 %all-to-all-start.11 = ((f32[8,64,128]{2,1,0:T(8,128)}), f32[8,64,128]{2,1,0:T(8,128)S(1)}, u32[]{:S(2)}, u32[]{:S(2)}) async-start(f32[8,64,128]{2,1,0:T(8,128)} %add.88), calls=%async_computation.11 | async-start | bytes 524288 | tf_op jit(solution)/shard_map/all_to_all | solution.py:34
  254.5 14.6 %collective-permute-start.20 = (f32[32,8,128]{2,1,0:T(8,128)S(1)}, f32[32,8,128]{2,1,0:T(8,128)S(1)}, u32[]{:S(2)}, u32[]{:S(2)}) collective-permute-start(f32[32,8,128]{2,1,0:T(8,128)S(1)} %get-tuple-element.110), channel_id=1, source_target_pairs={{0,16},{16,32},{32,48},{48,64},{64,80},{80,96},{96,112},{112,128},... | collective-permute-start | bytes 393224 | tf_op jit(solution)/shard_map/ppermute | solution.py:26
  259.8 9.3 %collective-permute-start.21 = (f32[32,8,128]{2,1,0:T(8,128)S(1)}, f32[32,8,128]{2,1,0:T(8,128)S(1)}, u32[]{:S(2)}, u32[]{:S(2)}) collective-permute-start(f32[32,8,128]{2,1,0:T(8,128)S(1)} %get-tuple-element.111), channel_id=1, source_target_pairs={{16,0},{32,16},{48,32},{64,48},{80,64},{96,80},{112,96},{128,112},... | collective-permute-start | bytes 393224 | tf_op jit(solution)/shard_map/ppermute | solution.py:26
  261.1 9.0 %collective-permute-start.22 = (f32[32,8,128]{2,1,0:T(8,128)S(1)}, f32[32,8,128]{2,1,0:T(8,128)S(1)}, u32[]{:S(2)}, u32[]{:S(2)}) collective-permute-start(f32[32,8,128]{2,1,0:T(8,128)S(1)} %get-tuple-element.112), channel_id=1, source_target_pairs={{0,1},{1,2},{2,3},{3,4},{4,5},{5,6},{6,7},{7,8},{8,9},{9,10},{10,1... | collective-permute-start | bytes 393224 | tf_op jit(solution)/shard_map/ppermute | solution.py:26
  265.2 6.9 %collective-permute-start.23 = (f32[32,8,128]{2,1,0:T(8,128)S(1)}, f32[32,8,128]{2,1,0:T(8,128)S(1)}, u32[]{:S(2)}, u32[]{:S(2)}) collective-permute-start(f32[32,8,128]{2,1,0:T(8,128)S(1)} %get-tuple-element.113), channel_id=1, source_target_pairs={{1,0},{2,1},{3,2},{4,3},{5,4},{6,5},{7,6},{8,7},{9,8},{10,9},{11,1... | collective-permute-start | bytes 393224 | tf_op jit(solution)/shard_map/ppermute | solution.py:26
  269.1 3.0 copy-start.15
  269.1 3.0 copy-start.16
  270.1 2.0 copy-start.17
  272.1 0.6 copy-start.18

commit v3 on v2

--- a/solution.py
+++ b/solution.py
@@ -114,11 +114,13 @@
     return (make((cases, width, lanes)),) * 2 + (make((cases, slabs, lanes)),) * 2
 
 
-def first_trace_kernel(field_ref, surface_ref, out_ref, *edge_refs):
-    slabs = field_ref.shape[1]
+def first_trace_kernel(field_ref, surface_ref, end_ref, out_ref, *edge_refs):
+    cases, slabs = field_ref.shape[:2]
     copies = out_ref.shape[0]
-    lane_index = jnp.broadcast_to(surface_ref[0:1, :], (8, 128))
-    block_index = jnp.broadcast_to(surface_ref[1:2, :], (8, 128))
+    edge_refs[0][cases] = end_ref[0]
+    edge_refs[2][cases] = end_ref[1]
+    local = jnp.broadcast_to(surface_ref[...], (8, 128))
+    lane_index, block_index = local & 127, local >> 7
 
     def step(case, carry):
         row = trace_of(field_ref, case, lane_index, block_index)
@@ -147,15 +149,11 @@
     return totals
 
 
-def scalars_of(pieces_ref):
-    return jnp.sum(pieces_ref[...], axis=0)
-
-
-def alpha_beta(sums):
-    norm = sums[:, 0:1]
-    curvature = sums[:, 1:2]
+def alpha_beta(sums_ref, cases):
+    row = jnp.sum(sums_ref[...], axis=0)
+    norm, curvature, crossed, squared = (row_to_column(row, i * cases, cases) for i in range(4))
     alpha = norm / curvature
-    following = norm - 2.0 * alpha * sums[:, 2:3] + alpha * alpha * sums[:, 3:4]
+    following = norm - 2.0 * alpha * crossed + alpha * alpha * squared
     beta = jnp.maximum(following, 0.0) / norm
     return alpha, beta
 
@@ -172,17 +170,20 @@
         direction_ref[count:] = other_ref[...]
     else:
         old_residual_ref, old_direction_ref, mine_ref, other_ref, sums_ref = refs[:5]
+        steps_ref, refs = refs[5], refs[6:]
         if last:
-            keep_ref, send_ref, direction_ref, low_ref = refs[5:9]
-            rest = refs[9:]
+            keep_ref, send_ref, direction_ref, low_ref = refs[:4]
+            rest = refs[4:]
         else:
-            residual_ref, direction_ref, slots_ref, keep_ref, send_ref, low_ref = refs[5:11]
-            rest = refs[11:]
+            residual_ref, direction_ref, slots_ref, keep_ref, send_ref, low_ref = refs[:6]
+            rest = refs[6:]
         cases = old_direction_ref.shape[1]
         count = mine_ref.shape[0]
-        alpha, beta = alpha_beta(scalars_of(sums_ref))
+        alpha, beta = alpha_beta(sums_ref, cases)
         alpha = jnp.broadcast_to(alpha, (cases, 128))
         beta = jnp.broadcast_to(beta, (cases, 128))
+        steps_ref[0] = alpha
+        steps_ref[1] = beta
         for half, image_ref in ((0, mine_ref), (1, other_ref)):
             for i in range(count):
                 b = half * count + i
@@ -208,7 +209,7 @@
             low_ref[d] = low
         return carry
 
-    lax.fori_loop(0, direction_ref.shape[0], step, 0, unroll=2)
+    lax.fori_loop(0, direction_ref.shape[0], step, 0, unroll=4)
     half_count = keep_ref.shape[0]
     sums_scratch = rest[0]
     sums_scratch[...] = jnp.zeros(sums_scratch.shape, F32)
@@ -256,7 +257,7 @@
                 out_ref[d, 8 * g : 8 * g + 8, :] = total
             return carry
 
-        lax.fori_loop(0, count, step, 0, unroll=2)
+        lax.fori_loop(0, count, step, 0, unroll=4)
 
 
 def low_kernel(pieces_ref, out_ref):
@@ -283,13 +284,13 @@
 
     def taken(a):
         if a < 0:
-            return before_ref[...]
+            return before_ref[:cases]
         if a == slabs:
             return after_ref[...]
         return direction_ref[:, a]
 
     high_ref[...] = product(right_ref[...], 3)
-    low_ref[...] = product(left_ref[...], 4)
+    low_ref[...] = product(left_ref[:cases], 4)
     for a in range(slabs):
         own = taken(a)
         result = weights_ref[0, a][None] * product(own, 0)
@@ -300,8 +301,8 @@
         result = result - weights_ref[5, a][None] * high_ref[:, a : a + 1, :]
         result = result - weights_ref[6, a][None] * low_ref[:, a : a + 1, :]
         image_ref[:, a] = result
-    lane_index = jnp.broadcast_to(surface_ref[0:1, :], (8, 128))
-    block_index = jnp.broadcast_to(surface_ref[1:2, :], (8, 128))
+    local = jnp.broadcast_to(surface_ref[...], (8, 128))
+    lane_index, block_index = local & 127, local >> 7
 
     def step(case, carry):
         r = residual_ref[case]
@@ -326,8 +327,9 @@
     dots_ref[...] = dots
 
 
-def first_stiffness_kernel(direction_ref, *refs):
-    stiffness(direction_ref, direction_ref, refs[:4], refs[4:7], refs[7:14], refs[14:])
+def stiffness_kernel(same, direction_ref, *refs):
+    residual_ref, refs = (direction_ref, refs) if same else (refs[0], refs[1:])
+    stiffness(direction_ref, residual_ref, refs[:4], refs[4:7], refs[7:14], refs[14:])
 
 
 def field_kernel(first, last, *refs):
@@ -338,10 +340,10 @@
         del refs[:n]
         return taken
 
-    sums_ref, own_ref, inverse_ref, image_ref, residual_ref, direction_ref = take(6)
+    steps_ref, own_ref, inverse_ref, image_ref, residual_ref, direction_ref = take(6)
     solution_ref = None if first else take(1)[0]
     halo_image_refs, halo_residual_refs, halo_direction_refs = take(4), take(4), take(4)
-    given_refs = take(3)
+    given_refs = take(3) if last else None
     new_solution_ref, new_direction_ref = take(2)
     if last:
         (dots_ref,) = take(1)
@@ -352,16 +354,11 @@
     else:
         (new_residual_ref,) = take(1)
         new_halo_residual_refs, new_halo_direction_refs = take(4), take(4)
-        out_refs = take(7)
-    alpha_ref, beta_ref = take(2)
     cases, slabs, width = direction_ref.shape[:3]
-    alpha, beta = alpha_beta(scalars_of(sums_ref))
-    alpha_ref[...] = jnp.broadcast_to(alpha, (cases, 128))
-    beta_ref[...] = jnp.broadcast_to(beta, (cases, 128))
 
     def step(case, carry):
-        alpha = jnp.broadcast_to(alpha_ref[pl.ds(case, 1), :], (width, 128))
-        beta = jnp.broadcast_to(beta_ref[pl.ds(case, 1), :], (width, 128))
+        alpha = jnp.broadcast_to(steps_ref[0, pl.ds(case, 1), :], (width, 128))
+        beta = jnp.broadcast_to(steps_ref[1, pl.ds(case, 1), :], (width, 128))
         own = jnp.broadcast_to(own_ref[pl.ds(case, 1), :], (width, 128))
         for i in range(4):
             r = halo_residual_refs[i][case] - alpha * halo_image_refs[i][case]
@@ -384,15 +381,13 @@
         return carry
 
     lax.fori_loop(0, cases, step, 0, unroll=4)
-    stiffness(
-        new_direction_ref, new_residual_ref, new_halo_direction_refs, given_refs, out_refs, refs
-    )
-
-
-def own_kernel(arrived_ref, trace_ref, dots_ref, slots_ref, inverse_ref, *refs):
-    edge_refs, (out_ref, own_ref), new_edge_refs = refs[:4], refs[4:6], refs[6:]
+    if last:
+        halo_refs = new_halo_direction_refs
+        stiffness(new_direction_ref, new_residual_ref, halo_refs, given_refs, out_refs, refs)
+
+
+def own_kernel(arrived_ref, trace_ref, dots_ref, slots_ref, out_ref, own_ref):
     copies, cases = out_ref.shape[0], trace_ref.shape[0]
-    slabs, width = inverse_ref.shape[:2]
     y = jnp.sum(arrived_ref[...], axis=0)
     own_ref[...] = y
     trace = trace_ref[...]
@@ -407,10 +402,20 @@
             column = column + jnp.sum(term, axis=1, keepdims=True)
         row = row + column_to_row(column, i * cases)
     image = trace + y
-    row8 = jnp.broadcast_to(row, (8, 128))
+    rows = jnp.broadcast_to(row, (8, 128))
     for i in range(copies):
         out_ref[i, :cases, :] = image
-        out_ref[i, cases:, :] = row8
+        out_ref[i, cases:, :] = rows
+
+
+def range_sum_kernel(cases, mine_ref, other_ref, out_ref):
+    row = jnp.sum(mine_ref[:, cases:, :], axis=0) + jnp.sum(other_ref[:, cases:, :], axis=0)
+    out_ref[...] = jnp.broadcast_to(row[0:1, :][None], out_ref.shape)
+
+
+def edges_kernel(own_ref, inverse_ref, *refs):
+    edge_refs, new_edge_refs = refs[:4], refs[4:]
+    slabs, width = inverse_ref.shape[:2]
     sides = (
         inverse_ref[slabs - 1],
         inverse_ref[0],
@@ -426,21 +431,7 @@
             new_edge_ref[case] = edge_ref[case] + jnp.where(there, extra, 0.0)
         return carry
 
-    lax.fori_loop(0, cases, step, 0, unroll=4)
-
-
-def range_sum_kernel(mine_ref, other_ref, out_ref):
-    copies, cases = out_ref.shape[0], out_ref.shape[1]
-    row = jnp.sum(mine_ref[:, cases : cases + 8, :], axis=0) + jnp.sum(
-        other_ref[:, cases : cases + 8, :], axis=0
-    )
-    row = row[0:1, :]
-    lane = lane_iota((cases, 128))
-    sums = jnp.zeros((cases, 128), F32)
-    for i in range(4):
-        sums = jnp.where(lane == i, row_to_column(row, i * cases, cases), sums)
-    for i in range(copies):
-        out_ref[i] = sums
+    lax.fori_loop(0, own_ref.shape[0], step, 0, unroll=4)
 
 
 def last_sums_kernel(arrived_ref, dots_ref, out_ref):
@@ -501,7 +492,7 @@
     owners = 2 * blk_count
     all_count = owners * clu_count
     slot_count = interface_slot.shape[0]
-    surface = jnp.stack([surface_local % lanes, surface_local // lanes])
+    surface = surface_local.reshape(1, lanes)
 
     def edges_by(make):
         return edge_outputs(cases, slabs, width, lanes, make)
@@ -513,10 +504,18 @@
         right = passed_along(edges[3], BLK, -1)
         return before, after, left, right
 
+    first_edges = [
+        kept((cases + 1, width, lanes)),
+        kept((cases, width, lanes)),
+        kept((cases + 1, slabs, lanes)),
+        kept((cases, slabs, lanes)),
+    ]
+    ends = jnp.stack([across_weight[-1, :], along_weight[:, -1]])
+    ends = jnp.broadcast_to(ends[:, :, None], (2, width, lanes))
     trace, *edges = kernel(
         first_trace_kernel,
-        (kept((blk_count, cases, lanes)), *edges_by(kept)),
-        (right_side, surface),
+        (kept((blk_count, cases, lanes)), *first_edges),
+        (right_side, surface, ends),
     )
     mine = exchanged(trace, BLK)
     other = partner(mine)
@@ -551,23 +550,6 @@
         .reshape(slabs, width, lanes)
     )
 
-    across_edge = passed_along(across_weight[-1:, :], SEC_CLU, 1)
-    across_lower = jnp.concatenate([across_edge, across_weight[:-1, :]], axis=0)
-    along_edge = passed_along(along_weight[:, -1:], BLK, 1)
-    along_lower = jnp.concatenate([along_edge, along_weight[:, :-1]], axis=1)
-    tile = jnp.arange(width, dtype=jnp.int32)[None, :]
-    weights = jnp.stack(
-        [
-            block_weight,
-            across_weight,
-            across_lower,
-            jnp.where(tile < width - 1, along_weight, 0.0),
-            jnp.where(tile > 0, along_lower, 0.0),
-            jnp.where(tile == width - 1, along_weight, 0.0),
-            jnp.where(tile == 0, along_lower, 0.0),
-        ]
-    )
-    weights = jnp.broadcast_to(weights[..., None], (*weights.shape, lanes))
     matrices = jnp.stack(
         [block_stiffness, across_matrix, across_matrix.T, along_matrix, along_matrix.T]
     )
@@ -583,13 +565,31 @@
         ]
     )
     forward_inputs = (pairs, slot_lanes, slot_blocks, near(blocks_local))
-    given = (weights, matrices, surface)
+
+    def weights_of(halo):
+        across_edge = halo[0][cases, :, 0][None, :]
+        along_edge = halo[2][cases, :, 0][:, None]
+        across_lower = jnp.concatenate([across_edge, across_weight[:-1, :]], axis=0)
+        along_lower = jnp.concatenate([along_edge, along_weight[:, :-1]], axis=1)
+        tile = jnp.arange(width, dtype=jnp.int32)[None, :]
+        weights = jnp.stack(
+            [
+                block_weight,
+                across_weight,
+                across_lower,
+                jnp.where(tile < width - 1, along_weight, 0.0),
+                jnp.where(tile > 0, along_lower, 0.0),
+                jnp.where(tile == width - 1, along_weight, 0.0),
+                jnp.where(tile == 0, along_lower, 0.0),
+            ]
+        )
+        return jnp.broadcast_to(weights[..., None], (*weights.shape, lanes))
+
     edge_kept, edge_like = edges_by(kept), edges_by(like)
-    own_slots_shape = like((2, cases, lanes))
+    own_slots_shape = steps_shape = like((2, cases, lanes))
     image_outputs = (like(field), like((cases, lanes)), like((cases, lanes)), *edge_like)
     stiffness_scratch = [pltpu.VMEM((cases, slabs, lanes), F32)] * 2
     stiffness_scratch += [pltpu.VMEM((4, cases, lanes), F32)]
-    field_scratch = [pltpu.VMEM((cases, lanes), F32)] * 2 + stiffness_scratch
     solution = None
     residual = right_side
     direction = right_side
@@ -603,6 +603,25 @@
             pltpu.VMEM((2 * half_columns, deep, lanes), F32),
         ]
         halves = (kept((half_columns, deep, lanes)),) * 2
+        if not first:
+            inputs = (*forward_inputs, slot_residual, slot_direction)
+            inputs += (near(mine), near(other), near(sums))
+            if last:
+                steps, keep, send = kernel(
+                    functools.partial(forward_kernel, False, True),
+                    (steps_shape, *halves),
+                    inputs,
+                    [pltpu.VMEM(slots_shape, F32)] + scratch,
+                    1,
+                )
+            else:
+                steps, slot_residual, slot_direction, own_slots, keep, send = kernel(
+                    functools.partial(forward_kernel, False, False),
+                    (steps_shape, *(like(slots_shape),) * 2, own_slots_shape, *halves),
+                    inputs,
+                    scratch,
+                    1,
+                )
         if first:
             slot_direction, own_slots, keep, send = kernel(
                 functools.partial(forward_kernel, True, False),
@@ -612,65 +631,50 @@
                 1,
             )
             slot_residual = slot_direction
-        else:
-            inputs = (*forward_inputs, slot_residual, slot_direction)
-            inputs += (near(mine), near(other), near(sums))
-            if last:
-                keep, send = kernel(
-                    functools.partial(forward_kernel, False, True),
-                    halves,
-                    inputs,
-                    [pltpu.VMEM(slots_shape, F32)] + scratch,
-                    1,
-                )
-            else:
-                slot_residual, slot_direction, own_slots, keep, send = kernel(
-                    functools.partial(forward_kernel, False, False),
-                    (like(slots_shape), like(slots_shape), own_slots_shape, *halves),
-                    inputs,
-                    scratch,
-                    1,
-                )
         pieces = keep + partner(send)
         column_pieces = exchanged(pieces, CLU)
 
         if first:
             halo_residual = halo_direction = sent(edges)
+            given = (weights_of(halo_direction), matrices, surface)
             image, dots, image_trace, *edges = kernel(
-                first_stiffness_kernel,
+                functools.partial(stiffness_kernel, True),
                 image_outputs,
                 (right_side, *halo_direction, *given),
                 stiffness_scratch,
             )
         else:
-            inputs = (sums, own, inverse, image, residual, direction)
+            inputs = (steps, own, inverse, image, residual, direction)
             if iteration > 1:
                 inputs += (solution,)
-            inputs += (*halo_image, *halo_residual, *halo_direction, *given)
+            inputs += (*halo_image, *halo_residual, *halo_direction)
             if last:
                 solution, direction, dots = kernel(
                     functools.partial(field_kernel, iteration == 1, True),
                     (like(field), like(field), like((cases, lanes))),
-                    inputs,
+                    (*inputs, *given),
                     [pltpu.VMEM(field, F32)] * 2
                     + [pltpu.VMEM(edge.shape, F32) for edge in halo_image]
-                    + field_scratch,
+                    + stiffness_scratch,
                 )
             else:
                 outs = kernel(
                     functools.partial(field_kernel, iteration == 1, False),
-                    (like(field),) * 3 + edge_like * 2 + image_outputs,
+                    (like(field),) * 3 + edge_like * 2,
                     inputs,
-                    field_scratch,
                 )
                 solution, direction, residual = outs[:3]
                 halo_residual, halo_direction = outs[3:7], outs[7:11]
-                image, dots, image_trace, *edges = outs[11:]
+            if not last:
+                image, dots, image_trace, *edges = kernel(
+                    functools.partial(stiffness_kernel, False),
+                    image_outputs,
+                    (direction, residual, *halo_direction, *given),
+                    stiffness_scratch,
+                )
         if last:
             rows = kernel(
-                last_sums_kernel,
-                kept((all_count, 1, lanes)),
-                (near(column_pieces), dots),
+                last_sums_kernel, kept((all_count, 1, lanes)), (near(column_pieces), dots)
             )
             totals = exchanged(rows, ALL)
             return kernel(
@@ -680,9 +684,7 @@
                 [pltpu.VMEM((cases, lanes), F32)],
             )
 
-        z_low = kernel(
-            low_kernel, kept((clu_count, cases, lanes), BF16), (near(column_pieces),)
-        )
+        z_low = kernel(low_kernel, kept((clu_count, cases, lanes), BF16), (near(column_pieces),))
         low_mine = exchanged(z_low, CLU)
         low_other = partner(low_mine)
         keep, send = kernel(
@@ -704,18 +706,21 @@
         )
         row_pieces = keep + partner(send)
         arrived = exchanged(row_pieces, BLK)
-        payload, own, *edges = kernel(
+        payload, own = kernel(
             own_kernel,
-            (kept((blk_count, cases + 8, lanes)), like((cases, lanes)), *edge_kept),
-            (near(arrived), image_trace, dots, own_slots, inverse, *edges),
+            (kept((blk_count, cases + 8, lanes)), like((cases, lanes))),
+            (near(arrived), image_trace, dots, own_slots),
         )
         mine = exchanged(payload, BLK)
+        edges = kernel(edges_kernel, edge_kept, (own, inverse, *edges))
         halo_image = sent(edges)
         other = partner(mine)
-        range_sums = kernel(
-            range_sum_kernel, kept((clu_count, cases, lanes)), (near(mine), near(other))
+        row = kernel(
+            functools.partial(range_sum_kernel, cases),
+            kept((clu_count, 1, lanes)),
+            (near(mine), near(other)),
         )
-        sums = exchanged(range_sums, CLU)
+        sums = exchanged(row, CLU)
 
 
 def solution(mesh):

time: 312 us -> 306 us (0.981)
  starting transfers between devices: 87.2 us -> 82.1 us
  blocking collectives: 103 us -> 99.3 us
    ppermute x14 -> x12, starting transfers between devices: 44.2 us -> 39.6 us  [passed_along(): return lax.ppermute(value, axis, pairs)]
    all_to_all x7, blocking collectives: 103 us -> 99.3 us  [exchanged(): return lax.all_to_all(pieces, axes, split_axis=0, concat_axis=0, tiled=True)]
    pallas_call x17 -> x20, Pallas kernels: 67.2 us -> 67.6 us  [kernel(): pl.pallas_call(body, out_shape=outs, in_specs=[SMEM] * scalars + [pl.Bloc...]
  transfers between devices with their start and end apart: 30 -> 28, of which waited for: 18 -> 18; matrix products, arithmetic and copies ran while one was open for 3% -> 3% of each run, Pallas kernels for 11% -> 13%
where the time goes in v3:
time: 306 us; the launch traced here: 302 us
  blocking collectives  99.3 us (32%)
  starting transfers between devices  82.1 us (27%)
  Pallas kernels  67.6 us (22%)
  waiting for transfers between devices  38 us (12%)
  other arithmetic  6.73 us (2%)
  local copies, waits for them, and re-layouts  5.68 us (2%)
    all_to_all x7, blocking collectives, exchanged(): return lax.all_to_all(pieces, axes, split_axis=0, concat_axis=0, tiled=True)  99.3 us
    pallas_call x20, Pallas kernels, kernel(): pl.pallas_call(body, out_shape=outs, in_specs=[SMEM] * scalars + [pl.Bloc...  67.6 us
    ppermute x12, starting transfers between devices, passed_along(): return lax.ppermute(value, axis, pairs)  39.6 us
    all_to_all x6, starting transfers between devices, exchanged(): return lax.all_to_all(pieces, axes, split_axis=0, concat_axis=0, tiled=True)  35.6 us
    all_to_all x6, waiting for transfers between devices, exchanged(): return lax.all_to_all(pieces, axes, split_axis=0, concat_axis=0, tiled=True)  19.8 us
    ppermute x10, waiting for transfers between devices, partner(): return lax.ppermute(value, 'sec', [(0, 1), (1, 0)])  12.8 us
    ppermute x10, starting transfers between devices, partner(): return lax.ppermute(value, 'sec', [(0, 1), (1, 0)])  6.9 us
  transfers between devices with their start and end apart: 28, of which 18 were waited for; matrix products, arithmetic and copies ran while one was open for 3% of the time, Pallas kernels for 13%

profile of v3, /device:TPU:8, one launch (start us, length us, event | category | flops | bytes accessed | tf_op | source)
XLA Modules:
  0.0 302.0 jit_solution(1775360615261965712)
XLA Ops:
  0.0 0.9 slice_reduce_fusion.1
  2.3 2.9 shard_map.127
  5.2 9.9 %all-to-all-start = ((f32[16,32,128]{2,1,0:T(8,128)}), f32[16,32,128]{2,1,0:T(8,128)S(1)}, u32[]{:S(2)}, u32[]{:S(2)}) async-start(f32[16,32,128]{2,1,0:T(8,128)} %get-tuple-element.67), calls=%async_computation | async-start | bytes 524288 | tf_op jit(solution)/shard_map/all_to_all | solution.py:34
  15.1 4.2 %collective-permute-start.4 = (f32[33,8,128]{2,1,0:T(8,128)S(1)}, f32[33,8,128]{2,1,0:T(8,128)S(1)}, u32[]{:S(2)}, u32[]{:S(2)}) collective-permute-start(f32[33,8,128]{2,1,0:T(8,128)S(1)} %get-tuple-element.73), channel_id=1, source_target_pairs={{0,16},{16,32},{32,48},{48,64},{64,80},{80,96},{96,112},{112,128},... | collective-permute-start | bytes 405512 | tf_op jit(solution)/shard_map/ppermute | solution.py:26
  19.3 1.3 collective-permute-start.5
  20.6 3.4 %collective-permute-start.6 = (f32[33,8,128]{2,1,0:T(8,128)S(1)}, f32[33,8,128]{2,1,0:T(8,128)S(1)}, u32[]{:S(2)}, u32[]{:S(2)}) collective-permute-start(f32[33,8,128]{2,1,0:T(8,128)S(1)} %get-tuple-element.75), channel_id=1, source_target_pairs={{0,1},{1,2},{2,3},{3,4},{4,5},{5,6},{6,7},{7,8},{8,9},{9,10},{10,1... | collective-permute-start | bytes 405512 | tf_op jit(solution)/shard_map/ppermute | solution.py:26
  24.0 4.6 %collective-permute-start.7 = (f32[32,8,128]{2,1,0:T(8,128)S(1)}, f32[32,8,128]{2,1,0:T(8,128)S(1)}, u32[]{:S(2)}, u32[]{:S(2)}) collective-permute-start(f32[32,8,128]{2,1,0:T(8,128)S(1)} %get-tuple-element.76), channel_id=1, source_target_pairs={{1,0},{2,1},{3,2},{4,3},{5,4},{6,5},{7,6},{8,7},{9,8},{10,9},{11,1... | collective-permute-start | bytes 393224 | tf_op jit(solution)/shard_map/ppermute | solution.py:26
  29.3 2.9 select_convert_fusion.1
  34.4 2.5 collective-permute-start
  37.1 0.9 collective-permute-done.refs_5_
  38.0 4.9 %shard_map.128 = (f32[32,32,128]{2,1,0:T(8,128)}, f32[2,32,128]{2,1,0:T(8,128)}, f32[8,32,128]{2,1,0:T(8,128)S(1)}, f32[8,32,128]{2,1,0:T(8,128)S(1)}) custom-call(s32[4,48]{1,0:T(4,128)S(1)} %add_add_fusion.refs_0_.pairs_ref, s32[32,128]{1,0:T(8,128)} %get-tuple-element.134.refs_1_, s32[32,128]{1,0:T(8,128)} %bitcast.66, ...), custom_call_target="tpu_custom_call" | custom-call | tf_op jit(solution)/shard_map/pallas_call | solution.py:51
  43.3 1.0 collective-permute-done.1
  45.0 5.9 %all-to-all-start.1 = ((f32[8,32,128]{2,1,0:T(8,128)}), f32[8,32,128]{2,1,0:T(8,128)S(1)}, u32[]{:S(2)}, u32[]{:S(2)}) async-start(f32[8,32,128]{2,1,0:T(8,128)} %add.66), calls=%async_computation.1 | async-start | bytes 262144 | tf_op jit(solution)/shard_map/all_to_all | solution.py:34
  50.8 7.9 %all-to-all-done.1.pieces_ref = f32[8,32,128]{2,1,0:T(8,128)S(1)} async-done(((f32[8,32,128]{2,1,0:T(8,128)}), f32[8,32,128]{2,1,0:T(8,128)S(1)}, u32[]{:S(2)}, u32[]{:S(2)}) %all-to-all-start.1) | async-done | bytes 131104 | tf_op jit(solution)/shard_map/all_to_all | solution.py:34
  59.4 3.4 %all-to-all-start.2 = ((bf16[8,32,128]{2,1,0:T(8,128)(2,1)}), bf16[8,32,128]{2,1,0:T(8,128)(2,1)S(1)}, u32[]{:S(2)}, u32[]{:S(2)}) async-start(bf16[8,32,128]{2,1,0:T(8,128)(2,1)} %shard_map.129), calls=%async_computation.2 | async-start | bytes 131072 | tf_op jit(solution)/shard_map/all_to_all | solution.py:34
  62.7 7.7 %all-to-all-done.2.mine_ref = bf16[8,32,128]{2,1,0:T(8,128)(2,1)S(1)} async-done(((bf16[8,32,128]{2,1,0:T(8,128)(2,1)}), bf16[8,32,128]{2,1,0:T(8,128)(2,1)S(1)}, u32[]{:S(2)}, u32[]{:S(2)}) %all-to-all-start.2) | async-done | bytes 65568 | tf_op jit(solution)/shard_map/all_to_all | solution.py:34
  70.5 1.1 collective-permute-done.2.other_ref
  71.7 6.6 %shard_map.130 = (f32[16,32,128]{2,1,0:T(8,128)S(1)}, f32[16,32,128]{2,1,0:T(8,128)S(1)}) custom-call(s32[4,48]{1,0:T(4,128)S(1)} %add_add_fusion.refs_0_.pairs_ref, s32[32,128]{1,0:T(8,128)} %get-tuple-element.130.lanes_ref, s32[32,128]{1,0:T(8,128)} %get-tuple-element.129.blocks_ref, bf16[48,128,128]{2,1,0:T(8,128)(2,1)S(1)} %bitcast.62, ...), custom_call_target="tpu_custom_call" | custom-call | tf_op jit(solution)/shard_map/pallas_call | solution.py:51
  78.6 1.3 collective-permute-done.3
  80.7 7.2 %all-to-all-start.3 = ((f32[16,32,128]{2,1,0:T(8,128)}), f32[16,32,128]{2,1,0:T(8,128)S(1)}, u32[]{:S(2)}, u32[]{:S(2)}) async-start(f32[16,32,128]{2,1,0:T(8,128)} %add.67), calls=%async_computation.3 | async-start | bytes 524288 | tf_op jit(solution)/shard_map/all_to_all | solution.py:34
  88.1 0.8 broadcast_in_dim.96.refs_4_.refs_5_.refs_19_
  88.9 4.5 %shard_map.131 = (f32[32,8,8,128]{3,2,1,0:T(8,128)}, f32[32,128]{1,0:T(8,128)}, f32[32,128]{1,0:T(8,128)}, f32[32,8,128]{2,1,0:T(8,128)}, f32[32,8,128]{2,1,0:T(...) custom-call(f32[32,8,8,128]{3,2,1,0:T(8,128)} %refs_5_.1, f32[33,8,128]{2,1,0:T(8,128)} %copy-done.2, ...), custom_call_target="tpu_custom_call" | custom-call | tf_op jit(solution)/shard_map/pallas_call | solution.py:51
  93.4 4.2 %all-to-all-done.3.arrived_ref = f32[16,32,128]{2,1,0:T(8,128)S(1)} async-done(((f32[16,32,128]{2,1,0:T(8,128)}), f32[16,32,128]{2,1,0:T(8,128)S(1)}, u32[]{:S(2)}, u32[]{:S(2)}) %all-to-all-start.3) | async-done | bytes 262176 | tf_op jit(solution)/shard_map/all_to_all | solution.py:34
  97.6 1.4 shard_map.132
  99.1 15.4 %all_to_all.65.mine_ref.refs_6_ = f32[16,40,128]{2,1,0:T(8,128)S(1)} all-to-all(f32[16,40,128]{2,1,0:T(8,128)S(1)} %get-tuple-element.80), channel_id=1, replica_groups=mesh['sec'=2,'clu_0'=4,'clu_1'=2,'blk_0'=2,'blk_1'=8] {'blk_0','blk_1'}, dimensions={0} | all-to-all | bytes 655360 | tf_op jit(solution)/shard_map/all_to_all | solution.py:34
  114.4 1.6 collective-permute-done.8.other_ref.refs_7_
  116.1 10.2 %all_to_all.66.refs_8_ = f32[8,1,128]{2,1,0:T(1,128)S(1)} all-to-all(f32[8,1,128]{2,1,0:T(1,128)S(1)} %shard_map.133), channel_id=1, replica_groups=mesh['sec'=2,'clu_0'=4,'clu_1'=2,'blk_0'=2,'blk_1'=8] {'clu_0','clu_1'}, dimensions={0} | all-to-all | bytes 8192 | tf_op jit(solution)/shard_map/all_to_all | solution.py:34
  126.2 5.8 %shard_map.134 = (f32[2,32,128]{2,1,0:T(8,128)}, f32[32,32,128]{2,1,0:T(8,128)}, f32[32,32,128]{2,1,0:T(8,128)}, f32[2,32,128]{2,1,0:T(8,128)}, f32[8,32,128]{2,1,0:T(8,128)S(1)}, /*index=5*/f32[8,32,128]{2,1,0:T(8,128)S(1)}) custom-call(s32[4,48]{1,0:T(4,128)S(1)} %add_add_fusion.refs_0_.pairs_ref, s32[32,128]{1,0:T(8,128)} %get-tuple-element.134.refs_1_, ...), custom_call_target="tpu_custom_call" | custom-call | tf_op jit(solution)/shard_map/pallas_call | solution.py:51
  132.1 1.3 collective-permute-done.9
  133.4 10.5 %all_to_all.67.pieces_ref = f32[8,32,128]{2,1,0:T(8,128)S(1)} all-to-all(f32[8,32,128]{2,1,0:T(8,128)S(1)} %add.68), channel_id=1, replica_groups=mesh['sec'=2,'clu_0'=4,'clu_1'=2,'blk_0'=2,'blk_1'=8] {'clu_0','clu_1'}, dimensions={0} | all-to-all | bytes 262144 | tf_op jit(solution)/shard_map/all_to_all | solution.py:34
  143.9 10.3 %all_to_all.68.mine_ref = bf16[8,32,128]{2,1,0:T(8,128)(2,1)S(1)} all-to-all(bf16[8,32,128]{2,1,0:T(8,128)(2,1)S(1)} %shard_map.135), channel_id=1, replica_groups=mesh['sec'=2,'clu_0'=4,'clu_1'=2,'blk_0'=2,'blk_1'=8] {'clu_0','clu_1'}, dimensions={0} | all-to-all | bytes 131072 | tf_op jit(solution)/shard_map/all_to_all | solution.py:34
  154.2 1.3 collective-permute-done.10.other_ref
  155.5 6.6 %shard_map.136 = (f32[16,32,128]{2,1,0:T(8,128)S(1)}, f32[16,32,128]{2,1,0:T(8,128)S(1)}) custom-call(s32[4,48]{1,0:T(4,128)S(1)} %add_add_fusion.refs_0_.pairs_ref, s32[32,128]{1,0:T(8,128)} %get-tuple-element.130.lanes_ref, s32[32,128]{1,0:T(8,128)} %get-tuple-element.129.blocks_ref, bf16[48,128,128]{2,1,0:T(8,128)(2,1)S(1)} %bitcast.64, ...), custom_call_target="tpu_custom_call" | custom-call | tf_op jit(solution)/shard_map/pallas_call | solution.py:51
  162.3 1.4 collective-permute-done.11
  164.5 5.8 %all-to-all-start.8 = ((f32[16,32,128]{2,1,0:T(8,128)}), f32[16,32,128]{2,1,0:T(8,128)S(1)}, u32[]{:S(2)}, u32[]{:S(2)}) async-start(f32[16,32,128]{2,1,0:T(8,128)} %add.69), calls=%async_computation.8 | async-start | bytes 524288 | tf_op jit(solution)/shard_map/all_to_all | solution.py:34
  170.4 0.8 fusion.7.inverse_ref.refs_2_
  171.2 2.0 shard_map.137
  173.2 2.4 collective-permute-start.12
  175.6 1.3 collective-permute-start.13
  176.9 3.4 %collective-permute-start.14 = (f32[32,8,128]{2,1,0:T(8,128)S(1)}, f32[32,8,128]{2,1,0:T(8,128)S(1)}, u32[]{:S(2)}, u32[]{:S(2)}) collective-permute-start(f32[32,8,128]{2,1,0:T(8,128)S(1)} %get-tuple-element.96), channel_id=1, source_target_pairs={{0,1},{1,2},{2,3},{3,4},{4,5},{5,6},{6,7},{7,8},{8,9},{9,10},{10,1... | collective-permute-start | bytes 393224 | tf_op jit(solution)/shard_map/ppermute | solution.py:26
  180.3 4.6 %collective-permute-start.15 = (f32[32,8,128]{2,1,0:T(8,128)S(1)}, f32[32,8,128]{2,1,0:T(8,128)S(1)}, u32[]{:S(2)}, u32[]{:S(2)}) collective-permute-start(f32[32,8,128]{2,1,0:T(8,128)S(1)} %get-tuple-element.97), channel_id=1, source_target_pairs={{1,0},{2,1},{3,2},{4,3},{5,4},{6,5},{7,6},{8,7},{9,8},{10,9},{11,1... | collective-permute-start | bytes 393224 | tf_op jit(solution)/shard_map/ppermute | solution.py:26
  185.1 0.8 collective-permute-done.14.refs_8_
  185.9 1.4 collective-permute-done.15.refs_9_
  188.0 5.6 %shard_map.138 = (f32[32,8,8,128]{3,2,1,0:T(8,128)}, f32[32,8,8,128]{3,2,1,0:T(8,128)}, f32[32,8,8,128]{3,2,1,0:T(8,128)}, f32[32,8,128]{2,1,0:T(8,128)}, f32[32...) custom-call(f32[2,32,128]{2,1,0:T(8,128)} %get-tuple-element.87.refs, ...), custom_call_target="tpu_custom_call" | custom-call | tf_op jit(solution)/shard_map/pallas_call | solution.py:51
  193.6 4.9 %shard_map.139 = (f32[32,8,8,128]{3,2,1,0:T(8,128)}, f32[32,128]{1,0:T(8,128)}, f32[32,128]{1,0:T(8,128)}, f32[32,8,128]{2,1,0:T(8,128)}, f32[32,8,128]{2,1,0:T(...) custom-call(f32[32,8,8,128]{3,2,1,0:T(8,128)} %get-tuple-element.98.direction_ref.refs_5_, ...), custom_call_target="tpu_custom_call" | custom-call | tf_op jit(solution)/shard_map/pallas_call | solution.py:51
  198.5 1.4 shard_map.140
  200.0 16.2 %all_to_all.69.mine_ref.refs_6_ = f32[16,40,128]{2,1,0:T(8,128)S(1)} all-to-all(f32[16,40,128]{2,1,0:T(8,128)S(1)} %get-tuple-element.107), channel_id=1, replica_groups=mesh['sec'=2,'clu_0'=4,'clu_1'=2,'blk_0'=2,'blk_1'=8] {'blk_0','blk_1'}, dimensions={0} | all-to-all | bytes 655360 | tf_op jit(solution)/shard_map/all_to_all | solution.py:34
  216.2 3.5 %collective-permute-start.16 = (f32[16,40,128]{2,1,0:T(8,128)S(1)}, f32[16,40,128]{2,1,0:T(8,128)S(1)}, u32[]{:S(2)}, u32[]{:S(2)}) collective-permute-start(f32[16,40,128]{2,1,0:T(8,128)S(1)} %all_to_all.69.mine_ref.refs_6_), channel_id=1, source_target_pairs={{0,128},{128,0},{1,129},{129,1},{2,130},{130,2},{3,131},{131,3},{4... | collective-permute-start | bytes 983048 | tf_op jit(solution)/shard_map/ppermute | solution.py:30
  219.7 1.3 collective-permute-done.16.other_ref.refs_7_
  221.0 11.8 %all_to_all.70.refs_8_ = f32[8,1,128]{2,1,0:T(1,128)S(1)} all-to-all(f32[8,1,128]{2,1,0:T(1,128)S(1)} %shard_map.141), channel_id=1, replica_groups=mesh['sec'=2,'clu_0'=4,'clu_1'=2,'blk_0'=2,'blk_1'=8] {'clu_0','clu_1'}, dimensions={0} | all-to-all | bytes 8192 | tf_op jit(solution)/shard_map/all_to_all | solution.py:34
  232.8 7.5 %shard_map.142 = (f32[2,32,128]{2,1,0:T(8,128)}, f32[8,64,128]{2,1,0:T(8,128)S(1)}, f32[8,64,128]{2,1,0:T(8,128)S(1)}) custom-call(s32[4,48]{1,0:T(4,128)S(1)} %add_add_fusion.refs_0_.pairs_ref, s32[32,128]{1,0:T(8,128)} %get-tuple-element.134.refs_1_, s32[32,128]{1,0:T(8,128)} %bitcast.68, bf16[48,128,128]{2,1,0:T(8,128)(2,1)S(1)} %bitcast.65, ...), custom_call_target="tpu_custom_call" | custom-call | tf_op jit(solution)/shard_map/pallas_call | solution.py:51
  240.4 1.5 collective-permute-done.17
  242.6 3.4 %all-to-all-start.11 = ((f32[8,64,128]{2,1,0:T(8,128)}), f32[8,64,128]{2,1,0:T(8,128)S(1)}, u32[]{:S(2)}, u32[]{:S(2)}) async-start(f32[8,64,128]{2,1,0:T(8,128)} %add.72), calls=%async_computation.11 | async-start | bytes 524288 | tf_op jit(solution)/shard_map/all_to_all | solution.py:34
  246.1 2.0 shard_map.143
  248.1 5.3 %collective-permute-start.18 = (f32[32,8,128]{2,1,0:T(8,128)S(1)}, f32[32,8,128]{2,1,0:T(8,128)S(1)}, u32[]{:S(2)}, u32[]{:S(2)}) collective-permute-start(f32[32,8,128]{2,1,0:T(8,128)S(1)} %get-tuple-element.118), channel_id=1, source_target_pairs={{0,16},{16,32},{32,48},{48,64},{64,80},{80,96},{96,112},{112,128},... | collective-permute-start | bytes 393224 | tf_op jit(solution)/shard_map/ppermute | solution.py:26
  253.4 1.3 collective-permute-start.19
  254.7 4.1 %collective-permute-start.20 = (f32[32,8,128]{2,1,0:T(8,128)S(1)}, f32[32,8,128]{2,1,0:T(8,128)S(1)}, u32[]{:S(2)}, u32[]{:S(2)}) collective-permute-start(f32[32,8,128]{2,1,0:T(8,128)S(1)} %get-tuple-element.120), channel_id=1, source_target_pairs={{0,1},{1,2},{2,3},{3,4},{4,5},{5,6},{6,7},{7,8},{8,9},{9,10},{10,1... | collective-permute-start | bytes 393224 | tf_op jit(solution)/shard_map/ppermute | solution.py:26
  258.9 3.8 %collective-permute-start.21 = (f32[32,8,128]{2,1,0:T(8,128)S(1)}, f32[32,8,128]{2,1,0:T(8,128)S(1)}, u32[]{:S(2)}, u32[]{:S(2)}) collective-permute-start(f32[32,8,128]{2,1,0:T(8,128)S(1)} %get-tuple-element.121), channel_id=1, source_target_pairs={{1,0},{2,1},{3,2},{4,3},{5,4},{6,5},{7,6},{8,7},{9,8},{10,9},{11,1... | collective-permute-start | bytes 393224 | tf_op jit(solution)/shard_map/ppermute | solution.py:26
  262.8 1.0 collective-permute-done.20.refs_9_
  263.7 2.0 collective-permute-done.21.refs_10_
  266.4 6.6 %shard_map.144 = (f32[32,8,8,128]{3,2,1,0:T(8,128)}, f32[32,8,8,128]{3,2,1,0:T(8,128)}, f32[32,128]{1,0:T(8,128)}) custom-call(f32[2,32,128]{2,1,0:T(8,128)} %get-tuple-element.110.refs_0_, f32[32,128]{1,0:T(8,128)} %get-tuple-element.111.own_ref.refs_1_, s32[8,8,128]{2,1,0:T(8,128)} %fusion.7.inverse_ref.refs_2_, ...), custom_call_target="tpu_custom_call" | custom-call | tf_op jit(solution)/shard_map/pallas_call | solution.py:51
  273.0 1.0 shard_map.145
  274.0 25.0 %all_to_all.71.sums_ref = f32[256,1,128]{2,1,0:T(1,128)S(1)} all-to-all(f32[256,1,128]{2,1,0:T(1,128)S(1)} %shard_map.145), channel_id=1, replica_groups=mesh['sec'=2,'clu_0'=4,'clu_1'=2,'blk_0'=2,'blk_1'=8] {'sec','clu_0','cl..., dimensions={0} | all-to-all | bytes 262144 | tf_op jit(solution)/shard_map/all_to_all | solution.py:34
  299.0 3.0 %shard_map.146 = f32[32,8,8,128]{3,2,1,0:T(8,128)} custom-call(f32[256,1,128]{2,1,0:T(1,128)S(1)} %all_to_all.71.sums_ref, f32[32,8,8,128]{3,2,1,0:T(8,128)} %get-tuple-element.127.direction_ref, f32[32,8,8,128]{3,2,1,0:T(8,128)} %get-tuple-element.128.solution_ref), custom_call_target="tpu_custom_call" | custom-call | tf_op jit(solution)/shard_map/pallas_call | solution.py:51
  (112 shorter events, 10.0 us)
Async XLA Ops:
  0.0 28.6 %copy-start.17 = (f32[8,8]{1,0:T(8,128)S(1)}, f32[8,8]{1,0:T(8,128)}, u32[]{:S(2)}) copy-start(f32[8,8]{1,0:T(8,128)} %param.16) | copy-start | bytes 772
  0.0 28.6 %copy-start.20 = (s32[4096]{0:T(1024)S(1)}, s32[4096]{0:T(1024)}, u32[]{:S(2)}) copy-start(s32[4096]{0:T(1024)} %param.25) | copy-start | bytes 49156
  5.2 29.2 %all-to-all-start = ((f32[16,32,128]{2,1,0:T(8,128)}), f32[16,32,128]{2,1,0:T(8,128)S(1)}, u32[]{:S(2)}, u32[]{:S(2)}) async-start(f32[16,32,128]{2,1,0:T(8,128)} %get-tuple-element.67), calls=%async_computation | async-start | bytes 524288 | tf_op jit(solution)/shard_map/all_to_all | solution.py:34
  15.1 55.3 %collective-permute-start.4 = (f32[33,8,128]{2,1,0:T(8,128)S(1)}, f32[33,8,128]{2,1,0:T(8,128)S(1)}, u32[]{:S(2)}, u32[]{:S(2)}) collective-permute-start(f32[33,8,128]{2,1,0:T(8,128)S(1)} %get-tuple-element.73), channel_id=1, source_target_pairs={{0,16},{16,32},{32,48},{48,64},{64,80},{80,96},{96,112},{112,128},... | collective-permute-start | bytes 405512 | tf_op jit(solution)/shard_map/ppermute | solution.py:26
  19.3 68.7 %collective-permute-start.5 = (f32[32,8,128]{2,1,0:T(8,128)S(1)}, f32[32,8,128]{2,1,0:T(8,128)S(1)}, u32[]{:S(2)}, u32[]{:S(2)}) collective-permute-start(f32[32,8,128]{2,1,0:T(8,128)S(1)} %get-tuple-element.74), channel_id=1, source_target_pairs={{16,0},{32,16},{48,32},{64,48},{80,64},{96,80},{112,96},{128,112},... | collective-permute-start | bytes 393224 | tf_op jit(solution)/shard_map/ppermute | solution.py:26
  20.6 58.0 %collective-permute-start.6 = (f32[33,8,128]{2,1,0:T(8,128)S(1)}, f32[33,8,128]{2,1,0:T(8,128)S(1)}, u32[]{:S(2)}, u32[]{:S(2)}) collective-permute-start(f32[33,8,128]{2,1,0:T(8,128)S(1)} %get-tuple-element.75), channel_id=1, source_target_pairs={{0,1},{1,2},{2,3},{3,4},{4,5},{5,6},{6,7},{7,8},{8,9},{9,10},{10,1... | collective-permute-start | bytes 405512 | tf_op jit(solution)/shard_map/ppermute | solution.py:26
  24.0 64.1 %collective-permute-start.7 = (f32[32,8,128]{2,1,0:T(8,128)S(1)}, f32[32,8,128]{2,1,0:T(8,128)S(1)}, u32[]{:S(2)}, u32[]{:S(2)}) collective-permute-start(f32[32,8,128]{2,1,0:T(8,128)S(1)} %get-tuple-element.76), channel_id=1, source_target_pairs={{1,0},{2,1},{3,2},{4,3},{5,4},{6,5},{7,6},{8,7},{9,8},{10,9},{11,1... | collective-permute-start | bytes 393224 | tf_op jit(solution)/shard_map/ppermute | solution.py:26
  29.3 3.5 %copy-start.6 = (s32[4096]{0:T(1024)}, s32[4096]{0:T(1024)S(1)}, u32[]{:S(2)}) copy-start(s32[4096]{0:T(1024)S(1)} %get-tuple-element.135) | copy-start | bytes 49156
  32.2 1.2 copy-start.22
  32.2 1.2 copy-start.18
  32.2 1.2 copy-start.15
  32.2 1.2 copy-start.24
  32.2 2.1 copy-start.16
  32.2 4.6 %copy-start.23 = (s32[1,1,48]{2,1,0:T(1,128)S(1)}, s32[1,1,48]{2,1,0:T(1,128)}, u32[]{:S(2)}) copy-start(s32[1,1,48]{2,1,0:T(1,128)} %param.21) | copy-start | bytes 580
  32.2 5.8 %copy-start = (bf16[1,1,48,128,128]{4,3,2,1,0:T(8,128)(2,1)S(1)}, bf16[1,1,48,128,128]{4,3,2,1,0:T(8,128)(2,1)}, u32[]{:S(2)}) copy-start(bf16[1,1,48,128,128]{4,3,2,1,0:T(8,128)(2,1)} %param.20) | copy-start | bytes 4718596
  32.7 10.6 %copy-start.19 = (f32[8,8]{1,0:T(8,128)S(1)}, f32[8,8]{1,0:T(8,128)}, u32[]{:S(2)}) copy-start(f32[8,8]{1,0:T(8,128)} %param.15) | copy-start | bytes 772
  34.4 3.6 %collective-permute-start = (f32[16,32,128]{2,1,0:T(8,128)S(1)}, f32[16,32,128]{2,1,0:T(8,128)S(1)}, u32[]{:S(2)}, u32[]{:S(2)}) collective-permute-start(f32[16,32,128]{2,1,0:T(8,128)S(1)} %all-to-all-done.refs_4_), channel_id=1, source_target_pairs={{0,128},{128,0},{1,129},{129,1},{2,130},{130,2},{3,131},{131,3},{4... | collective-permute-start | bytes 786440 | tf_op jit(solution)/shard_map/ppermute | solution.py:30
  37.1 34.6 %copy-start.1 = (bf16[5,128,128]{2,1,0:T(8,128)(2,1)}, bf16[5,128,128]{2,1,0:T(8,128)(2,1)S(1)}, u32[]{:S(2)}) copy-start(bf16[5,128,128]{2,1,0:T(8,128)(2,1)S(1)} %bitcast_dynamic-update-slice_fusion.refs_5_.refs_6_.refs_20_) | copy-start | bytes 491524
  42.9 1.4 collective-permute-start.1
  45.0 13.8 %all-to-all-start.1 = ((f32[8,32,128]{2,1,0:T(8,128)}), f32[8,32,128]{2,1,0:T(8,128)S(1)}, u32[]{:S(2)}, u32[]{:S(2)}) async-start(f32[8,32,128]{2,1,0:T(8,128)} %add.66), calls=%async_computation.1 | async-start | bytes 262144 | tf_op jit(solution)/shard_map/all_to_all | solution.py:34
  59.4 11.0 %all-to-all-start.2 = ((bf16[8,32,128]{2,1,0:T(8,128)(2,1)}), bf16[8,32,128]{2,1,0:T(8,128)(2,1)S(1)}, u32[]{:S(2)}, u32[]{:S(2)}) async-start(bf16[8,32,128]{2,1,0:T(8,128)(2,1)} %shard_map.129), calls=%async_computation.2 | async-start | bytes 131072 | tf_op jit(solution)/shard_map/all_to_all | solution.py:34
  70.4 1.3 collective-permute-start.2
  70.4 18.5 %copy-start.2 = (f32[33,8,128]{2,1,0:T(8,128)}, f32[33,8,128]{2,1,0:T(8,128)S(1)}, u32[]{:S(2)}) copy-start(f32[33,8,128]{2,1,0:T(8,128)S(1)} %collective-permute-done.4.refs_0_.refs_10_.refs_14_) | copy-start | bytes 405508
  78.3 1.6 collective-permute-start.3
  78.6 10.3 %copy-start.3 = (f32[33,8,128]{2,1,0:T(8,128)}, f32[33,8,128]{2,1,0:T(8,128)S(1)}, u32[]{:S(2)}) copy-start(f32[33,8,128]{2,1,0:T(8,128)S(1)} %collective-permute-done.6.refs_2_.refs_12_.refs_16_) | copy-start | bytes 405508
  80.7 17.0 %all-to-all-start.3 = ((f32[16,32,128]{2,1,0:T(8,128)}), f32[16,32,128]{2,1,0:T(8,128)S(1)}, u32[]{:S(2)}, u32[]{:S(2)}) async-start(f32[16,32,128]{2,1,0:T(8,128)} %add.67), calls=%async_computation.3 | async-start | bytes 524288 | tf_op jit(solution)/shard_map/all_to_all | solution.py:34
  88.0 0.9 copy-start.4
  88.0 0.8 copy-start.5
  114.4 1.6 collective-permute-start.8
  132.1 1.3 collective-permute-start.9
  143.9 26.4 %copy-start.21 = (s32[1,1,128]{2,1,0:T(1,128)S(1)}, s32[1,1,128]{2,1,0:T(1,128)}, u32[]{:S(2)}) copy-start(s32[1,1,128]{2,1,0:T(1,128)} %param.24) | copy-start | bytes 1540
  154.2 1.3 collective-permute-start.10
  162.1 1.6 collective-permute-start.11
  164.5 34.0 %all-to-all-start.8 = ((f32[16,32,128]{2,1,0:T(8,128)}), f32[16,32,128]{2,1,0:T(8,128)S(1)}, u32[]{:S(2)}, u32[]{:S(2)}) async-start(f32[16,32,128]{2,1,0:T(8,128)} %add.69), calls=%async_computation.8 | async-start | bytes 524288 | tf_op jit(solution)/shard_map/all_to_all | solution.py:34
  173.2 11.6 %collective-permute-start.12 = (f32[32,8,128]{2,1,0:T(8,128)S(1)}, f32[32,8,128]{2,1,0:T(8,128)S(1)}, u32[]{:S(2)}, u32[]{:S(2)}) collective-permute-start(f32[32,8,128]{2,1,0:T(8,128)S(1)} %get-tuple-element.94), channel_id=1, source_target_pairs={{0,16},{16,32},{32,48},{48,64},{64,80},{80,96},{96,112},{112,128},... | collective-permute-start | bytes 393224 | tf_op jit(solution)/shard_map/ppermute | solution.py:26
  175.6 9.5 %collective-permute-start.13 = (f32[32,8,128]{2,1,0:T(8,128)S(1)}, f32[32,8,128]{2,1,0:T(8,128)S(1)}, u32[]{:S(2)}, u32[]{:S(2)}) collective-permute-start(f32[32,8,128]{2,1,0:T(8,128)S(1)} %get-tuple-element.95), channel_id=1, source_target_pairs={{16,0},{32,16},{48,32},{64,48},{80,64},{96,80},{112,96},{128,112},... | collective-permute-start | bytes 393224 | tf_op jit(solution)/shard_map/ppermute | solution.py:26
  176.9 9.1 %collective-permute-start.14 = (f32[32,8,128]{2,1,0:T(8,128)S(1)}, f32[32,8,128]{2,1,0:T(8,128)S(1)}, u32[]{:S(2)}, u32[]{:S(2)}) collective-permute-start(f32[32,8,128]{2,1,0:T(8,128)S(1)} %get-tuple-element.96), channel_id=1, source_target_pairs={{0,1},{1,2},{2,3},{3,4},{4,5},{5,6},{6,7},{7,8},{8,9},{9,10},{10,1... | collective-permute-start | bytes 393224 | tf_op jit(solution)/shard_map/ppermute | solution.py:26
  180.3 7.1 %collective-permute-start.15 = (f32[32,8,128]{2,1,0:T(8,128)S(1)}, f32[32,8,128]{2,1,0:T(8,128)S(1)}, u32[]{:S(2)}, u32[]{:S(2)}) collective-permute-start(f32[32,8,128]{2,1,0:T(8,128)S(1)} %get-tuple-element.97), channel_id=1, source_target_pairs={{1,0},{2,1},{3,2},{4,3},{5,4},{6,5},{7,6},{8,7},{9,8},{10,9},{11,1... | collective-permute-start | bytes 393224 | tf_op jit(solution)/shard_map/ppermute | solution.py:26
  184.9 2.5 copy-start.9
  185.1 2.3 copy-start.11
  185.9 1.4 copy-start.12
  187.4 0.6 copy-start.14
  216.2 4.8 %collective-permute-start.16 = (f32[16,40,128]{2,1,0:T(8,128)S(1)}, f32[16,40,128]{2,1,0:T(8,128)S(1)}, u32[]{:S(2)}, u32[]{:S(2)}) collective-permute-start(f32[16,40,128]{2,1,0:T(8,128)S(1)} %all_to_all.69.mine_ref.refs_6_), channel_id=1, source_target_pairs={{0,128},{128,0},{1,129},{129,1},{2,130},{130,2},{3,131},{131,3},{4... | collective-permute-start | bytes 983048 | tf_op jit(solution)/shard_map/ppermute | solution.py:30
  240.4 1.5 collective-permute-start.17
  242.6 30.4 %all-to-all-start.11 = ((f32[8,64,128]{2,1,0:T(8,128)}), f32[8,64,128]{2,1,0:T(8,128)S(1)}, u32[]{:S(2)}, u32[]{:S(2)}) async-start(f32[8,64,128]{2,1,0:T(8,128)} %add.72), calls=%async_computation.11 | async-start | bytes 524288 | tf_op jit(solution)/shard_map/all_to_all | solution.py:34
  248.1 14.6 %collective-permute-start.18 = (f32[32,8,128]{2,1,0:T(8,128)S(1)}, f32[32,8,128]{2,1,0:T(8,128)S(1)}, u32[]{:S(2)}, u32[]{:S(2)}) collective-permute-start(f32[32,8,128]{2,1,0:T(8,128)S(1)} %get-tuple-element.118), channel_id=1, source_target_pairs={{0,16},{16,32},{32,48},{48,64},{64,80},{80,96},{96,112},{112,128},... | collective-permute-start | bytes 393224 | tf_op jit(solution)/shard_map/ppermute | solution.py:26
  253.4 9.3 %collective-permute-start.19 = (f32[32,8,128]{2,1,0:T(8,128)S(1)}, f32[32,8,128]{2,1,0:T(8,128)S(1)}, u32[]{:S(2)}, u32[]{:S(2)}) collective-permute-start(f32[32,8,128]{2,1,0:T(8,128)S(1)} %get-tuple-element.119), channel_id=1, source_target_pairs={{16,0},{32,16},{48,32},{64,48},{80,64},{96,80},{112,96},{128,112},... | collective-permute-start | bytes 393224 | tf_op jit(solution)/shard_map/ppermute | solution.py:26
  254.7 9.0 %collective-permute-start.20 = (f32[32,8,128]{2,1,0:T(8,128)S(1)}, f32[32,8,128]{2,1,0:T(8,128)S(1)}, u32[]{:S(2)}, u32[]{:S(2)}) collective-permute-start(f32[32,8,128]{2,1,0:T(8,128)S(1)} %get-tuple-element.120), channel_id=1, source_target_pairs={{0,1},{1,2},{2,3},{3,4},{4,5},{5,6},{6,7},{7,8},{8,9},{9,10},{10,1... | collective-permute-start | bytes 393224 | tf_op jit(solution)/shard_map/ppermute | solution.py:26
  258.9 6.9 %collective-permute-start.21 = (f32[32,8,128]{2,1,0:T(8,128)S(1)}, f32[32,8,128]{2,1,0:T(8,128)S(1)}, u32[]{:S(2)}, u32[]{:S(2)}) collective-permute-start(f32[32,8,128]{2,1,0:T(8,128)S(1)} %get-tuple-element.121), channel_id=1, source_target_pairs={{1,0},{2,1},{3,2},{4,3},{5,4},{6,5},{7,6},{8,7},{9,8},{10,9},{11,1... | collective-permute-start | bytes 393224 | tf_op jit(solution)/shard_map/ppermute | solution.py:26
  262.7 3.0 %copy-start.7 = (f32[32,8,128]{2,1,0:T(8,128)}, f32[32,8,128]{2,1,0:T(8,128)S(1)}, u32[]{:S(2)}) copy-start(f32[32,8,128]{2,1,0:T(8,128)S(1)} %collective-permute-done.18.refs_7_) | copy-start | bytes 393220
  262.7 3.0 copy-start.8
  263.7 2.0 copy-start.10
  265.8 0.7 copy-start.13

commit v4 on v3

--- a/solution.py
+++ b/solution.py
@@ -114,11 +114,14 @@
     return (make((cases, width, lanes)),) * 2 + (make((cases, slabs, lanes)),) * 2
 
 
-def first_trace_kernel(field_ref, surface_ref, end_ref, out_ref, *edge_refs):
+def first_trace_kernel(field_ref, surface_ref, across_ref, along_ref, out_ref, *edge_refs):
     cases, slabs = field_ref.shape[:2]
     copies = out_ref.shape[0]
-    edge_refs[0][cases] = end_ref[0]
-    edge_refs[2][cases] = end_ref[1]
+    square = across_ref.shape
+    here = lax.broadcasted_iota(jnp.int32, square, 0) == lax.broadcasted_iota(jnp.int32, square, 1)
+    last_row = jnp.sum(jnp.where(here, across_ref[slabs - 1 :, :], 0.0), axis=1, keepdims=True)
+    edge_refs[0][cases] = jnp.broadcast_to(last_row, (square[1], 128))
+    edge_refs[2][cases] = jnp.broadcast_to(along_ref[:, square[1] - 1 :], (square[0], 128))
     local = jnp.broadcast_to(surface_ref[...], (8, 128))
     lane_index, block_index = local & 127, local >> 7
 
@@ -149,6 +152,28 @@
     return totals
 
 
+def selected_block(flat_ref, lanes_ref, blocks_ref, d, cases):
+    width = flat_ref.shape[1] // 128
+    wanted = jnp.broadcast_to(lanes_ref[pl.ds(d, 1), :], (128, 128))
+    chosen = jnp.where(row_iota((128, 128)) == wanted, 1.0, 0.0).astype(BF16)
+    chosen = jnp.concatenate([chosen] * width, axis=0)
+    block_index = jnp.broadcast_to(blocks_ref[pl.ds(d, 1), :], (cases, 128))
+    step = 256 // cases
+    total = jnp.zeros((cases, 128), F32)
+    for g in range(flat_ref.shape[0] // 256):
+        found = jnp.dot(
+            flat_ref[256 * g : 256 * g + 256, :], chosen, preferred_element_type=F32
+        ).reshape(step, cases, 128)
+        for j in range(step):
+            total = jnp.where(block_index == g * step + j, found[j], total)
+    return total
+
+
+def high_and_low(value):
+    high = value.astype(BF16)
+    return high, (value - high.astype(F32)).astype(BF16)
+
+
 def alpha_beta(sums_ref, cases):
     row = jnp.sum(sums_ref[...], axis=0)
     norm, curvature, crossed, squared = (row_to_column(row, i * cases, cases) for i in range(4))
@@ -160,11 +185,10 @@
 
 def forward_kernel(first, last, *refs):
     refs = list(refs)
-    pairs_ref, lanes_ref, blocks_ref, boundary_ref = refs[:4]
-    refs = refs[4:]
+    pairs_ref, lanes_ref, blocks_ref, *boundary_refs = refs[:5]
+    refs = refs[5:]
     if first:
-        mine_ref, other_ref, direction_ref, slots_ref, keep_ref, send_ref, low_ref = refs[:7]
-        rest = refs[7:]
+        mine_ref, other_ref, direction_ref, slots_ref, out_ref, low_ref, flat_ref = refs
         count = mine_ref.shape[0]
         direction_ref[:count] = mine_ref[...]
         direction_ref[count:] = other_ref[...]
@@ -172,11 +196,9 @@
         old_residual_ref, old_direction_ref, mine_ref, other_ref, sums_ref = refs[:5]
         steps_ref, refs = refs[5], refs[6:]
         if last:
-            keep_ref, send_ref, direction_ref, low_ref = refs[:4]
-            rest = refs[4:]
+            out_ref, direction_ref, low_ref, flat_ref = refs
         else:
-            residual_ref, direction_ref, slots_ref, keep_ref, send_ref, low_ref = refs[:6]
-            rest = refs[6:]
+            residual_ref, direction_ref, slots_ref, out_ref, low_ref, flat_ref = refs
         cases = old_direction_ref.shape[1]
         count = mine_ref.shape[0]
         alpha, beta = alpha_beta(sums_ref, cases)
@@ -193,33 +215,43 @@
                 direction_ref[b] = residual + beta * old_direction_ref[b]
     cases = direction_ref.shape[1]
     if not last:
-        place = pairs_ref[3, 0]
+        place = pairs_ref[5, 0]
         slots_ref[0] = direction_ref[place] if first else residual_ref[place]
         slots_ref[1] = direction_ref[place]
 
+    owners = direction_ref.shape[0]
+    half = owners // 2
+    for i in range(0, owners, 8):
+        value = direction_ref[i : i + 8].reshape(8 * cases, 128)
+        if last:
+            high, low = high_and_low(value)
+            flat_ref[i * cases : (i + 8) * cases, :128] = high
+            flat_ref[i * cases : (i + 8) * cases, 128:] = low
+        else:
+            flat_ref[i * cases : (i + 8) * cases, :] = value.astype(BF16)
+
     def step(d, carry):
-        totals = permuted_block(direction_ref, lanes_ref, blocks_ref, d)
-        value = jnp.concatenate(totals, axis=0)
-        low = value.astype(BF16)
-        if last:
-            left = value - low.astype(F32)
-            second = left.astype(BF16)
-            low_ref[d] = jnp.concatenate([low, second], axis=0)
-        else:
-            low_ref[d] = low
+        one = permuted_block(direction_ref, lanes_ref, blocks_ref, d)
+        two = selected_block(flat_ref, lanes_ref, blocks_ref, half + d, cases)
+        for at, value in ((d, jnp.concatenate(one, axis=0)), (half + d, two)):
+            if last:
+                low_ref[at] = jnp.concatenate(high_and_low(value), axis=0)
+            else:
+                low_ref[at] = value.astype(BF16)
         return carry
 
-    lax.fori_loop(0, direction_ref.shape[0], step, 0, unroll=4)
-    half_count = keep_ref.shape[0]
-    sums_scratch = rest[0]
-    sums_scratch[...] = jnp.zeros(sums_scratch.shape, F32)
-    live = pairs_ref[2, 0]
-    for p in range(boundary_ref.shape[0]):
-        product = jnp.dot(low_ref[pairs_ref[0, p]], boundary_ref[p], preferred_element_type=F32)
-        product = jnp.where(p < live, product, 0.0)
-        sums_scratch[pairs_ref[1, p]] += product
-    keep_ref[...] = sums_scratch[:half_count]
-    send_ref[...] = sums_scratch[half_count:]
+    lax.fori_loop(0, half, step, 0, unroll=2)
+    out_ref[...] = jnp.zeros(out_ref.shape, F32)
+    for p, block in pair_blocks(boundary_refs):
+        product = jnp.dot(low_ref[pairs_ref[0, p]], block, preferred_element_type=F32)
+        out_ref[pairs_ref[1, p]] += jnp.where(pairs_ref[3, p] > 0, product, 0.0)
+
+
+def pair_blocks(refs):
+    count = refs[0].shape[0]
+    for i, ref in enumerate(refs):
+        for p in range(count):
+            yield i * count + p, ref[p]
 
 
 def backward_kernel(
@@ -227,10 +259,10 @@
     lanes_ref,
     blocks_ref,
     boundary_ref,
+    boundary_other_ref,
     mine_ref,
     other_ref,
-    keep_ref,
-    send_ref,
+    out_ref,
     low_ref,
     rows_scratch,
 ):
@@ -238,26 +270,21 @@
     low_ref[:half_count] = mine_ref[...]
     low_ref[half_count:] = other_ref[...]
     rows_scratch[...] = jnp.zeros(rows_scratch.shape, F32)
-    live = pairs_ref[2, 0]
-    for p in range(boundary_ref.shape[0]):
+    for p, block in pair_blocks((boundary_ref, boundary_other_ref)):
         product = lax.dot_general(
-            low_ref[pairs_ref[1, p]],
-            boundary_ref[p],
+            low_ref[pairs_ref[2, p]],
+            block,
             (((1,), (1,)), ((), ())),
             preferred_element_type=F32,
         )
-        product = jnp.where(p < live, product, 0.0)
-        rows_scratch[pairs_ref[0, p]] += product
-    count = keep_ref.shape[0]
-    for at, out_ref in ((0, keep_ref), (count, send_ref)):
-
-        def step(d, carry, at=at, out_ref=out_ref):
-            totals = permuted_block(rows_scratch, lanes_ref, blocks_ref, at + d)
-            for g, total in enumerate(totals):
-                out_ref[d, 8 * g : 8 * g + 8, :] = total
-            return carry
-
-        lax.fori_loop(0, count, step, 0, unroll=4)
+        rows_scratch[pairs_ref[0, p]] += jnp.where(pairs_ref[4, p] > 0, product, 0.0)
+
+    def step(d, carry):
+        for g, total in enumerate(permuted_block(rows_scratch, lanes_ref, blocks_ref, d)):
+            out_ref[d, 8 * g : 8 * g + 8, :] = total
+        return carry
+
+    lax.fori_loop(0, out_ref.shape[0], step, 0, unroll=4)
 
 
 def low_kernel(pieces_ref, out_ref):
@@ -510,12 +537,10 @@
         kept((cases + 1, slabs, lanes)),
         kept((cases, slabs, lanes)),
     ]
-    ends = jnp.stack([across_weight[-1, :], along_weight[:, -1]])
-    ends = jnp.broadcast_to(ends[:, :, None], (2, width, lanes))
     trace, *edges = kernel(
         first_trace_kernel,
-        (kept((blk_count, cases, lanes)), *first_edges),
-        (right_side, surface, ends),
+        (like((blk_count, cases, lanes)), *first_edges),
+        (right_side, surface, across_weight, along_weight),
     )
     mine = exchanged(trace, BLK)
     other = partner(mine)
@@ -556,15 +581,23 @@
 
     half_columns = clu_count
     slots_shape = (owners, cases, lanes)
+    live = jnp.arange(rows_local.shape[0], dtype=jnp.int32) < live_local
+    listed = jnp.stack([rows_local, columns_local, live.astype(jnp.int32)])
+    blocks_other = partner(blocks_local)
+    listed_other = partner(listed)
+    listed = jnp.concatenate([listed, listed_other], axis=1)
+    in_half = listed[1] // half_columns == half
     pairs = jnp.stack(
         [
-            rows_local,
-            columns_local ^ (half * half_columns),
-            jnp.broadcast_to(live_local, rows_local.shape),
-            jnp.broadcast_to(place, rows_local.shape),
+            listed[0],
+            listed[1] % half_columns,
+            listed[1] ^ (half * half_columns),
+            jnp.where(in_half, listed[2], 0),
+            listed[2],
+            jnp.broadcast_to(place, listed[0].shape),
         ]
     )
-    forward_inputs = (pairs, slot_lanes, slot_blocks, near(blocks_local))
+    forward_inputs = (pairs, slot_lanes, slot_blocks, near(blocks_local), near(blocks_other))
 
     def weights_of(halo):
         across_edge = halo[0][cases, :, 0][None, :]
@@ -600,38 +633,37 @@
         deep = 2 * cases if last else cases
         scratch = [
             pltpu.VMEM((slot_count // lanes, deep, lanes), BF16),
-            pltpu.VMEM((2 * half_columns, deep, lanes), F32),
+            pltpu.VMEM((owners * cases, 2 * lanes if last else lanes), BF16),
         ]
-        halves = (kept((half_columns, deep, lanes)),) * 2
+        column_sums = like((half_columns, deep, lanes))
         if not first:
             inputs = (*forward_inputs, slot_residual, slot_direction)
-            inputs += (near(mine), near(other), near(sums))
+            inputs += (mine, other, near(sums))
             if last:
-                steps, keep, send = kernel(
+                steps, pieces = kernel(
                     functools.partial(forward_kernel, False, True),
-                    (steps_shape, *halves),
+                    (steps_shape, column_sums),
                     inputs,
                     [pltpu.VMEM(slots_shape, F32)] + scratch,
                     1,
                 )
             else:
-                steps, slot_residual, slot_direction, own_slots, keep, send = kernel(
+                steps, slot_residual, slot_direction, own_slots, pieces = kernel(
                     functools.partial(forward_kernel, False, False),
-                    (steps_shape, *(like(slots_shape),) * 2, own_slots_shape, *halves),
+                    (steps_shape, *(like(slots_shape),) * 2, own_slots_shape, column_sums),
                     inputs,
                     scratch,
                     1,
                 )
         if first:
-            slot_direction, own_slots, keep, send = kernel(
+            slot_direction, own_slots, pieces = kernel(
                 functools.partial(forward_kernel, True, False),
-                (like(slots_shape), own_slots_shape, *halves),
+                (like(slots_shape), own_slots_shape, column_sums),
                 (*forward_inputs, near(mine), near(other)),
                 scratch,
                 1,
             )
             slot_residual = slot_direction
-        pieces = keep + partner(send)
         column_pieces = exchanged(pieces, CLU)
 
         if first:
@@ -684,17 +716,18 @@
                 [pltpu.VMEM((cases, lanes), F32)],
             )
 
-        z_low = kernel(low_kernel, kept((clu_count, cases, lanes), BF16), (near(column_pieces),))
+        z_low = kernel(low_kernel, like((clu_count, cases, lanes), BF16), (near(column_pieces),))
         low_mine = exchanged(z_low, CLU)
         low_other = partner(low_mine)
-        keep, send = kernel(
+        row_pieces = kernel(
             backward_kernel,
-            (kept((blk_count, cases, lanes)),) * 2,
+            like((blk_count, cases, lanes)),
             (
                 pairs,
                 dof_lanes,
                 dof_blocks,
                 near(blocks_local),
+                near(blocks_other),
                 near(low_mine),
                 near(low_other),
             ),
@@ -704,11 +737,10 @@
             ],
             1,
         )
-        row_pieces = keep + partner(send)
         arrived = exchanged(row_pieces, BLK)
         payload, own = kernel(
             own_kernel,
-            (kept((blk_count, cases + 8, lanes)), like((cases, lanes))),
+            (like((blk_count, cases + 8, lanes)), like((cases, lanes))),
             (near(arrived), image_trace, dots, own_slots),
         )
         mine = exchanged(payload, BLK)
@@ -716,9 +748,7 @@
         halo_image = sent(edges)
         other = partner(mine)
         row = kernel(
-            functools.partial(range_sum_kernel, cases),
-            kept((clu_count, 1, lanes)),
-            (near(mine), near(other)),
+            functools.partial(range_sum_kernel, cases), like((clu_count, 1, lanes)), (mine, other)
         )
         sums = exchanged(row, CLU)
 

time: 306 us -> 320 us (1.046)
  local copies, waits for them, and re-layouts: 5.68 us -> 17.1 us
  waiting for transfers between devices: 38 us -> 28.2 us
  other arithmetic: 6.73 us -> 13.5 us
    unnamed x58 -> x60, local copies, waits for them, and re-layouts: 1.66 us -> 11 us
    ppermute x10 -> x7, waiting for transfers between devices: 12.8 us -> 4.14 us  [partner(): return lax.ppermute(value, 'sec', [(0, 1), (1, 0)])]
    another operation x3 -> x2, other arithmetic: 2.98 us -> 6.53 us
    ppermute x10 -> x7, starting transfers between devices: 6.9 us -> 4.6 us  [partner(): return lax.ppermute(value, 'sec', [(0, 1), (1, 0)])]
  transfers between devices with their start and end apart: 28 -> 25, of which waited for: 18 -> 11; matrix products, arithmetic and copies ran while one was open for 3% -> 9% of each run, Pallas kernels for 13% -> 13%
where the time goes in v4:
time: 320 us; the launch traced here: 315 us
  blocking collectives  102 us (32%)
  starting transfers between devices  81 us (25%)
  Pallas kernels  70.1 us (22%)
  waiting for transfers between devices  28.2 us (9%)
  local copies, waits for them, and re-layouts  17.1 us (5%)
  other arithmetic  13.5 us (4%)
    all_to_all x7, blocking collectives, exchanged(): return lax.all_to_all(pieces, axes, split_axis=0, concat_axis=0, tiled=True)  102 us
    pallas_call x20, Pallas kernels, kernel(): pl.pallas_call(body, out_shape=outs, in_specs=[SMEM] * scalars + [pl.Bloc...  70.1 us
    ppermute x12, starting transfers between devices, passed_along(): return lax.ppermute(value, axis, pairs)  40.5 us
    all_to_all x6, starting transfers between devices, exchanged(): return lax.all_to_all(pieces, axes, split_axis=0, concat_axis=0, tiled=True)  36 us
    all_to_all x6, waiting for transfers between devices, exchanged(): return lax.all_to_all(pieces, axes, split_axis=0, concat_axis=0, tiled=True)  18.6 us
    unnamed x60, local copies, waits for them, and re-layouts  11 us
  transfers between devices with their start and end apart: 25, of which 11 were waited for; matrix products, arithmetic and copies ran while one was open for 9% of the time, Pallas kernels for 13%

profile of v4, /device:TPU:8, one launch (start us, length us, event | category | flops | bytes accessed | tf_op | source)
XLA Modules:
  0.0 314.9 jit_solution(17662192202291674975)
XLA Ops:
  0.8 1.3 pad_add_fusion
  2.1 3.0 shard_map.127
  5.0 9.9 %all-to-all-start = ((f32[16,32,128]{2,1,0:T(8,128)}), f32[16,32,128]{2,1,0:T(8,128)S(1)}, u32[]{:S(2)}, u32[]{:S(2)}) async-start(f32[16,32,128]{2,1,0:T(8,128)} %get-tuple-element.60), calls=%async_computation | async-start | bytes 524288 | tf_op jit(solution)/shard_map/all_to_all | solution.py:34
  15.0 1.3 collective-permute-start.5
  16.3 4.6 %collective-permute-start.7 = (f32[32,8,128]{2,1,0:T(8,128)}, f32[32,8,128]{2,1,0:T(8,128)}, u32[]{:S(2)}, u32[]{:S(2)}) collective-permute-start(f32[32,8,128]{2,1,0:T(8,128)} %get-tuple-element.66), channel_id=1, source_target_pairs={{1,0},{2,1},{3,2},{4,3},{5,4},{6,5},{7,6},{8,7},{9,8},{10,9},{11,1... | collective-permute-start | bytes 393224 | tf_op jit(solution)/shard_map/ppermute | solution.py:26
  20.9 6.1 %collective-permute-start.4 = (f32[33,8,128]{2,1,0:T(8,128)}, f32[33,8,128]{2,1,0:T(8,128)}, u32[]{:S(2)}, u32[]{:S(2)}) collective-permute-start(f32[33,8,128]{2,1,0:T(8,128)} %get-tuple-element.63), channel_id=1, source_target_pairs={{0,16},{16,32},{32,48},{48,64},{64,80},{80,96},{96,112},{112,128},... | collective-permute-start | bytes 405512 | tf_op jit(solution)/shard_map/ppermute | solution.py:26
  27.0 1.5 collective-permute-start.1
  30.2 1.5 copy.16
  31.7 1.4 bitcast_dynamic-update-slice_fusion.4
  33.1 1.4 bitcast_dynamic-update-slice_fusion.3
  34.4 1.3 add_select_fusion.2
  35.8 5.3 %select_convert_fusion.1 = (bf16[4096,128]{1,0:T(8,128)(2,1)S(1)}, bf16[4096,128]{1,0:T(8,128)(2,1)S(1)}) fusion(s32[4096]{0:T(1024)} %get-tuple-element.130, s32[4096]{0:T(1024)S(1)} %get-tuple-element.119, s32[4096]{0:T(1024)} %get-tuple-element.129), kind=kLoop, calls=%fused_computation.5 | loop fusion | flops 2621440 | bytes 2146304 | tf_op jit(solution)/shard_map/convert
  44.6 1.5 copy.17
  46.6 1.4 bitcast_dynamic-update-slice_fusion.refs_5_.refs_6_.refs_20_
  51.2 1.9 collective-permute-start.6
  53.1 5.1 %shard_map.128 = (f32[32,32,128]{2,1,0:T(8,128)}, f32[2,32,128]{2,1,0:T(8,128)}, f32[8,32,128]{2,1,0:T(8,128)}) custom-call(s32[6,96]{1,0:T(8,128)S(1)} %stack.49.refs_0_.pairs_ref, s32[32,128]{1,0:T(8,128)} %get-tuple-element.120.refs_1_, s32[32,128]{1,0:T(8,128)} %bitcast.62, bf16[48,128,128]{2,1,0:T(8,128)(2,1)S(1)} %bitcast.57, ...), custom_call_target="tpu_custom_call" | custom-call | tf_op jit(solution)/shard_map/pallas_call | solution.py:51
  58.2 7.0 %all-to-all-start.1 = ((f32[8,32,128]{2,1,0:T(8,128)}), f32[8,32,128]{2,1,0:T(8,128)S(1)}, u32[]{:S(2)}, u32[]{:S(2)}) async-start(f32[8,32,128]{2,1,0:T(8,128)} %get-tuple-element.62), calls=%async_computation.1 | async-start | bytes 262144 | tf_op jit(solution)/shard_map/all_to_all | solution.py:34
  66.0 7.1 %all-to-all-done.1.pieces_ref = f32[8,32,128]{2,1,0:T(8,128)S(1)} async-done(((f32[8,32,128]{2,1,0:T(8,128)}), f32[8,32,128]{2,1,0:T(8,128)S(1)}, u32[]{:S(2)}, u32[]{:S(2)}) %all-to-all-start.1) | async-done | bytes 131104 | tf_op jit(solution)/shard_map/all_to_all | solution.py:34
  73.8 3.4 %all-to-all-start.2 = ((bf16[8,32,128]{2,1,0:T(8,128)(2,1)}), bf16[8,32,128]{2,1,0:T(8,128)(2,1)S(1)}, u32[]{:S(2)}, u32[]{:S(2)}) async-start(bf16[8,32,128]{2,1,0:T(8,128)(2,1)} %shard_map.129), calls=%async_computation.2 | async-start | bytes 131072 | tf_op jit(solution)/shard_map/all_to_all | solution.py:34
  77.7 7.1 %all-to-all-done.2.mine_ref = bf16[8,32,128]{2,1,0:T(8,128)(2,1)S(1)} async-done(((bf16[8,32,128]{2,1,0:T(8,128)(2,1)}), bf16[8,32,128]{2,1,0:T(8,128)(2,1)S(1)}, u32[]{:S(2)}, u32[]{:S(2)}) %all-to-all-start.2) | async-done | bytes 65568 | tf_op jit(solution)/shard_map/all_to_all | solution.py:34
  84.8 1.3 constant_dynamic-update-slice_fusion.3
  86.8 5.7 %shard_map.130 = f32[16,32,128]{2,1,0:T(8,128)} custom-call(s32[6,96]{1,0:T(8,128)S(1)} %stack.49.refs_0_.pairs_ref, s32[32,128]{1,0:T(8,128)} %get-tuple-element.116.lanes_ref, s32[32,128]{1,0:T(8,128)} %get-tuple-element.115.blocks_ref, bf16[48,128,128]{2,1,0:T(8,128)(2,1)S(1)} %bitcast.58, ...), custom_call_target="tpu_custom_call" | custom-call | tf_op jit(solution)/shard_map/pallas_call | solution.py:51
  92.5 6.9 %all-to-all-start.3 = ((f32[16,32,128]{2,1,0:T(8,128)}), f32[16,32,128]{2,1,0:T(8,128)S(1)}, u32[]{:S(2)}, u32[]{:S(2)}) async-start(f32[16,32,128]{2,1,0:T(8,128)} %shard_map.130), calls=%async_computation.3 | async-start | bytes 524288 | tf_op jit(solution)/shard_map/all_to_all | solution.py:34
  100.4 4.5 %shard_map.131 = (f32[32,8,8,128]{3,2,1,0:T(8,128)}, f32[32,128]{1,0:T(8,128)}, f32[32,128]{1,0:T(8,128)}, f32[32,8,128]{2,1,0:T(8,128)}, f32[32,8,128]{2,1,0:T(...) custom-call(f32[32,8,8,128]{3,2,1,0:T(8,128)} %refs_5_.1, ...), custom_call_target="tpu_custom_call" | custom-call | tf_op jit(solution)/shard_map/pallas_call | solution.py:51
  104.9 4.4 %all-to-all-done.3.arrived_ref = f32[16,32,128]{2,1,0:T(8,128)S(1)} async-done(((f32[16,32,128]{2,1,0:T(8,128)}), f32[16,32,128]{2,1,0:T(8,128)S(1)}, u32[]{:S(2)}, u32[]{:S(2)}) %all-to-all-start.3) | async-done | bytes 262176 | tf_op jit(solution)/shard_map/all_to_all | solution.py:34
  109.3 1.7 shard_map.132
  111.0 15.9 %all_to_all.65.mine_ref.refs_7_ = f32[16,40,128]{2,1,0:T(8,128)S(1)} all-to-all(f32[16,40,128]{2,1,0:T(8,128)} %get-tuple-element.70), channel_id=1, replica_groups=mesh['sec'=2,'clu_0'=4,'clu_1'=2,'blk_0'=2,'blk_1'=8] {'blk_0','blk_1'}, dimensions={0} | all-to-all | bytes 655360 | tf_op jit(solution)/shard_map/all_to_all | solution.py:34
  127.0 1.6 collective-permute-done.8.other_ref.refs_8_
  129.4 1.7 shard_map.133
  131.0 10.8 %all_to_all.66.refs_9_ = f32[8,1,128]{2,1,0:T(1,128)S(1)} all-to-all(f32[8,1,128]{2,1,0:T(1,128)} %shard_map.133), channel_id=1, replica_groups=mesh['sec'=2,'clu_0'=4,'clu_1'=2,'blk_0'=2,'blk_1'=8] {'clu_0','clu_1'}, dimensions={0} | all-to-all | bytes 8192 | tf_op jit(solution)/shard_map/all_to_all | solution.py:34
  141.9 6.0 %shard_map.134 = (f32[2,32,128]{2,1,0:T(8,128)}, f32[32,32,128]{2,1,0:T(8,128)}, f32[32,32,128]{2,1,0:T(8,128)}, f32[2,32,128]{2,1,0:T(8,128)}, f32[8,32,128]{2,1,0:T(8,128)}) custom-call(s32[6,96]{1,0:T(8,128)S(1)} %stack.49.refs_0_.pairs_ref, s32[32,128]{1,0:T(8,128)} %get-tuple-element.120.refs_1_, s32[32,128]{1,0:T(8,128)} %bitcast.63, ...), custom_call_target="tpu_custom_call" | custom-call | tf_op jit(solution)/shard_map/pallas_call | solution.py:51
  147.8 11.2 %all_to_all.67.pieces_ref = f32[8,32,128]{2,1,0:T(8,128)S(1)} all-to-all(f32[8,32,128]{2,1,0:T(8,128)} %get-tuple-element.73), channel_id=1, replica_groups=mesh['sec'=2,'clu_0'=4,'clu_1'=2,'blk_0'=2,'blk_1'=8] {'clu_0','clu_1'}, dimensions={0} | all-to-all | bytes 262144 | tf_op jit(solution)/shard_map/all_to_all | solution.py:34
  159.7 11.0 %all_to_all.68.mine_ref = bf16[8,32,128]{2,1,0:T(8,128)(2,1)S(1)} all-to-all(bf16[8,32,128]{2,1,0:T(8,128)(2,1)} %shard_map.135), channel_id=1, replica_groups=mesh['sec'=2,'clu_0'=4,'clu_1'=2,'blk_0'=2,'blk_1'=8] {'clu_0','clu_1'}, dimensions={0} | all-to-all | bytes 131072 | tf_op jit(solution)/shard_map/all_to_all | solution.py:34
  170.7 1.3 collective-permute-done.9.other_ref
  171.9 5.7 %shard_map.136 = f32[16,32,128]{2,1,0:T(8,128)} custom-call(s32[6,96]{1,0:T(8,128)S(1)} %stack.49.refs_0_.pairs_ref, s32[32,128]{1,0:T(8,128)} %get-tuple-element.116.lanes_ref, s32[32,128]{1,0:T(8,128)} %get-tuple-element.115.blocks_ref, bf16[48,128,128]{2,1,0:T(8,128)(2,1)S(1)} %bitcast.60, ...), custom_call_target="tpu_custom_call" | custom-call | tf_op jit(solution)/shard_map/pallas_call | solution.py:51
  177.6 5.4 %all-to-all-start.8 = ((f32[16,32,128]{2,1,0:T(8,128)}), f32[16,32,128]{2,1,0:T(8,128)S(1)}, u32[]{:S(2)}, u32[]{:S(2)}) async-start(f32[16,32,128]{2,1,0:T(8,128)} %shard_map.136), calls=%async_computation.8 | async-start | bytes 524288 | tf_op jit(solution)/shard_map/all_to_all | solution.py:34
  183.1 0.8 fusion.7.inverse_ref.refs_2_
  183.9 2.0 shard_map.137
  186.0 2.7 collective-permute-start.10
  188.7 1.3 collective-permute-start.11
  190.0 3.4 %collective-permute-start.12 = (f32[32,8,128]{2,1,0:T(8,128)S(1)}, f32[32,8,128]{2,1,0:T(8,128)S(1)}, u32[]{:S(2)}, u32[]{:S(2)}) collective-permute-start(f32[32,8,128]{2,1,0:T(8,128)S(1)} %get-tuple-element.83), channel_id=1, source_target_pairs={{0,1},{1,2},{2,3},{3,4},{4,5},{5,6},{6,7},{7,8},{8,9},{9,10},{10,1... | collective-permute-start | bytes 393224 | tf_op jit(solution)/shard_map/ppermute | solution.py:26
  193.4 4.6 %collective-permute-start.13 = (f32[32,8,128]{2,1,0:T(8,128)S(1)}, f32[32,8,128]{2,1,0:T(8,128)S(1)}, u32[]{:S(2)}, u32[]{:S(2)}) collective-permute-start(f32[32,8,128]{2,1,0:T(8,128)S(1)} %get-tuple-element.84), channel_id=1, source_target_pairs={{1,0},{2,1},{3,2},{4,3},{5,4},{6,5},{7,6},{8,7},{9,8},{10,9},{11,1... | collective-permute-start | bytes 393224 | tf_op jit(solution)/shard_map/ppermute | solution.py:26
  199.0 1.5 collective-permute-done.13.refs_9_
  201.1 5.6 %shard_map.138 = (f32[32,8,8,128]{3,2,1,0:T(8,128)}, f32[32,8,8,128]{3,2,1,0:T(8,128)}, f32[32,8,8,128]{3,2,1,0:T(8,128)}, f32[32,8,128]{2,1,0:T(8,128)}, f32[32...) custom-call(f32[2,32,128]{2,1,0:T(8,128)} %get-tuple-element.74.refs, ...), custom_call_target="tpu_custom_call" | custom-call | tf_op jit(solution)/shard_map/pallas_call | solution.py:51
  206.7 4.9 %shard_map.139 = (f32[32,8,8,128]{3,2,1,0:T(8,128)}, f32[32,128]{1,0:T(8,128)}, f32[32,128]{1,0:T(8,128)}, f32[32,8,128]{2,1,0:T(8,128)}, f32[32,8,128]{2,1,0:T(...) custom-call(f32[32,8,8,128]{3,2,1,0:T(8,128)} %get-tuple-element.85.direction_ref.refs_5_, ...), custom_call_target="tpu_custom_call" | custom-call | tf_op jit(solution)/shard_map/pallas_call | solution.py:51
  211.6 1.8 shard_map.140
  213.4 16.9 %all_to_all.69.mine_ref.refs_7_ = f32[16,40,128]{2,1,0:T(8,128)S(1)} all-to-all(f32[16,40,128]{2,1,0:T(8,128)} %get-tuple-element.94), channel_id=1, replica_groups=mesh['sec'=2,'clu_0'=4,'clu_1'=2,'blk_0'=2,'blk_1'=8] {'blk_0','blk_1'}, dimensions={0} | all-to-all | bytes 655360 | tf_op jit(solution)/shard_map/all_to_all | solution.py:34
  230.3 3.1 collective-permute-start.14
  233.4 1.3 collective-permute-done.14.other_ref.refs_8_
  235.4 1.7 shard_map.141
  237.0 11.6 %all_to_all.70.refs_9_ = f32[8,1,128]{2,1,0:T(1,128)S(1)} all-to-all(f32[8,1,128]{2,1,0:T(1,128)} %shard_map.141), channel_id=1, replica_groups=mesh['sec'=2,'clu_0'=4,'clu_1'=2,'blk_0'=2,'blk_1'=8] {'clu_0','clu_1'}, dimensions={0} | all-to-all | bytes 8192 | tf_op jit(solution)/shard_map/all_to_all | solution.py:34
  248.7 6.9 %shard_map.142 = (f32[2,32,128]{2,1,0:T(8,128)}, f32[8,64,128]{2,1,0:T(8,128)}) custom-call(s32[6,96]{1,0:T(8,128)S(1)} %stack.49.refs_0_.pairs_ref, s32[32,128]{1,0:T(8,128)} %get-tuple-element.120.refs_1_, s32[32,128]{1,0:T(8,128)} %bitcast.64, bf16[48,128,128]{2,1,0:T(8,128)(2,1)S(1)} %bitcast.61, ...), custom_call_target="tpu_custom_call" | custom-call | tf_op jit(solution)/shard_map/pallas_call | solution.py:51
  255.6 3.4 %all-to-all-start.11 = ((f32[8,64,128]{2,1,0:T(8,128)}), f32[8,64,128]{2,1,0:T(8,128)S(1)}, u32[]{:S(2)}, u32[]{:S(2)}) async-start(f32[8,64,128]{2,1,0:T(8,128)} %get-tuple-element.95), calls=%async_computation.11 | async-start | bytes 524288 | tf_op jit(solution)/shard_map/all_to_all | solution.py:34
  259.0 2.0 shard_map.143
  261.0 5.3 %collective-permute-start.15 = (f32[32,8,128]{2,1,0:T(8,128)S(1)}, f32[32,8,128]{2,1,0:T(8,128)S(1)}, u32[]{:S(2)}, u32[]{:S(2)}) collective-permute-start(f32[32,8,128]{2,1,0:T(8,128)S(1)} %get-tuple-element.104), channel_id=1, source_target_pairs={{0,16},{16,32},{32,48},{48,64},{64,80},{80,96},{96,112},{112,128},... | collective-permute-start | bytes 393224 | tf_op jit(solution)/shard_map/ppermute | solution.py:26
  266.4 1.3 collective-permute-start.16
  267.7 4.1 %collective-permute-start.17 = (f32[32,8,128]{2,1,0:T(8,128)S(1)}, f32[32,8,128]{2,1,0:T(8,128)S(1)}, u32[]{:S(2)}, u32[]{:S(2)}) collective-permute-start(f32[32,8,128]{2,1,0:T(8,128)S(1)} %get-tuple-element.106), channel_id=1, source_target_pairs={{0,1},{1,2},{2,3},{3,4},{4,5},{5,6},{6,7},{7,8},{8,9},{9,10},{10,1... | collective-permute-start | bytes 393224 | tf_op jit(solution)/shard_map/ppermute | solution.py:26
  271.8 3.8 %collective-permute-start.18 = (f32[32,8,128]{2,1,0:T(8,128)S(1)}, f32[32,8,128]{2,1,0:T(8,128)S(1)}, u32[]{:S(2)}, u32[]{:S(2)}) collective-permute-start(f32[32,8,128]{2,1,0:T(8,128)S(1)} %get-tuple-element.107), channel_id=1, source_target_pairs={{1,0},{2,1},{3,2},{4,3},{5,4},{6,5},{7,6},{8,7},{9,8},{10,9},{11,1... | collective-permute-start | bytes 393224 | tf_op jit(solution)/shard_map/ppermute | solution.py:26
  275.7 1.0 collective-permute-done.17.refs_9_
  276.6 2.0 collective-permute-done.18.refs_10_
  279.3 6.6 %shard_map.144 = (f32[32,8,8,128]{3,2,1,0:T(8,128)}, f32[32,8,8,128]{3,2,1,0:T(8,128)}, f32[32,128]{1,0:T(8,128)}) custom-call(f32[2,32,128]{2,1,0:T(8,128)} %get-tuple-element.96.refs_0_, f32[32,128]{1,0:T(8,128)} %get-tuple-element.97.own_ref.refs_1_, s32[8,8,128]{2,1,0:T(8,128)} %fusion.7.inverse_ref.refs_2_, ...), custom_call_target="tpu_custom_call" | custom-call | tf_op jit(solution)/shard_map/pallas_call | solution.py:51
  285.9 1.0 shard_map.145
  286.9 25.0 %all_to_all.71.sums_ref = f32[256,1,128]{2,1,0:T(1,128)S(1)} all-to-all(f32[256,1,128]{2,1,0:T(1,128)S(1)} %shard_map.145), channel_id=1, replica_groups=mesh['sec'=2,'clu_0'=4,'clu_1'=2,'blk_0'=2,'blk_1'=8] {'sec','clu_0','cl..., dimensions={0} | all-to-all | bytes 262144 | tf_op jit(solution)/shard_map/all_to_all | solution.py:34
  311.9 3.0 shard_map.146
  (101 shorter events, 17.3 us)
Async XLA Ops:
  0.0 28.4 %copy-start.16 = (f32[8,8]{1,0:T(8,128)S(1)}, f32[8,8]{1,0:T(8,128)}, u32[]{:S(2)}) copy-start(f32[8,8]{1,0:T(8,128)} %along_ref.1) | copy-start | bytes 772
  0.0 27.0 %copy-start = (bf16[1,1,48,128,128]{4,3,2,1,0:T(8,128)(2,1)S(1)}, bf16[1,1,48,128,128]{4,3,2,1,0:T(8,128)(2,1)}, u32[]{:S(2)}) copy-start(bf16[1,1,48,128,128]{4,3,2,1,0:T(8,128)(2,1)} %param.20) | copy-start | bytes 4718596
  0.0 29.6 %copy-start.21 = (f32[8,8]{1,0:T(8,128)S(1)}, f32[8,8]{1,0:T(8,128)}, u32[]{:S(2)}) copy-start(f32[8,8]{1,0:T(8,128)} %param.14) | copy-start | bytes 772
  0.8 1.3 copy-start.23
  2.1 46.5 %collective-permute-start = (s32[3,48]{1,0:T(4,128)}, s32[3,48]{1,0:T(4,128)}, u32[]{:S(2)}, u32[]{:S(2)}) collective-permute-start(s32[3,48]{1,0:T(4,128)} %pad_add_fusion), channel_id=1, source_target_pairs={{0,128},{128,0},{1,129},{129,1},{2,130},{130,2},{3,131},{131,3},{4... | collective-permute-start | bytes 1736 | tf_op jit(solution)/shard_map/ppermute | solution.py:30
  5.0 43.5 %all-to-all-start = ((f32[16,32,128]{2,1,0:T(8,128)}), f32[16,32,128]{2,1,0:T(8,128)S(1)}, u32[]{:S(2)}, u32[]{:S(2)}) async-start(f32[16,32,128]{2,1,0:T(8,128)} %get-tuple-element.60), calls=%async_computation | async-start | bytes 524288 | tf_op jit(solution)/shard_map/all_to_all | solution.py:34
  15.0 84.6 %collective-permute-start.5 = (f32[32,8,128]{2,1,0:T(8,128)}, f32[32,8,128]{2,1,0:T(8,128)}, u32[]{:S(2)}, u32[]{:S(2)}) collective-permute-start(f32[32,8,128]{2,1,0:T(8,128)} %get-tuple-element.64), channel_id=1, source_target_pairs={{16,0},{32,16},{48,32},{64,48},{80,64},{96,80},{112,96},{128,112},... | collective-permute-start | bytes 393224 | tf_op jit(solution)/shard_map/ppermute | solution.py:26
  16.3 83.3 %collective-permute-start.7 = (f32[32,8,128]{2,1,0:T(8,128)}, f32[32,8,128]{2,1,0:T(8,128)}, u32[]{:S(2)}, u32[]{:S(2)}) collective-permute-start(f32[32,8,128]{2,1,0:T(8,128)} %get-tuple-element.66), channel_id=1, source_target_pairs={{1,0},{2,1},{3,2},{4,3},{5,4},{6,5},{7,6},{8,7},{9,8},{10,9},{11,1... | collective-permute-start | bytes 393224 | tf_op jit(solution)/shard_map/ppermute | solution.py:26
  20.9 44.4 %collective-permute-start.4 = (f32[33,8,128]{2,1,0:T(8,128)}, f32[33,8,128]{2,1,0:T(8,128)}, u32[]{:S(2)}, u32[]{:S(2)}) collective-permute-start(f32[33,8,128]{2,1,0:T(8,128)} %get-tuple-element.63), channel_id=1, source_target_pairs={{0,16},{16,32},{32,48},{48,64},{64,80},{80,96},{96,112},{112,128},... | collective-permute-start | bytes 405512 | tf_op jit(solution)/shard_map/ppermute | solution.py:26
  27.0 26.1 %collective-permute-start.1 = (bf16[48,128,128]{2,1,0:T(8,128)(2,1)S(1)}, bf16[48,128,128]{2,1,0:T(8,128)(2,1)S(1)}, u32[]{:S(2)}, u32[]{:S(2)}) collective-permute-start(bf16[48,128,128]{2,1,0:T(8,128)(2,1)S(1)} %bitcast.56), channel_id=1, source_target_pairs={{0,128},{128,0},{1,129},{129,1},{2,130},{130,2},{3,131},{131,3},{4... | collective-permute-start | bytes 4718600 | tf_op jit(solution)/shard_map/ppermute | solution.py:30
  35.8 5.8 %copy-start.5 = (s32[4096]{0:T(1024)}, s32[4096]{0:T(1024)S(1)}, u32[]{:S(2)}) copy-start(s32[4096]{0:T(1024)S(1)} %get-tuple-element.121) | copy-start | bytes 49156
  41.0 1.1 copy-start.18
  41.1 1.7 copy-start.15
  41.1 2.3 copy-start.14
  41.1 7.5 %copy-start.22 = (s32[1,1,48]{2,1,0:T(1,128)S(1)}, s32[1,1,48]{2,1,0:T(1,128)}, u32[]{:S(2)}) copy-start(s32[1,1,48]{2,1,0:T(1,128)} %param.22) | copy-start | bytes 580
  48.5 2.7 collective-permute-start.2
  51.2 34.9 %collective-permute-start.6 = (f32[33,8,128]{2,1,0:T(8,128)S(1)}, f32[33,8,128]{2,1,0:T(8,128)}, u32[]{:S(2)}, u32[]{:S(2)}) collective-permute-start(f32[33,8,128]{2,1,0:T(8,128)S(1)} %get-tuple-element.65), channel_id=1, source_target_pairs={{0,1},{1,2},{2,3},{3,4},{4,5},{5,6},{6,7},{7,8},{8,9},{9,10},{10,1... | collective-permute-start | bytes 405512 | tf_op jit(solution)/shard_map/ppermute | solution.py:26
  58.2 14.9 %all-to-all-start.1 = ((f32[8,32,128]{2,1,0:T(8,128)}), f32[8,32,128]{2,1,0:T(8,128)S(1)}, u32[]{:S(2)}, u32[]{:S(2)}) async-start(f32[8,32,128]{2,1,0:T(8,128)} %get-tuple-element.62), calls=%async_computation.1 | async-start | bytes 262144 | tf_op jit(solution)/shard_map/all_to_all | solution.py:34
  73.8 11.0 %all-to-all-start.2 = ((bf16[8,32,128]{2,1,0:T(8,128)(2,1)}), bf16[8,32,128]{2,1,0:T(8,128)(2,1)S(1)}, u32[]{:S(2)}, u32[]{:S(2)}) async-start(bf16[8,32,128]{2,1,0:T(8,128)(2,1)} %shard_map.129), calls=%async_computation.2 | async-start | bytes 131072 | tf_op jit(solution)/shard_map/all_to_all | solution.py:34
  84.8 2.0 collective-permute-start.3
  86.8 12.6 %copy-start.17 = (f32[7,8,8]{2,1,0:T(8,128)S(1)}, f32[7,8,8]{2,1,0:T(8,128)}, u32[]{:S(2)}) copy-start(f32[7,8,8]{2,1,0:T(8,128)} %constant_dynamic-update-slice_fusion.3) | copy-start | bytes 5380
  86.8 12.6 %copy-start.19 = (f32[1,8,7]{2,1,0:T(8,128)S(1)}, f32[1,8,7]{2,1,0:T(8,128)}, u32[]{:S(2)}) copy-start(f32[1,8,7]{2,1,0:T(8,128)} %slice_bitcast_fusion) | copy-start | bytes 676
  86.8 12.6 %copy-start.24 = (pred[8]{0:T(512)(128)(4,1)S(1)}, pred[8]{0:T(512)(128)(4,1)}, u32[]{:S(2)}) copy-start(pred[8]{0:T(512)(128)(4,1)} %iota_compare_fusion.8) | copy-start | bytes 28
  86.8 12.7 %copy-start.25 = (pred[8]{0:T(512)(128)(4,1)S(1)}, pred[8]{0:T(512)(128)(4,1)}, u32[]{:S(2)}) copy-start(pred[8]{0:T(512)(128)(4,1)} %iota_compare_fusion.7) | copy-start | bytes 28
  92.5 16.8 %all-to-all-start.3 = ((f32[16,32,128]{2,1,0:T(8,128)}), f32[16,32,128]{2,1,0:T(8,128)S(1)}, u32[]{:S(2)}, u32[]{:S(2)}) async-start(f32[16,32,128]{2,1,0:T(8,128)} %shard_map.130), calls=%async_computation.3 | async-start | bytes 524288 | tf_op jit(solution)/shard_map/all_to_all | solution.py:34
  126.9 1.6 copy-start.2
  127.0 1.6 collective-permute-start.8
  128.6 0.8 copy-start.4
  170.7 12.4 %copy-start.20 = (s32[1,1,128]{2,1,0:T(1,128)S(1)}, s32[1,1,128]{2,1,0:T(1,128)}, u32[]{:S(2)}) copy-start(s32[1,1,128]{2,1,0:T(1,128)} %param.24) | copy-start | bytes 1540
  170.7 1.3 collective-permute-start.9
  177.6 34.0 %all-to-all-start.8 = ((f32[16,32,128]{2,1,0:T(8,128)}), f32[16,32,128]{2,1,0:T(8,128)S(1)}, u32[]{:S(2)}, u32[]{:S(2)}) async-start(f32[16,32,128]{2,1,0:T(8,128)} %shard_map.136), calls=%async_computation.8 | async-start | bytes 524288 | tf_op jit(solution)/shard_map/all_to_all | solution.py:34
  186.0 12.0 %collective-permute-start.10 = (f32[32,8,128]{2,1,0:T(8,128)S(1)}, f32[32,8,128]{2,1,0:T(8,128)S(1)}, u32[]{:S(2)}, u32[]{:S(2)}) collective-permute-start(f32[32,8,128]{2,1,0:T(8,128)S(1)} %get-tuple-element.81), channel_id=1, source_target_pairs={{0,16},{16,32},{32,48},{48,64},{64,80},{80,96},{96,112},{112,128},... | collective-permute-start | bytes 393224 | tf_op jit(solution)/shard_map/ppermute | solution.py:26
  188.7 9.5 %collective-permute-start.11 = (f32[32,8,128]{2,1,0:T(8,128)S(1)}, f32[32,8,128]{2,1,0:T(8,128)S(1)}, u32[]{:S(2)}, u32[]{:S(2)}) collective-permute-start(f32[32,8,128]{2,1,0:T(8,128)S(1)} %get-tuple-element.82), channel_id=1, source_target_pairs={{16,0},{32,16},{48,32},{64,48},{80,64},{96,80},{112,96},{128,112},... | collective-permute-start | bytes 393224 | tf_op jit(solution)/shard_map/ppermute | solution.py:26
  190.0 9.0 %collective-permute-start.12 = (f32[32,8,128]{2,1,0:T(8,128)S(1)}, f32[32,8,128]{2,1,0:T(8,128)S(1)}, u32[]{:S(2)}, u32[]{:S(2)}) collective-permute-start(f32[32,8,128]{2,1,0:T(8,128)S(1)} %get-tuple-element.83), channel_id=1, source_target_pairs={{0,1},{1,2},{2,3},{3,4},{4,5},{5,6},{6,7},{7,8},{8,9},{9,10},{10,1... | collective-permute-start | bytes 393224 | tf_op jit(solution)/shard_map/ppermute | solution.py:26
  193.4 7.1 %collective-permute-start.13 = (f32[32,8,128]{2,1,0:T(8,128)S(1)}, f32[32,8,128]{2,1,0:T(8,128)S(1)}, u32[]{:S(2)}, u32[]{:S(2)}) collective-permute-start(f32[32,8,128]{2,1,0:T(8,128)S(1)} %get-tuple-element.84), channel_id=1, source_target_pairs={{1,0},{2,1},{3,2},{4,3},{5,4},{6,5},{7,6},{8,7},{9,8},{10,9},{11,1... | collective-permute-start | bytes 393224 | tf_op jit(solution)/shard_map/ppermute | solution.py:26
  198.0 2.5 copy-start.8
  198.2 2.3 copy-start.10
  199.0 1.5 copy-start.11
  200.5 0.6 copy-start.13
  230.3 4.4 %copy-start.1 = (f32[16,40,128]{2,1,0:T(8,128)}, f32[16,40,128]{2,1,0:T(8,128)S(1)}, u32[]{:S(2)}) copy-start(f32[16,40,128]{2,1,0:T(8,128)S(1)} %all_to_all.69.mine_ref.refs_7_) | copy-start | bytes 983044
  230.3 4.4 %collective-permute-start.14 = (f32[16,40,128]{2,1,0:T(8,128)S(1)}, f32[16,40,128]{2,1,0:T(8,128)S(1)}, u32[]{:S(2)}, u32[]{:S(2)}) collective-permute-start(f32[16,40,128]{2,1,0:T(8,128)S(1)} %all_to_all.69.mine_ref.refs_7_), channel_id=1, source_target_pairs={{0,128},{128,0},{1,129},{129,1},{2,130},{130,2},{3,131},{131,3},{4... | collective-permute-start | bytes 983048 | tf_op jit(solution)/shard_map/ppermute | solution.py:30
  234.6 0.7 copy-start.3
  255.6 30.4 %all-to-all-start.11 = ((f32[8,64,128]{2,1,0:T(8,128)}), f32[8,64,128]{2,1,0:T(8,128)S(1)}, u32[]{:S(2)}, u32[]{:S(2)}) async-start(f32[8,64,128]{2,1,0:T(8,128)} %get-tuple-element.95), calls=%async_computation.11 | async-start | bytes 524288 | tf_op jit(solution)/shard_map/all_to_all | solution.py:34
  261.0 14.6 %collective-permute-start.15 = (f32[32,8,128]{2,1,0:T(8,128)S(1)}, f32[32,8,128]{2,1,0:T(8,128)S(1)}, u32[]{:S(2)}, u32[]{:S(2)}) collective-permute-start(f32[32,8,128]{2,1,0:T(8,128)S(1)} %get-tuple-element.104), channel_id=1, source_target_pairs={{0,16},{16,32},{32,48},{48,64},{64,80},{80,96},{96,112},{112,128},... | collective-permute-start | bytes 393224 | tf_op jit(solution)/shard_map/ppermute | solution.py:26
  266.4 9.3 %collective-permute-start.16 = (f32[32,8,128]{2,1,0:T(8,128)S(1)}, f32[32,8,128]{2,1,0:T(8,128)S(1)}, u32[]{:S(2)}, u32[]{:S(2)}) collective-permute-start(f32[32,8,128]{2,1,0:T(8,128)S(1)} %get-tuple-element.105), channel_id=1, source_target_pairs={{16,0},{32,16},{48,32},{64,48},{80,64},{96,80},{112,96},{128,112},... | collective-permute-start | bytes 393224 | tf_op jit(solution)/shard_map/ppermute | solution.py:26
  267.7 9.0 %collective-permute-start.17 = (f32[32,8,128]{2,1,0:T(8,128)S(1)}, f32[32,8,128]{2,1,0:T(8,128)S(1)}, u32[]{:S(2)}, u32[]{:S(2)}) collective-permute-start(f32[32,8,128]{2,1,0:T(8,128)S(1)} %get-tuple-element.106), channel_id=1, source_target_pairs={{0,1},{1,2},{2,3},{3,4},{4,5},{5,6},{6,7},{7,8},{8,9},{9,10},{10,1... | collective-permute-start | bytes 393224 | tf_op jit(solution)/shard_map/ppermute | solution.py:26
  271.8 6.9 %collective-permute-start.18 = (f32[32,8,128]{2,1,0:T(8,128)S(1)}, f32[32,8,128]{2,1,0:T(8,128)S(1)}, u32[]{:S(2)}, u32[]{:S(2)}) collective-permute-start(f32[32,8,128]{2,1,0:T(8,128)S(1)} %get-tuple-element.107), channel_id=1, source_target_pairs={{1,0},{2,1},{3,2},{4,3},{5,4},{6,5},{7,6},{8,7},{9,8},{10,9},{11,1... | collective-permute-start | bytes 393224 | tf_op jit(solution)/shard_map/ppermute | solution.py:26
  275.6 3.0 copy-start.6
  275.7 3.0 copy-start.7
  276.6 2.0 copy-start.9
  278.6 0.7 copy-start.12

commit v5 on v3

--- a/solution.py
+++ b/solution.py
@@ -114,11 +114,14 @@
     return (make((cases, width, lanes)),) * 2 + (make((cases, slabs, lanes)),) * 2
 
 
-def first_trace_kernel(field_ref, surface_ref, end_ref, out_ref, *edge_refs):
+def first_trace_kernel(field_ref, surface_ref, across_ref, along_ref, out_ref, *edge_refs):
     cases, slabs = field_ref.shape[:2]
     copies = out_ref.shape[0]
-    edge_refs[0][cases] = end_ref[0]
-    edge_refs[2][cases] = end_ref[1]
+    square = across_ref.shape
+    here = lax.broadcasted_iota(jnp.int32, square, 0) == lax.broadcasted_iota(jnp.int32, square, 1)
+    last_row = jnp.sum(jnp.where(here, across_ref[slabs - 1 :, :], 0.0), axis=1, keepdims=True)
+    edge_refs[0][cases] = jnp.broadcast_to(last_row, (square[1], 128))
+    edge_refs[2][cases] = jnp.broadcast_to(along_ref[:, square[1] - 1 :], (square[0], 128))
     local = jnp.broadcast_to(surface_ref[...], (8, 128))
     lane_index, block_index = local & 127, local >> 7
 
@@ -147,6 +150,28 @@
             picked = lanes_taken(source_ref[b, 8 * g : 8 * g + 8, :], lane_index)
             totals[g] = jnp.where(here, picked, totals[g])
     return totals
+
+
+def selected_block(flat_ref, lanes_ref, blocks_ref, d, cases):
+    width = flat_ref.shape[1] // 128
+    wanted = jnp.broadcast_to(lanes_ref[pl.ds(d, 1), :], (128, 128))
+    chosen = jnp.where(row_iota((128, 128)) == wanted, 1.0, 0.0).astype(BF16)
+    chosen = jnp.concatenate([chosen] * width, axis=0)
+    block_index = jnp.broadcast_to(blocks_ref[pl.ds(d, 1), :], (cases, 128))
+    step = 256 // cases
+    total = jnp.zeros((cases, 128), F32)
+    for g in range(flat_ref.shape[0] // 256):
+        found = jnp.dot(
+            flat_ref[256 * g : 256 * g + 256, :], chosen, preferred_element_type=F32
+        ).reshape(step, cases, 128)
+        for j in range(step):
+            total = jnp.where(block_index == g * step + j, found[j], total)
+    return total
+
+
+def high_and_low(value):
+    high = value.astype(BF16)
+    return high, (value - high.astype(F32)).astype(BF16)
 
 
 def alpha_beta(sums_ref, cases):
@@ -192,26 +217,35 @@
                     residual_ref[b] = residual
                 direction_ref[b] = residual + beta * old_direction_ref[b]
     cases = direction_ref.shape[1]
+    sums_scratch, flat_ref = rest
     if not last:
         place = pairs_ref[3, 0]
         slots_ref[0] = direction_ref[place] if first else residual_ref[place]
         slots_ref[1] = direction_ref[place]
 
+    owners = direction_ref.shape[0]
+    half = owners // 2
+    for i in range(0, owners, 8):
+        value = direction_ref[i : i + 8].reshape(8 * cases, 128)
+        if last:
+            high, low = high_and_low(value)
+            flat_ref[i * cases : (i + 8) * cases, :128] = high
+            flat_ref[i * cases : (i + 8) * cases, 128:] = low
+        else:
+            flat_ref[i * cases : (i + 8) * cases, :] = value.astype(BF16)
+
     def step(d, carry):
-        totals = permuted_block(direction_ref, lanes_ref, blocks_ref, d)
-        value = jnp.concatenate(totals, axis=0)
-        low = value.astype(BF16)
-        if last:
-            left = value - low.astype(F32)
-            second = left.astype(BF16)
-            low_ref[d] = jnp.concatenate([low, second], axis=0)
-        else:
-            low_ref[d] = low
+        one = permuted_block(direction_ref, lanes_ref, blocks_ref, d)
+        two = selected_block(flat_ref, lanes_ref, blocks_ref, half + d, cases)
+        for at, value in ((d, jnp.concatenate(one, axis=0)), (half + d, two)):
+            if last:
+                low_ref[at] = jnp.concatenate(high_and_low(value), axis=0)
+            else:
+                low_ref[at] = value.astype(BF16)
         return carry
 
-    lax.fori_loop(0, direction_ref.shape[0], step, 0, unroll=4)
+    lax.fori_loop(0, half, step, 0, unroll=2)
     half_count = keep_ref.shape[0]
-    sums_scratch = rest[0]
     sums_scratch[...] = jnp.zeros(sums_scratch.shape, F32)
     live = pairs_ref[2, 0]
     for p in range(boundary_ref.shape[0]):
@@ -510,12 +544,10 @@
         kept((cases + 1, slabs, lanes)),
         kept((cases, slabs, lanes)),
     ]
-    ends = jnp.stack([across_weight[-1, :], along_weight[:, -1]])
-    ends = jnp.broadcast_to(ends[:, :, None], (2, width, lanes))
     trace, *edges = kernel(
         first_trace_kernel,
         (kept((blk_count, cases, lanes)), *first_edges),
-        (right_side, surface, ends),
+        (right_side, surface, across_weight, along_weight),
     )
     mine = exchanged(trace, BLK)
     other = partner(mine)
@@ -601,6 +633,7 @@
         scratch = [
             pltpu.VMEM((slot_count // lanes, deep, lanes), BF16),
             pltpu.VMEM((2 * half_columns, deep, lanes), F32),
+            pltpu.VMEM((owners * cases, 2 * lanes if last else lanes), BF16),
         ]
         halves = (kept((half_columns, deep, lanes)),) * 2
         if not first:

time: 306 us -> 301 us (0.984)
  no operation moved by 1% of the time
where the time goes in v5:
time: 301 us; the launch traced here: 297 us
  blocking collectives  99.3 us (33%)
  starting transfers between devices  82.1 us (27%)
  Pallas kernels  65.3 us (22%)
  waiting for transfers between devices  38.1 us (13%)
  other arithmetic  6.71 us (2%)
  local copies, waits for them, and re-layouts  3.34 us (1%)
    all_to_all x7, blocking collectives, exchanged(): return lax.all_to_all(pieces, axes, split_axis=0, concat_axis=0, tiled=True)  99.3 us
    pallas_call x20, Pallas kernels, kernel(): pl.pallas_call(body, out_shape=outs, in_specs=[SMEM] * scalars + [pl.Bloc...  65.3 us
    ppermute x12, starting transfers between devices, passed_along(): return lax.ppermute(value, axis, pairs)  39.6 us
    all_to_all x6, starting transfers between devices, exchanged(): return lax.all_to_all(pieces, axes, split_axis=0, concat_axis=0, tiled=True)  35.6 us
    all_to_all x6, waiting for transfers between devices, exchanged(): return lax.all_to_all(pieces, axes, split_axis=0, concat_axis=0, tiled=True)  19.8 us
    ppermute x10, waiting for transfers between devices, partner(): return lax.ppermute(value, 'sec', [(0, 1), (1, 0)])  12.8 us
    ppermute x10, starting transfers between devices, partner(): return lax.ppermute(value, 'sec', [(0, 1), (1, 0)])  6.9 us
  transfers between devices with their start and end apart: 28, of which 18 were waited for; matrix products, arithmetic and copies ran while one was open for 3% of the time, Pallas kernels for 13%

profile of v5, /device:TPU:8, one launch (start us, length us, event | category | flops | bytes accessed | tf_op | source)
XLA Modules:
  0.0 297.4 jit_solution(10412523442061773746)
XLA Ops:
  0.0 3.0 %shard_map.127 = (f32[16,32,128]{2,1,0:T(8,128)}, f32[33,8,128]{2,1,0:T(8,128)S(1)}, f32[32,8,128]{2,1,0:T(8,128)S(1)}, f32[33,8,128]{2,1,0:T(8,128)S(1)}, f32[32,8,128]{2,1,0:T(8,128)S(1)}) custom-call(f32[32,8,8,128]{3,2,1,0:T(8,128)} %refs_5_.1, s32[1,128]{1,0:T(1,128)} %bitcast.69, f32[8,8]{1,0:T(8,128)} %across_ref.1, f32[8,8]{1,0:T(8,128)} %along_ref.1), custom_call_target="tpu_custom_call" | custom-call | tf_op jit(solution)/shard_map/pallas_call | solution.py:51
  3.0 9.9 %all-to-all-start = ((f32[16,32,128]{2,1,0:T(8,128)}), f32[16,32,128]{2,1,0:T(8,128)S(1)}, u32[]{:S(2)}, u32[]{:S(2)}) async-start(f32[16,32,128]{2,1,0:T(8,128)} %get-tuple-element.67), calls=%async_computation | async-start | bytes 524288 | tf_op jit(solution)/shard_map/all_to_all | solution.py:34
  12.9 4.2 %collective-permute-start.4 = (f32[33,8,128]{2,1,0:T(8,128)S(1)}, f32[33,8,128]{2,1,0:T(8,128)S(1)}, u32[]{:S(2)}, u32[]{:S(2)}) collective-permute-start(f32[33,8,128]{2,1,0:T(8,128)S(1)} %get-tuple-element.73), channel_id=1, source_target_pairs={{0,16},{16,32},{32,48},{48,64},{64,80},{80,96},{96,112},{112,128},... | collective-permute-start | bytes 405512 | tf_op jit(solution)/shard_map/ppermute | solution.py:26
  17.1 1.3 collective-permute-start.5
  18.4 3.4 %collective-permute-start.6 = (f32[33,8,128]{2,1,0:T(8,128)S(1)}, f32[33,8,128]{2,1,0:T(8,128)S(1)}, u32[]{:S(2)}, u32[]{:S(2)}) collective-permute-start(f32[33,8,128]{2,1,0:T(8,128)S(1)} %get-tuple-element.75), channel_id=1, source_target_pairs={{0,1},{1,2},{2,3},{3,4},{4,5},{5,6},{6,7},{7,8},{8,9},{9,10},{10,1... | collective-permute-start | bytes 405512 | tf_op jit(solution)/shard_map/ppermute | solution.py:26
  21.8 4.6 %collective-permute-start.7 = (f32[32,8,128]{2,1,0:T(8,128)S(1)}, f32[32,8,128]{2,1,0:T(8,128)S(1)}, u32[]{:S(2)}, u32[]{:S(2)}) collective-permute-start(f32[32,8,128]{2,1,0:T(8,128)S(1)} %get-tuple-element.76), channel_id=1, source_target_pairs={{1,0},{2,1},{3,2},{4,3},{5,4},{6,5},{7,6},{8,7},{9,8},{10,9},{11,1... | collective-permute-start | bytes 393224 | tf_op jit(solution)/shard_map/ppermute | solution.py:26
  27.1 2.9 select_convert_fusion.1
  32.2 2.5 collective-permute-start
  34.9 0.9 collective-permute-done.refs_5_
  35.8 4.5 %shard_map.128 = (f32[32,32,128]{2,1,0:T(8,128)}, f32[2,32,128]{2,1,0:T(8,128)}, f32[8,32,128]{2,1,0:T(8,128)S(1)}, f32[8,32,128]{2,1,0:T(8,128)S(1)}) custom-call(s32[4,48]{1,0:T(4,128)S(1)} %add_add_fusion.refs_0_.pairs_ref, s32[32,128]{1,0:T(8,128)} %get-tuple-element.134.refs_1_, s32[32,128]{1,0:T(8,128)} %bitcast.65, ...), custom_call_target="tpu_custom_call" | custom-call | tf_op jit(solution)/shard_map/pallas_call | solution.py:51
  40.7 1.0 collective-permute-done.1
  42.3 5.8 %all-to-all-start.1 = ((f32[8,32,128]{2,1,0:T(8,128)}), f32[8,32,128]{2,1,0:T(8,128)S(1)}, u32[]{:S(2)}, u32[]{:S(2)}) async-start(f32[8,32,128]{2,1,0:T(8,128)} %add.66), calls=%async_computation.1 | async-start | bytes 262144 | tf_op jit(solution)/shard_map/all_to_all | solution.py:34
  48.2 7.9 %all-to-all-done.1.pieces_ref = f32[8,32,128]{2,1,0:T(8,128)S(1)} async-done(((f32[8,32,128]{2,1,0:T(8,128)}), f32[8,32,128]{2,1,0:T(8,128)S(1)}, u32[]{:S(2)}, u32[]{:S(2)}) %all-to-all-start.1) | async-done | bytes 131104 | tf_op jit(solution)/shard_map/all_to_all | solution.py:34
  56.7 3.4 %all-to-all-start.2 = ((bf16[8,32,128]{2,1,0:T(8,128)(2,1)}), bf16[8,32,128]{2,1,0:T(8,128)(2,1)S(1)}, u32[]{:S(2)}, u32[]{:S(2)}) async-start(bf16[8,32,128]{2,1,0:T(8,128)(2,1)} %shard_map.129), calls=%async_computation.2 | async-start | bytes 131072 | tf_op jit(solution)/shard_map/all_to_all | solution.py:34
  60.1 7.7 %all-to-all-done.2.mine_ref = bf16[8,32,128]{2,1,0:T(8,128)(2,1)S(1)} async-done(((bf16[8,32,128]{2,1,0:T(8,128)(2,1)}), bf16[8,32,128]{2,1,0:T(8,128)(2,1)S(1)}, u32[]{:S(2)}, u32[]{:S(2)}) %all-to-all-start.2) | async-done | bytes 65568 | tf_op jit(solution)/shard_map/all_to_all | solution.py:34
  67.9 1.1 collective-permute-done.2.other_ref
  69.0 6.6 %shard_map.130 = (f32[16,32,128]{2,1,0:T(8,128)S(1)}, f32[16,32,128]{2,1,0:T(8,128)S(1)}) custom-call(s32[4,48]{1,0:T(4,128)S(1)} %add_add_fusion.refs_0_.pairs_ref, s32[32,128]{1,0:T(8,128)} %get-tuple-element.130.lanes_ref, s32[32,128]{1,0:T(8,128)} %get-tuple-element.129.blocks_ref, bf16[48,128,128]{2,1,0:T(8,128)(2,1)S(1)} %bitcast.61, ...), custom_call_target="tpu_custom_call" | custom-call | tf_op jit(solution)/shard_map/pallas_call | solution.py:51
  76.0 1.3 collective-permute-done.3
  78.0 7.2 %all-to-all-start.3 = ((f32[16,32,128]{2,1,0:T(8,128)}), f32[16,32,128]{2,1,0:T(8,128)S(1)}, u32[]{:S(2)}, u32[]{:S(2)}) async-start(f32[16,32,128]{2,1,0:T(8,128)} %add.67), calls=%async_computation.3 | async-start | bytes 524288 | tf_op jit(solution)/shard_map/all_to_all | solution.py:34
  85.4 0.8 broadcast_in_dim.89.refs_4_.refs_5_.refs_19_
  86.3 4.5 %shard_map.131 = (f32[32,8,8,128]{3,2,1,0:T(8,128)}, f32[32,128]{1,0:T(8,128)}, f32[32,128]{1,0:T(8,128)}, f32[32,8,128]{2,1,0:T(8,128)}, f32[32,8,128]{2,1,0:T(...) custom-call(f32[32,8,8,128]{3,2,1,0:T(8,128)} %refs_5_.1, f32[33,8,128]{2,1,0:T(8,128)} %copy-done.2, ...), custom_call_target="tpu_custom_call" | custom-call | tf_op jit(solution)/shard_map/pallas_call | solution.py:51
  90.8 4.2 %all-to-all-done.3.arrived_ref = f32[16,32,128]{2,1,0:T(8,128)S(1)} async-done(((f32[16,32,128]{2,1,0:T(8,128)}), f32[16,32,128]{2,1,0:T(8,128)S(1)}, u32[]{:S(2)}, u32[]{:S(2)}) %all-to-all-start.3) | async-done | bytes 262176 | tf_op jit(solution)/shard_map/all_to_all | solution.py:34
  95.0 1.5 shard_map.132
  96.4 15.4 %all_to_all.65.mine_ref.refs_6_ = f32[16,40,128]{2,1,0:T(8,128)S(1)} all-to-all(f32[16,40,128]{2,1,0:T(8,128)S(1)} %get-tuple-element.80), channel_id=1, replica_groups=mesh['sec'=2,'clu_0'=4,'clu_1'=2,'blk_0'=2,'blk_1'=8] {'blk_0','blk_1'}, dimensions={0} | all-to-all | bytes 655360 | tf_op jit(solution)/shard_map/all_to_all | solution.py:34
  111.8 1.6 collective-permute-done.8.other_ref.refs_7_
  113.5 10.2 %all_to_all.66.refs_8_ = f32[8,1,128]{2,1,0:T(1,128)S(1)} all-to-all(f32[8,1,128]{2,1,0:T(1,128)S(1)} %shard_map.133), channel_id=1, replica_groups=mesh['sec'=2,'clu_0'=4,'clu_1'=2,'blk_0'=2,'blk_1'=8] {'clu_0','clu_1'}, dimensions={0} | all-to-all | bytes 8192 | tf_op jit(solution)/shard_map/all_to_all | solution.py:34
  123.6 5.3 %shard_map.134 = (f32[2,32,128]{2,1,0:T(8,128)}, f32[32,32,128]{2,1,0:T(8,128)}, f32[32,32,128]{2,1,0:T(8,128)}, f32[2,32,128]{2,1,0:T(8,128)}, f32[8,32,128]{2,1,0:T(8,128)S(1)}, /*index=5*/f32[8,32,128]{2,1,0:T(8,128)S(1)}) custom-call(s32[4,48]{1,0:T(4,128)S(1)} %add_add_fusion.refs_0_.pairs_ref, s32[32,128]{1,0:T(8,128)} %get-tuple-element.134.refs_1_, ...), custom_call_target="tpu_custom_call" | custom-call | tf_op jit(solution)/shard_map/pallas_call | solution.py:51
  129.0 1.3 collective-permute-done.9
  130.3 10.5 %all_to_all.67.pieces_ref = f32[8,32,128]{2,1,0:T(8,128)S(1)} all-to-all(f32[8,32,128]{2,1,0:T(8,128)S(1)} %add.68), channel_id=1, replica_groups=mesh['sec'=2,'clu_0'=4,'clu_1'=2,'blk_0'=2,'blk_1'=8] {'clu_0','clu_1'}, dimensions={0} | all-to-all | bytes 262144 | tf_op jit(solution)/shard_map/all_to_all | solution.py:34
  140.8 10.3 %all_to_all.68.mine_ref = bf16[8,32,128]{2,1,0:T(8,128)(2,1)S(1)} all-to-all(bf16[8,32,128]{2,1,0:T(8,128)(2,1)S(1)} %shard_map.135), channel_id=1, replica_groups=mesh['sec'=2,'clu_0'=4,'clu_1'=2,'blk_0'=2,'blk_1'=8] {'clu_0','clu_1'}, dimensions={0} | all-to-all | bytes 131072 | tf_op jit(solution)/shard_map/all_to_all | solution.py:34
  151.1 1.3 collective-permute-done.10.other_ref
  152.4 6.6 %shard_map.136 = (f32[16,32,128]{2,1,0:T(8,128)S(1)}, f32[16,32,128]{2,1,0:T(8,128)S(1)}) custom-call(s32[4,48]{1,0:T(4,128)S(1)} %add_add_fusion.refs_0_.pairs_ref, s32[32,128]{1,0:T(8,128)} %get-tuple-element.130.lanes_ref, s32[32,128]{1,0:T(8,128)} %get-tuple-element.129.blocks_ref, bf16[48,128,128]{2,1,0:T(8,128)(2,1)S(1)} %bitcast.63, ...), custom_call_target="tpu_custom_call" | custom-call | tf_op jit(solution)/shard_map/pallas_call | solution.py:51
  159.3 1.4 collective-permute-done.11
  160.7 0.7 add.69
  161.4 5.8 %all-to-all-start.8 = ((f32[16,32,128]{2,1,0:T(8,128)}), f32[16,32,128]{2,1,0:T(8,128)S(1)}, u32[]{:S(2)}, u32[]{:S(2)}) async-start(f32[16,32,128]{2,1,0:T(8,128)} %add.69), calls=%async_computation.8 | async-start | bytes 524288 | tf_op jit(solution)/shard_map/all_to_all | solution.py:34
  167.3 0.8 fusion.7.inverse_ref.refs_2_
  168.1 2.0 shard_map.137
  170.1 2.4 collective-permute-start.12
  172.5 1.3 collective-permute-start.13
  173.8 3.4 %collective-permute-start.14 = (f32[32,8,128]{2,1,0:T(8,128)S(1)}, f32[32,8,128]{2,1,0:T(8,128)S(1)}, u32[]{:S(2)}, u32[]{:S(2)}) collective-permute-start(f32[32,8,128]{2,1,0:T(8,128)S(1)} %get-tuple-element.96), channel_id=1, source_target_pairs={{0,1},{1,2},{2,3},{3,4},{4,5},{5,6},{6,7},{7,8},{8,9},{9,10},{10,1... | collective-permute-start | bytes 393224 | tf_op jit(solution)/shard_map/ppermute | solution.py:26
  177.2 4.6 %collective-permute-start.15 = (f32[32,8,128]{2,1,0:T(8,128)S(1)}, f32[32,8,128]{2,1,0:T(8,128)S(1)}, u32[]{:S(2)}, u32[]{:S(2)}) collective-permute-start(f32[32,8,128]{2,1,0:T(8,128)S(1)} %get-tuple-element.97), channel_id=1, source_target_pairs={{1,0},{2,1},{3,2},{4,3},{5,4},{6,5},{7,6},{8,7},{9,8},{10,9},{11,1... | collective-permute-start | bytes 393224 | tf_op jit(solution)/shard_map/ppermute | solution.py:26
  182.0 0.8 collective-permute-done.14.refs_8_
  182.8 1.4 collective-permute-done.15.refs_9_
  184.9 5.6 %shard_map.138 = (f32[32,8,8,128]{3,2,1,0:T(8,128)}, f32[32,8,8,128]{3,2,1,0:T(8,128)}, f32[32,8,8,128]{3,2,1,0:T(8,128)}, f32[32,8,128]{2,1,0:T(8,128)}, f32[32...) custom-call(f32[2,32,128]{2,1,0:T(8,128)} %get-tuple-element.87.refs, ...), custom_call_target="tpu_custom_call" | custom-call | tf_op jit(solution)/shard_map/pallas_call | solution.py:51
  190.5 4.9 %shard_map.139 = (f32[32,8,8,128]{3,2,1,0:T(8,128)}, f32[32,128]{1,0:T(8,128)}, f32[32,128]{1,0:T(8,128)}, f32[32,8,128]{2,1,0:T(8,128)}, f32[32,8,128]{2,1,0:T(...) custom-call(f32[32,8,8,128]{3,2,1,0:T(8,128)} %get-tuple-element.98.direction_ref.refs_5_, ...), custom_call_target="tpu_custom_call" | custom-call | tf_op jit(solution)/shard_map/pallas_call | solution.py:51
  195.4 1.4 shard_map.140
  196.8 16.2 %all_to_all.69.mine_ref.refs_6_ = f32[16,40,128]{2,1,0:T(8,128)S(1)} all-to-all(f32[16,40,128]{2,1,0:T(8,128)S(1)} %get-tuple-element.107), channel_id=1, replica_groups=mesh['sec'=2,'clu_0'=4,'clu_1'=2,'blk_0'=2,'blk_1'=8] {'blk_0','blk_1'}, dimensions={0} | all-to-all | bytes 655360 | tf_op jit(solution)/shard_map/all_to_all | solution.py:34
  213.0 3.5 %collective-permute-start.16 = (f32[16,40,128]{2,1,0:T(8,128)S(1)}, f32[16,40,128]{2,1,0:T(8,128)S(1)}, u32[]{:S(2)}, u32[]{:S(2)}) collective-permute-start(f32[16,40,128]{2,1,0:T(8,128)S(1)} %all_to_all.69.mine_ref.refs_6_), channel_id=1, source_target_pairs={{0,128},{128,0},{1,129},{129,1},{2,130},{130,2},{3,131},{131,3},{4... | collective-permute-start | bytes 983048 | tf_op jit(solution)/shard_map/ppermute | solution.py:30
  216.6 1.3 collective-permute-done.16.other_ref.refs_7_
  217.8 11.8 %all_to_all.70.refs_8_ = f32[8,1,128]{2,1,0:T(1,128)S(1)} all-to-all(f32[8,1,128]{2,1,0:T(1,128)S(1)} %shard_map.141), channel_id=1, replica_groups=mesh['sec'=2,'clu_0'=4,'clu_1'=2,'blk_0'=2,'blk_1'=8] {'clu_0','clu_1'}, dimensions={0} | all-to-all | bytes 8192 | tf_op jit(solution)/shard_map/all_to_all | solution.py:34
  229.7 6.1 %shard_map.142 = (f32[2,32,128]{2,1,0:T(8,128)}, f32[8,64,128]{2,1,0:T(8,128)S(1)}, f32[8,64,128]{2,1,0:T(8,128)S(1)}) custom-call(s32[4,48]{1,0:T(4,128)S(1)} %add_add_fusion.refs_0_.pairs_ref, s32[32,128]{1,0:T(8,128)} %get-tuple-element.134.refs_1_, s32[32,128]{1,0:T(8,128)} %bitcast.67, bf16[48,128,128]{2,1,0:T(8,128)(2,1)S(1)} %bitcast.64, ...), custom_call_target="tpu_custom_call" | custom-call | tf_op jit(solution)/shard_map/pallas_call | solution.py:51
  235.8 1.5 collective-permute-done.17
  238.0 3.4 %all-to-all-start.11 = ((f32[8,64,128]{2,1,0:T(8,128)}), f32[8,64,128]{2,1,0:T(8,128)S(1)}, u32[]{:S(2)}, u32[]{:S(2)}) async-start(f32[8,64,128]{2,1,0:T(8,128)} %add.72), calls=%async_computation.11 | async-start | bytes 524288 | tf_op jit(solution)/shard_map/all_to_all | solution.py:34
  241.5 2.0 shard_map.143
  243.5 5.3 %collective-permute-start.18 = (f32[32,8,128]{2,1,0:T(8,128)S(1)}, f32[32,8,128]{2,1,0:T(8,128)S(1)}, u32[]{:S(2)}, u32[]{:S(2)}) collective-permute-start(f32[32,8,128]{2,1,0:T(8,128)S(1)} %get-tuple-element.118), channel_id=1, source_target_pairs={{0,16},{16,32},{32,48},{48,64},{64,80},{80,96},{96,112},{112,128},... | collective-permute-start | bytes 393224 | tf_op jit(solution)/shard_map/ppermute | solution.py:26
  248.8 1.3 collective-permute-start.19
  250.1 4.2 %collective-permute-start.20 = (f32[32,8,128]{2,1,0:T(8,128)S(1)}, f32[32,8,128]{2,1,0:T(8,128)S(1)}, u32[]{:S(2)}, u32[]{:S(2)}) collective-permute-start(f32[32,8,128]{2,1,0:T(8,128)S(1)} %get-tuple-element.120), channel_id=1, source_target_pairs={{0,1},{1,2},{2,3},{3,4},{4,5},{5,6},{6,7},{7,8},{8,9},{9,10},{10,1... | collective-permute-start | bytes 393224 | tf_op jit(solution)/shard_map/ppermute | solution.py:26
  254.3 3.8 %collective-permute-start.21 = (f32[32,8,128]{2,1,0:T(8,128)S(1)}, f32[32,8,128]{2,1,0:T(8,128)S(1)}, u32[]{:S(2)}, u32[]{:S(2)}) collective-permute-start(f32[32,8,128]{2,1,0:T(8,128)S(1)} %get-tuple-element.121), channel_id=1, source_target_pairs={{1,0},{2,1},{3,2},{4,3},{5,4},{6,5},{7,6},{8,7},{9,8},{10,9},{11,1... | collective-permute-start | bytes 393224 | tf_op jit(solution)/shard_map/ppermute | solution.py:26
  258.1 1.0 collective-permute-done.20.refs_9_
  259.1 2.0 collective-permute-done.21.refs_10_
  261.8 6.6 %shard_map.144 = (f32[32,8,8,128]{3,2,1,0:T(8,128)}, f32[32,8,8,128]{3,2,1,0:T(8,128)}, f32[32,128]{1,0:T(8,128)}) custom-call(f32[2,32,128]{2,1,0:T(8,128)} %get-tuple-element.110.refs_0_, f32[32,128]{1,0:T(8,128)} %get-tuple-element.111.own_ref.refs_1_, s32[8,8,128]{2,1,0:T(8,128)} %fusion.7.inverse_ref.refs_2_, ...), custom_call_target="tpu_custom_call" | custom-call | tf_op jit(solution)/shard_map/pallas_call | solution.py:51
  268.4 1.0 shard_map.145
  269.4 24.9 %all_to_all.71.sums_ref = f32[256,1,128]{2,1,0:T(1,128)S(1)} all-to-all(f32[256,1,128]{2,1,0:T(1,128)S(1)} %shard_map.145), channel_id=1, replica_groups=mesh['sec'=2,'clu_0'=4,'clu_1'=2,'blk_0'=2,'blk_1'=8] {'sec','clu_0','cl..., dimensions={0} | all-to-all | bytes 262144 | tf_op jit(solution)/shard_map/all_to_all | solution.py:34
  294.3 3.0 %shard_map.146 = f32[32,8,8,128]{3,2,1,0:T(8,128)} custom-call(f32[256,1,128]{2,1,0:T(1,128)S(1)} %all_to_all.71.sums_ref, f32[32,8,8,128]{3,2,1,0:T(8,128)} %get-tuple-element.127.direction_ref, f32[32,8,8,128]{3,2,1,0:T(8,128)} %get-tuple-element.128.solution_ref), custom_call_target="tpu_custom_call" | custom-call | tf_op jit(solution)/shard_map/pallas_call | solution.py:51
  (108 shorter events, 7.9 us)
Async XLA Ops:
  0.0 26.4 %copy-start.17 = (f32[8,8]{1,0:T(8,128)S(1)}, f32[8,8]{1,0:T(8,128)}, u32[]{:S(2)}) copy-start(f32[8,8]{1,0:T(8,128)} %along_ref.1) | copy-start | bytes 772
  0.0 26.4 %copy-start.20 = (s32[4096]{0:T(1024)S(1)}, s32[4096]{0:T(1024)}, u32[]{:S(2)}) copy-start(s32[4096]{0:T(1024)} %param.25) | copy-start | bytes 49156
  3.0 29.2 %all-to-all-start = ((f32[16,32,128]{2,1,0:T(8,128)}), f32[16,32,128]{2,1,0:T(8,128)S(1)}, u32[]{:S(2)}, u32[]{:S(2)}) async-start(f32[16,32,128]{2,1,0:T(8,128)} %get-tuple-element.67), calls=%async_computation | async-start | bytes 524288 | tf_op jit(solution)/shard_map/all_to_all | solution.py:34
  12.9 54.9 %collective-permute-start.4 = (f32[33,8,128]{2,1,0:T(8,128)S(1)}, f32[33,8,128]{2,1,0:T(8,128)S(1)}, u32[]{:S(2)}, u32[]{:S(2)}) collective-permute-start(f32[33,8,128]{2,1,0:T(8,128)S(1)} %get-tuple-element.73), channel_id=1, source_target_pairs={{0,16},{16,32},{32,48},{48,64},{64,80},{80,96},{96,112},{112,128},... | collective-permute-start | bytes 405512 | tf_op jit(solution)/shard_map/ppermute | solution.py:26
  17.1 68.3 %collective-permute-start.5 = (f32[32,8,128]{2,1,0:T(8,128)S(1)}, f32[32,8,128]{2,1,0:T(8,128)S(1)}, u32[]{:S(2)}, u32[]{:S(2)}) collective-permute-start(f32[32,8,128]{2,1,0:T(8,128)S(1)} %get-tuple-element.74), channel_id=1, source_target_pairs={{16,0},{32,16},{48,32},{64,48},{80,64},{96,80},{112,96},{128,112},... | collective-permute-start | bytes 393224 | tf_op jit(solution)/shard_map/ppermute | solution.py:26
  18.4 57.5 %collective-permute-start.6 = (f32[33,8,128]{2,1,0:T(8,128)S(1)}, f32[33,8,128]{2,1,0:T(8,128)S(1)}, u32[]{:S(2)}, u32[]{:S(2)}) collective-permute-start(f32[33,8,128]{2,1,0:T(8,128)S(1)} %get-tuple-element.75), channel_id=1, source_target_pairs={{0,1},{1,2},{2,3},{3,4},{4,5},{5,6},{6,7},{7,8},{8,9},{9,10},{10,1... | collective-permute-start | bytes 405512 | tf_op jit(solution)/shard_map/ppermute | solution.py:26
  21.8 63.6 %collective-permute-start.7 = (f32[32,8,128]{2,1,0:T(8,128)S(1)}, f32[32,8,128]{2,1,0:T(8,128)S(1)}, u32[]{:S(2)}, u32[]{:S(2)}) collective-permute-start(f32[32,8,128]{2,1,0:T(8,128)S(1)} %get-tuple-element.76), channel_id=1, source_target_pairs={{1,0},{2,1},{3,2},{4,3},{5,4},{6,5},{7,6},{8,7},{9,8},{10,9},{11,1... | collective-permute-start | bytes 393224 | tf_op jit(solution)/shard_map/ppermute | solution.py:26
  27.1 3.5 %copy-start.6 = (s32[4096]{0:T(1024)}, s32[4096]{0:T(1024)S(1)}, u32[]{:S(2)}) copy-start(s32[4096]{0:T(1024)S(1)} %get-tuple-element.135) | copy-start | bytes 49156
  30.0 1.2 copy-start.22
  30.0 1.2 copy-start.19
  30.0 1.2 copy-start.15
  30.0 1.2 copy-start.24
  30.0 2.1 copy-start.16
  30.0 4.6 %copy-start.23 = (s32[1,1,48]{2,1,0:T(1,128)S(1)}, s32[1,1,48]{2,1,0:T(1,128)}, u32[]{:S(2)}) copy-start(s32[1,1,48]{2,1,0:T(1,128)} %param.21) | copy-start | bytes 580
  30.1 5.8 %copy-start = (bf16[1,1,48,128,128]{4,3,2,1,0:T(8,128)(2,1)S(1)}, bf16[1,1,48,128,128]{4,3,2,1,0:T(8,128)(2,1)}, u32[]{:S(2)}) copy-start(bf16[1,1,48,128,128]{4,3,2,1,0:T(8,128)(2,1)} %param.20) | copy-start | bytes 4718596
  30.5 10.1 %copy-start.18 = (f32[8,8]{1,0:T(8,128)S(1)}, f32[8,8]{1,0:T(8,128)}, u32[]{:S(2)}) copy-start(f32[8,8]{1,0:T(8,128)} %across_ref.1) | copy-start | bytes 772
  32.2 3.6 %collective-permute-start = (f32[16,32,128]{2,1,0:T(8,128)S(1)}, f32[16,32,128]{2,1,0:T(8,128)S(1)}, u32[]{:S(2)}, u32[]{:S(2)}) collective-permute-start(f32[16,32,128]{2,1,0:T(8,128)S(1)} %all-to-all-done.refs_4_), channel_id=1, source_target_pairs={{0,128},{128,0},{1,129},{129,1},{2,130},{130,2},{3,131},{131,3},{4... | collective-permute-start | bytes 786440 | tf_op jit(solution)/shard_map/ppermute | solution.py:30
  34.9 34.2 %copy-start.1 = (bf16[5,128,128]{2,1,0:T(8,128)(2,1)}, bf16[5,128,128]{2,1,0:T(8,128)(2,1)S(1)}, u32[]{:S(2)}) copy-start(bf16[5,128,128]{2,1,0:T(8,128)(2,1)S(1)} %bitcast_dynamic-update-slice_fusion.refs_5_.refs_6_.refs_20_) | copy-start | bytes 491524
  40.3 1.4 collective-permute-start.1
  42.3 13.8 %all-to-all-start.1 = ((f32[8,32,128]{2,1,0:T(8,128)}), f32[8,32,128]{2,1,0:T(8,128)S(1)}, u32[]{:S(2)}, u32[]{:S(2)}) async-start(f32[8,32,128]{2,1,0:T(8,128)} %add.66), calls=%async_computation.1 | async-start | bytes 262144 | tf_op jit(solution)/shard_map/all_to_all | solution.py:34
  56.7 11.0 %all-to-all-start.2 = ((bf16[8,32,128]{2,1,0:T(8,128)(2,1)}), bf16[8,32,128]{2,1,0:T(8,128)(2,1)S(1)}, u32[]{:S(2)}, u32[]{:S(2)}) async-start(bf16[8,32,128]{2,1,0:T(8,128)(2,1)} %shard_map.129), calls=%async_computation.2 | async-start | bytes 131072 | tf_op jit(solution)/shard_map/all_to_all | solution.py:34
  67.8 1.3 collective-permute-start.2
  67.8 18.5 %copy-start.2 = (f32[33,8,128]{2,1,0:T(8,128)}, f32[33,8,128]{2,1,0:T(8,128)S(1)}, u32[]{:S(2)}) copy-start(f32[33,8,128]{2,1,0:T(8,128)S(1)} %collective-permute-done.4.refs_0_.refs_10_.refs_14_) | copy-start | bytes 405508
  75.7 1.6 collective-permute-start.3
  75.9 10.3 %copy-start.3 = (f32[33,8,128]{2,1,0:T(8,128)}, f32[33,8,128]{2,1,0:T(8,128)S(1)}, u32[]{:S(2)}) copy-start(f32[33,8,128]{2,1,0:T(8,128)S(1)} %collective-permute-done.6.refs_2_.refs_12_.refs_16_) | copy-start | bytes 405508
  78.0 17.0 %all-to-all-start.3 = ((f32[16,32,128]{2,1,0:T(8,128)}), f32[16,32,128]{2,1,0:T(8,128)S(1)}, u32[]{:S(2)}, u32[]{:S(2)}) async-start(f32[16,32,128]{2,1,0:T(8,128)} %add.67), calls=%async_computation.3 | async-start | bytes 524288 | tf_op jit(solution)/shard_map/all_to_all | solution.py:34
  85.4 0.8 copy-start.4
  85.4 0.8 copy-start.5
  111.8 1.6 collective-permute-start.8
  129.0 1.3 collective-permute-start.9
  140.8 26.4 %copy-start.21 = (s32[1,1,128]{2,1,0:T(1,128)S(1)}, s32[1,1,128]{2,1,0:T(1,128)}, u32[]{:S(2)}) copy-start(s32[1,1,128]{2,1,0:T(1,128)} %param.24) | copy-start | bytes 1540
  151.1 1.3 collective-permute-start.10
  159.0 1.6 collective-permute-start.11
  161.4 34.0 %all-to-all-start.8 = ((f32[16,32,128]{2,1,0:T(8,128)}), f32[16,32,128]{2,1,0:T(8,128)S(1)}, u32[]{:S(2)}, u32[]{:S(2)}) async-start(f32[16,32,128]{2,1,0:T(8,128)} %add.69), calls=%async_computation.8 | async-start | bytes 524288 | tf_op jit(solution)/shard_map/all_to_all | solution.py:34
  170.1 11.6 %collective-permute-start.12 = (f32[32,8,128]{2,1,0:T(8,128)S(1)}, f32[32,8,128]{2,1,0:T(8,128)S(1)}, u32[]{:S(2)}, u32[]{:S(2)}) collective-permute-start(f32[32,8,128]{2,1,0:T(8,128)S(1)} %get-tuple-element.94), channel_id=1, source_target_pairs={{0,16},{16,32},{32,48},{48,64},{64,80},{80,96},{96,112},{112,128},... | collective-permute-start | bytes 393224 | tf_op jit(solution)/shard_map/ppermute | solution.py:26
  172.5 9.5 %collective-permute-start.13 = (f32[32,8,128]{2,1,0:T(8,128)S(1)}, f32[32,8,128]{2,1,0:T(8,128)S(1)}, u32[]{:S(2)}, u32[]{:S(2)}) collective-permute-start(f32[32,8,128]{2,1,0:T(8,128)S(1)} %get-tuple-element.95), channel_id=1, source_target_pairs={{16,0},{32,16},{48,32},{64,48},{80,64},{96,80},{112,96},{128,112},... | collective-permute-start | bytes 393224 | tf_op jit(solution)/shard_map/ppermute | solution.py:26
  173.8 9.1 %collective-permute-start.14 = (f32[32,8,128]{2,1,0:T(8,128)S(1)}, f32[32,8,128]{2,1,0:T(8,128)S(1)}, u32[]{:S(2)}, u32[]{:S(2)}) collective-permute-start(f32[32,8,128]{2,1,0:T(8,128)S(1)} %get-tuple-element.96), channel_id=1, source_target_pairs={{0,1},{1,2},{2,3},{3,4},{4,5},{5,6},{6,7},{7,8},{8,9},{9,10},{10,1... | collective-permute-start | bytes 393224 | tf_op jit(solution)/shard_map/ppermute | solution.py:26
  177.2 7.1 %collective-permute-start.15 = (f32[32,8,128]{2,1,0:T(8,128)S(1)}, f32[32,8,128]{2,1,0:T(8,128)S(1)}, u32[]{:S(2)}, u32[]{:S(2)}) collective-permute-start(f32[32,8,128]{2,1,0:T(8,128)S(1)} %get-tuple-element.97), channel_id=1, source_target_pairs={{1,0},{2,1},{3,2},{4,3},{5,4},{6,5},{7,6},{8,7},{9,8},{10,9},{11,1... | collective-permute-start | bytes 393224 | tf_op jit(solution)/shard_map/ppermute | solution.py:26
  181.8 2.5 copy-start.9
  182.0 2.3 copy-start.11
  182.8 1.4 copy-start.12
  184.3 0.6 copy-start.14
  213.0 4.8 %collective-permute-start.16 = (f32[16,40,128]{2,1,0:T(8,128)S(1)}, f32[16,40,128]{2,1,0:T(8,128)S(1)}, u32[]{:S(2)}, u32[]{:S(2)}) collective-permute-start(f32[16,40,128]{2,1,0:T(8,128)S(1)} %all_to_all.69.mine_ref.refs_6_), channel_id=1, source_target_pairs={{0,128},{128,0},{1,129},{129,1},{2,130},{130,2},{3,131},{131,3},{4... | collective-permute-start | bytes 983048 | tf_op jit(solution)/shard_map/ppermute | solution.py:30
  235.8 1.5 collective-permute-start.17
  238.0 30.4 %all-to-all-start.11 = ((f32[8,64,128]{2,1,0:T(8,128)}), f32[8,64,128]{2,1,0:T(8,128)S(1)}, u32[]{:S(2)}, u32[]{:S(2)}) async-start(f32[8,64,128]{2,1,0:T(8,128)} %add.72), calls=%async_computation.11 | async-start | bytes 524288 | tf_op jit(solution)/shard_map/all_to_all | solution.py:34
  243.5 14.6 %collective-permute-start.18 = (f32[32,8,128]{2,1,0:T(8,128)S(1)}, f32[32,8,128]{2,1,0:T(8,128)S(1)}, u32[]{:S(2)}, u32[]{:S(2)}) collective-permute-start(f32[32,8,128]{2,1,0:T(8,128)S(1)} %get-tuple-element.118), channel_id=1, source_target_pairs={{0,16},{16,32},{32,48},{48,64},{64,80},{80,96},{96,112},{112,128},... | collective-permute-start | bytes 393224 | tf_op jit(solution)/shard_map/ppermute | solution.py:26
  248.8 9.3 %collective-permute-start.19 = (f32[32,8,128]{2,1,0:T(8,128)S(1)}, f32[32,8,128]{2,1,0:T(8,128)S(1)}, u32[]{:S(2)}, u32[]{:S(2)}) collective-permute-start(f32[32,8,128]{2,1,0:T(8,128)S(1)} %get-tuple-element.119), channel_id=1, source_target_pairs={{16,0},{32,16},{48,32},{64,48},{80,64},{96,80},{112,96},{128,112},... | collective-permute-start | bytes 393224 | tf_op jit(solution)/shard_map/ppermute | solution.py:26
  250.1 9.0 %collective-permute-start.20 = (f32[32,8,128]{2,1,0:T(8,128)S(1)}, f32[32,8,128]{2,1,0:T(8,128)S(1)}, u32[]{:S(2)}, u32[]{:S(2)}) collective-permute-start(f32[32,8,128]{2,1,0:T(8,128)S(1)} %get-tuple-element.120), channel_id=1, source_target_pairs={{0,1},{1,2},{2,3},{3,4},{4,5},{5,6},{6,7},{7,8},{8,9},{9,10},{10,1... | collective-permute-start | bytes 393224 | tf_op jit(solution)/shard_map/ppermute | solution.py:26
  254.3 6.9 %collective-permute-start.21 = (f32[32,8,128]{2,1,0:T(8,128)S(1)}, f32[32,8,128]{2,1,0:T(8,128)S(1)}, u32[]{:S(2)}, u32[]{:S(2)}) collective-permute-start(f32[32,8,128]{2,1,0:T(8,128)S(1)} %get-tuple-element.121), channel_id=1, source_target_pairs={{1,0},{2,1},{3,2},{4,3},{5,4},{6,5},{7,6},{8,7},{9,8},{10,9},{11,1... | collective-permute-start | bytes 393224 | tf_op jit(solution)/shard_map/ppermute | solution.py:26
  258.1 3.0 %copy-start.7 = (f32[32,8,128]{2,1,0:T(8,128)}, f32[32,8,128]{2,1,0:T(8,128)S(1)}, u32[]{:S(2)}) copy-start(f32[32,8,128]{2,1,0:T(8,128)S(1)} %collective-permute-done.18.refs_7_) | copy-start | bytes 393220
  258.1 3.0 %copy-start.8 = (f32[32,8,128]{2,1,0:T(8,128)}, f32[32,8,128]{2,1,0:T(8,128)S(1)}, u32[]{:S(2)}) copy-start(f32[32,8,128]{2,1,0:T(8,128)S(1)} %collective-permute-done.19.refs_8_) | copy-start | bytes 393220
  259.1 2.1 copy-start.10
  261.2 0.7 copy-start.13
